TPU v7x, 32 devices: a whole 2x2x4 slice. The times are simulated.
32 devices in a mesh: dp: 4 (over z), blk: 2 (over core), uly: 4 (over y, x).
Axes of the slice: x: 2, y: 2, z: 4, core: 2. Of those that a mesh axis runs over, the one named last changes fastest.
Arguments:
- tokens: bfloat16 [4, 2048, 768], P('dp', ('blk', 'uly')), may hold values from -6 to 6
- lengths: int32 [4], P('dp'), may hold values from 512 to 2048, as said below
- cotangent: bfloat16 [4, 2048, 768], P('dp', ('blk', 'uly')), may hold values from -6 to 6
- attend_weight: bfloat16 [768, 2304], P('dp'), may hold values from -0.3125 to 0.3125
- query_bias: bfloat16 [768], P('dp'), may hold values from -3 to 3
- value_bias: bfloat16 [768], P('dp'), may hold values from -0.8984375 to 0.8984375
- mixer_weight: bfloat16 [768, 768], P('dp'), may hold values from -1.5 to 1.5
- mixer_bias: bfloat16 [768], P('dp'), may hold values from -3 to 3
- attn_gain: bfloat16 [768], P('dp'), may hold values from 0.5 to 1.5
- attn_shift: bfloat16 [768], P('dp'), may hold values from -2 to 2
- expand_weight: bfloat16 [768, 3072], P('dp'), may hold values from -0.21875 to 0.21875
- expand_bias: bfloat16 [3072], P('dp'), may hold values from -3 to 3
- shrink_weight: bfloat16 [3072, 768], P('dp'), may hold values from -0.109375 to 0.109375
- shrink_bias: bfloat16 [768], P('dp'), may hold values from -2 to 2
- final_gain: bfloat16 [768], P('dp'), may hold values from 0.5 to 1.5
- final_shift: bfloat16 [768], P('dp'), may hold values from -2 to 2
Outputs:
- mixed: bfloat16 [4, 2048, 768], P('dp', ('blk', 'uly'))
- tokens_grad: float32 [4, 2048, 768], P('dp', ('blk', 'uly'))
- attend_grad: float32 [768, 2304], P('dp')
- query_bias_grad: float32 [768], P('dp')
- value_bias_grad: float32 [768], P('dp')
- mixer_grad: float32 [768, 768], P('dp')
- mixer_bias_grad: float32 [768], P('dp')
- attn_gain_grad: float32 [768], P('dp')
- attn_shift_grad: float32 [768], P('dp')
- expand_grad: float32 [768, 3072], P('dp')
- expand_bias_grad: float32 [3072], P('dp')
- shrink_grad: float32 [3072, 768], P('dp')
- shrink_bias_grad: float32 [768], P('dp')
- final_gain_grad: float32 [768], P('dp')
- final_shift_grad: float32 [768], P('dp')
Inputs may be any that keep to these rules, and one draw needn't show every extreme that they name: `lengths`: the number of leading positions of each sequence that hold real tokens; in every draw one sequence has 2048 and another 2048 // 4.
All inputs are finite; a program needn't handle non-finite values.
Results may differ from a plain program's by a relative error of at most 0.04.
Values may be sent and summed in bfloat16 or wider, within the bound.
No kernel may reach another device: no remote copies, remote signals or barrier semaphores. Data moves between devices by JAX's collectives and lax.ppermute only.
A program may use at most 128 MiB of HBM per device.

v0:
```python
import jax
import jax.numpy as jnp
from jax import lax
from jax.sharding import PartitionSpec as P

HEADS = 12
HD = 64


EPSILON = 1e-12
MASKED = -1000000000.0


def contract_rows(left_mat, right_mat):
    return lax.dot_general(
        left_mat, right_mat, (((0,), (0,)), ((), ())), preferred_element_type=jnp.float32
    )


def contract_cols(left_mat, right_mat):
    return lax.dot_general(
        left_mat, right_mat, (((1,), (1,)), ((), ())), preferred_element_type=jnp.float32
    )


def norm_forward(hidden, gain_vec, shift_vec):
    center = hidden - jnp.mean(hidden, -1, keepdims=True)
    scale_inv = lax.rsqrt(jnp.mean(center * center, -1, keepdims=True) + EPSILON)
    normed = center * scale_inv
    return (normed * gain_vec + shift_vec, normed, scale_inv)


def norm_backward(upstream, normed, scale_inv, gain_vec):
    gain_grad = jnp.sum(upstream * normed, 0)
    shift_grad = jnp.sum(upstream, 0)
    scaled = upstream * gain_vec
    hidden_grad = scale_inv * (
        scaled
        - jnp.mean(scaled, -1, keepdims=True)
        - normed * jnp.mean(scaled * normed, -1, keepdims=True)
    )
    return (hidden_grad, gain_grad, shift_grad)


def on_device(
    tokens,
    lengths,
    cotangent,
    attend_weight,
    query_bias,
    value_bias,
    mixer_weight,
    mixer_bias,
    attn_gain,
    attn_shift,
    expand_weight,
    expand_bias,
    shrink_weight,
    shrink_bias,
    final_gain,
    final_shift,
):
    uly_size = lax.axis_size("uly")
    blk_size = lax.axis_size("blk")
    seq_count, seq_piece, model_width = tokens.shape
    local_heads = HEADS // uly_size
    group_width = local_heads * HD
    block_rows = uly_size * seq_piece
    row_count = seq_count * seq_piece
    gathered = (
        lax.all_gather(attend_weight, "dp", axis=0, tiled=True),
        lax.all_gather(query_bias, "dp", axis=0, tiled=True),
        lax.all_gather(value_bias, "dp", axis=0, tiled=True),
        lax.all_gather(mixer_weight, "dp", axis=0, tiled=True),
        lax.all_gather(mixer_bias, "dp", axis=0, tiled=True),
        lax.all_gather(attn_gain, "dp", axis=0, tiled=True),
        lax.all_gather(attn_shift, "dp", axis=0, tiled=True),
        lax.all_gather(expand_weight, "dp", axis=0, tiled=True),
        lax.all_gather(expand_bias, "dp", axis=0, tiled=True),
        lax.all_gather(shrink_weight, "dp", axis=0, tiled=True),
        lax.all_gather(shrink_bias, "dp", axis=0, tiled=True),
        lax.all_gather(final_gain, "dp", axis=0, tiled=True),
        lax.all_gather(final_shift, "dp", axis=0, tiled=True),
    )
    attend_full = gathered[0]
    mixer_full = gathered[3]
    expand_full = gathered[7]
    shrink_full = gathered[9]
    bias_query = gathered[1].astype(jnp.float32)
    bias_value = gathered[2].astype(jnp.float32)
    bias_mixer = gathered[4].astype(jnp.float32)
    gain_attn = gathered[5].astype(jnp.float32)
    shift_attn = gathered[6].astype(jnp.float32)
    bias_expand = gathered[8].astype(jnp.float32)
    bias_shrink = gathered[10].astype(jnp.float32)
    gain_final = gathered[11].astype(jnp.float32)
    shift_final = gathered[12].astype(jnp.float32)
    flat_tokens = tokens.reshape(row_count, model_width)
    projected = jnp.dot(flat_tokens, attend_full, preferred_element_type=jnp.float32)
    zero_width = jnp.zeros((model_width,), jnp.float32)
    bias_all = jnp.concatenate([bias_query, zero_width, bias_value])
    scale_all = jnp.concatenate(
        [jnp.full((model_width,), 0.125, jnp.float32), jnp.ones((2 * model_width,), jnp.float32)]
    )
    rounded = ((projected + bias_all) * scale_all).astype(jnp.bfloat16)
    outgoing = rounded.reshape(seq_count, seq_piece, 3, uly_size, group_width).transpose(
        0, 2, 3, 1, 4
    )
    outgoing = outgoing.reshape(seq_count, 3, uly_size, seq_piece * group_width)
    arrived = lax.all_to_all(outgoing, "uly", split_axis=2, concat_axis=3, tiled=True).reshape(
        seq_count, 3, block_rows, local_heads, HD
    )
    query_heads = arrived[:, 0]
    keys_values = (
        arrived[:, 1:].transpose(0, 2, 1, 3, 4).reshape(seq_count, block_rows, 2 * group_width)
    )
    keys_only = arrived[:, 1].reshape(seq_count, block_rows, group_width)
    key_offsets = jnp.arange(block_rows, dtype=jnp.int32)

    def masked_scores(query_block, key_heads, first_key):
        scores = jnp.einsum(
            "sqhe,skhe->shqk", query_block, key_heads, preferred_element_type=jnp.float32
        )
        valid_mask = (first_key + key_offsets)[None, :] < lengths[:, None]
        return jnp.where(valid_mask[:, None, None, :], scores, MASKED)

    def split_keys(query_block, key_block, first_key):
        key_heads = key_block[..., :group_width].reshape(seq_count, block_rows, local_heads, HD)
        value_heads = key_block[..., group_width:].reshape(seq_count, block_rows, local_heads, HD)
        return (masked_scores(query_block, key_heads, first_key), key_heads, value_heads)

    start_stats = (
        jnp.full((seq_count, local_heads, block_rows), -jnp.inf, jnp.float32),
        jnp.zeros((seq_count, local_heads, block_rows), jnp.float32),
    )
    key_piece = lax.all_gather(keys_only, "blk", axis=1, tiled=True)

    def one_block(block_index, inner):
        row_max, row_sum = inner
        key_block = lax.dynamic_slice_in_dim(key_piece, block_index * block_rows, block_rows, 1)
        key_heads = key_block.reshape(seq_count, block_rows, local_heads, HD)
        scores = masked_scores(query_heads, key_heads, block_index * block_rows)
        newest = jnp.maximum(row_max, jnp.max(scores, -1))
        row_sum = row_sum * jnp.exp(row_max - newest) + jnp.sum(
            jnp.exp(scores - newest[..., None]), -1
        )
        return (newest, row_sum)

    row_max, row_sum = lax.fori_loop(0, key_piece.shape[1] // block_rows, one_block, start_stats)
    log_total = row_max + jnp.log(row_sum)
    fold_key_piece = lax.all_gather(keys_values, "blk", axis=1, tiled=True)

    def one_block(block_index, inner):
        key_block = lax.dynamic_slice_in_dim(
            fold_key_piece, block_index * block_rows, block_rows, 1
        )
        scores, key_heads, value_heads = split_keys(
            query_heads, key_block, block_index * block_rows
        )
        probs = jnp.exp(scores - log_total[..., None]).astype(jnp.bfloat16)
        return inner + jnp.einsum(
            "shqk,skhe->shqe", probs, value_heads, preferred_element_type=jnp.float32
        )

    attended = lax.fori_loop(
        0,
        fold_key_piece.shape[1] // block_rows,
        one_block,
        jnp.zeros((seq_count, local_heads, block_rows, HD), jnp.float32),
    )
    head_out = (
        attended.astype(jnp.bfloat16)
        .transpose(0, 2, 1, 3)
        .reshape(seq_count, uly_size, seq_piece * group_width)
    )
    returned = lax.all_to_all(head_out, "uly", split_axis=1, concat_axis=2, tiled=True)
    mixer_in = (
        returned.reshape(seq_count, uly_size, seq_piece, group_width)
        .transpose(0, 2, 1, 3)
        .reshape(row_count, model_width)
    )
    tokens_wide = flat_tokens.astype(jnp.float32)
    first_sum = tokens_wide + (
        jnp.dot(mixer_in, mixer_full, preferred_element_type=jnp.float32) + bias_mixer
    )
    first_out, first_normed, first_inv = norm_forward(first_sum, gain_attn, shift_attn)
    first_low = first_out.astype(jnp.bfloat16)
    pre_act = jnp.dot(first_low, expand_full, preferred_element_type=jnp.float32) + bias_expand
    activation = jax.nn.gelu(pre_act, approximate=False).astype(jnp.bfloat16)
    second_sum = first_out + (
        jnp.dot(activation, shrink_full, preferred_element_type=jnp.float32) + bias_shrink
    )
    second_out, second_normed, second_inv = norm_forward(second_sum, gain_final, shift_final)
    mixed_out = second_out.astype(jnp.bfloat16).reshape(seq_count, seq_piece, model_width)
    attend_back, mixer_back, expand_back, shrink_back = (
        lax.all_gather(attend_weight, "dp", axis=0, tiled=True),
        lax.all_gather(mixer_weight, "dp", axis=0, tiled=True),
        lax.all_gather(expand_weight, "dp", axis=0, tiled=True),
        lax.all_gather(shrink_weight, "dp", axis=0, tiled=True),
    )
    upstream = cotangent.reshape(row_count, model_width).astype(jnp.float32)
    second_grad, final_gain_grad, final_shift_grad = norm_backward(
        upstream, second_normed, second_inv, gain_final
    )
    shrink_bias_grad = jnp.sum(second_grad, 0)
    second_low = second_grad.astype(jnp.bfloat16)
    shrink_grad = contract_rows(activation, second_low)
    act_grad = contract_cols(second_low, shrink_back)
    gelu_pullback = jax.vjp(lambda pre_value: jax.nn.gelu(pre_value, approximate=False), pre_act)[1]
    pre_grad = gelu_pullback(act_grad)[0].astype(jnp.bfloat16)
    expand_bias_grad = jnp.sum(pre_grad.astype(jnp.float32), 0)
    expand_grad = contract_rows(first_low, pre_grad)
    first_grad = second_grad + contract_cols(pre_grad, expand_back)
    attn_grad, attn_gain_grad, attn_shift_grad = norm_backward(
        first_grad, first_normed, first_inv, gain_attn
    )
    mixer_bias_grad = jnp.sum(attn_grad, 0)
    attn_low = attn_grad.astype(jnp.bfloat16)
    mixer_grad = contract_rows(mixer_in, attn_low)
    out_grad = contract_cols(attn_low, mixer_back).astype(jnp.bfloat16)
    grad_send = (
        out_grad.reshape(seq_count, seq_piece, uly_size, group_width)
        .transpose(0, 2, 1, 3)
        .reshape(seq_count, uly_size, seq_piece * group_width)
    )
    head_grad = lax.all_to_all(grad_send, "uly", split_axis=1, concat_axis=2, tiled=True).reshape(
        seq_count, block_rows, local_heads, HD
    )
    delta_rows = jnp.sum(
        head_grad.astype(jnp.float32) * attended.transpose(0, 2, 1, 3), -1
    ).transpose(0, 2, 1)

    def pair_grads(query_block, grad_block, total_block, delta_block, key_block, first_key):
        scores, key_heads, value_heads = split_keys(query_block, key_block, first_key)
        softmax_rows = jnp.exp(scores - total_block[..., None])
        value_grad = jnp.einsum(
            "shqk,sqhe->skhe",
            softmax_rows.astype(jnp.bfloat16),
            grad_block,
            preferred_element_type=jnp.float32,
        )
        prob_grad = jnp.einsum(
            "sqhe,skhe->shqk", grad_block, value_heads, preferred_element_type=jnp.float32
        )
        score_grad = (softmax_rows * (prob_grad - delta_block[..., None])).astype(jnp.bfloat16)
        query_part = jnp.einsum(
            "shqk,skhe->sqhe", score_grad, key_heads, preferred_element_type=jnp.float32
        )
        key_grad = jnp.einsum(
            "shqk,sqhe->skhe", score_grad, query_block, preferred_element_type=jnp.float32
        )
        return (query_part, key_grad, value_grad)

    all_keys = lax.all_gather(keys_values, "blk", axis=1, tiled=True)

    def back_block(block_index, inner):
        query_grad, key_grads = inner
        first_key = block_index * block_rows
        key_block = lax.dynamic_slice_in_dim(all_keys, first_key, block_rows, 1)
        query_part, key_grad, value_grad = pair_grads(
            query_heads, head_grad, log_total, delta_rows, key_block, first_key
        )
        joined = jnp.concatenate(
            [
                key_grad.reshape(seq_count, block_rows, group_width),
                value_grad.reshape(seq_count, block_rows, group_width),
            ],
            -1,
        )
        return (
            query_grad + query_part,
            lax.dynamic_update_slice_in_dim(key_grads, joined, first_key, 1),
        )

    start_grads = (
        jnp.zeros((seq_count, block_rows, local_heads, HD), jnp.float32),
        jnp.zeros((seq_count, block_rows * blk_size, 2 * group_width), jnp.float32),
    )
    query_grad, key_grads = lax.fori_loop(0, blk_size, back_block, start_grads)
    key_sums = lax.psum_scatter(
        key_grads.astype(jnp.bfloat16), "blk", scatter_dimension=1, tiled=True
    )
    pair_back = key_sums.reshape(seq_count, block_rows, 2, group_width).transpose(0, 2, 1, 3)
    query_back = query_grad.astype(jnp.bfloat16).reshape(seq_count, 1, block_rows, group_width)
    triple = jnp.concatenate([query_back, pair_back], 1).reshape(
        seq_count, 3, uly_size, seq_piece * group_width
    )
    token_grads = lax.all_to_all(triple, "uly", split_axis=2, concat_axis=3, tiled=True).reshape(
        seq_count, 3, uly_size, seq_piece, group_width
    )
    proj_grad = token_grads.transpose(0, 3, 1, 2, 4).reshape(
        row_count, 3 * model_width
    ) * scale_all.astype(jnp.bfloat16)
    query_bias_grad = jnp.sum(proj_grad[:, :model_width].astype(jnp.float32), 0)
    value_bias_grad = jnp.sum(proj_grad[:, 2 * model_width :].astype(jnp.float32), 0)
    attend_grad = contract_rows(flat_tokens, proj_grad)
    tokens_grad = (attn_grad + contract_cols(proj_grad, attend_back)).reshape(
        seq_count, seq_piece, model_width
    )
    param_grads = (
        attend_grad,
        query_bias_grad,
        value_bias_grad,
        mixer_grad,
        mixer_bias_grad,
        attn_gain_grad,
        attn_shift_grad,
        expand_grad,
        expand_bias_grad,
        shrink_grad,
        shrink_bias_grad,
        final_gain_grad,
        final_shift_grad,
    )
    owned_grads = (
        lax.psum_scatter(
            param_grads[0].astype(jnp.bfloat16), "dp", scatter_dimension=0, tiled=True
        ).astype(jnp.float32),
        lax.psum_scatter(
            param_grads[1].astype(jnp.bfloat16), "dp", scatter_dimension=0, tiled=True
        ).astype(jnp.float32),
        lax.psum_scatter(
            param_grads[2].astype(jnp.bfloat16), "dp", scatter_dimension=0, tiled=True
        ).astype(jnp.float32),
        lax.psum_scatter(
            param_grads[3].astype(jnp.bfloat16), "dp", scatter_dimension=0, tiled=True
        ).astype(jnp.float32),
        lax.psum_scatter(
            param_grads[4].astype(jnp.bfloat16), "dp", scatter_dimension=0, tiled=True
        ).astype(jnp.float32),
        lax.psum_scatter(
            param_grads[5].astype(jnp.bfloat16), "dp", scatter_dimension=0, tiled=True
        ).astype(jnp.float32),
        lax.psum_scatter(
            param_grads[6].astype(jnp.bfloat16), "dp", scatter_dimension=0, tiled=True
        ).astype(jnp.float32),
        lax.psum_scatter(
            param_grads[7].astype(jnp.bfloat16), "dp", scatter_dimension=0, tiled=True
        ).astype(jnp.float32),
        lax.psum_scatter(
            param_grads[8].astype(jnp.bfloat16), "dp", scatter_dimension=0, tiled=True
        ).astype(jnp.float32),
        lax.psum_scatter(
            param_grads[9].astype(jnp.bfloat16), "dp", scatter_dimension=0, tiled=True
        ).astype(jnp.float32),
        lax.psum_scatter(
            param_grads[10].astype(jnp.bfloat16), "dp", scatter_dimension=0, tiled=True
        ).astype(jnp.float32),
        lax.psum_scatter(
            param_grads[11].astype(jnp.bfloat16), "dp", scatter_dimension=0, tiled=True
        ).astype(jnp.float32),
        lax.psum_scatter(
            param_grads[12].astype(jnp.bfloat16), "dp", scatter_dimension=0, tiled=True
        ).astype(jnp.float32),
    )
    owned_grads = (
        lax.psum(owned_grads[0].astype(jnp.bfloat16), ("blk", "uly")).astype(jnp.float32),
        lax.psum(owned_grads[1].astype(jnp.bfloat16), ("blk", "uly")).astype(jnp.float32),
        lax.psum(owned_grads[2].astype(jnp.bfloat16), ("blk", "uly")).astype(jnp.float32),
        lax.psum(owned_grads[3].astype(jnp.bfloat16), ("blk", "uly")).astype(jnp.float32),
        lax.psum(owned_grads[4].astype(jnp.bfloat16), ("blk", "uly")).astype(jnp.float32),
        lax.psum(owned_grads[5].astype(jnp.bfloat16), ("blk", "uly")).astype(jnp.float32),
        lax.psum(owned_grads[6].astype(jnp.bfloat16), ("blk", "uly")).astype(jnp.float32),
        lax.psum(owned_grads[7].astype(jnp.bfloat16), ("blk", "uly")).astype(jnp.float32),
        lax.psum(owned_grads[8].astype(jnp.bfloat16), ("blk", "uly")).astype(jnp.float32),
        lax.psum(owned_grads[9].astype(jnp.bfloat16), ("blk", "uly")).astype(jnp.float32),
        lax.psum(owned_grads[10].astype(jnp.bfloat16), ("blk", "uly")).astype(jnp.float32),
        lax.psum(owned_grads[11].astype(jnp.bfloat16), ("blk", "uly")).astype(jnp.float32),
        lax.psum(owned_grads[12].astype(jnp.bfloat16), ("blk", "uly")).astype(jnp.float32),
    )
    return (mixed_out, tokens_grad) + tuple(owned_grads)


def solution(mesh):
    return jax.shard_map(
        on_device,
        mesh=mesh,
        in_specs=(
            P("dp", ("blk", "uly"), None),
            P("dp"),
            P("dp", ("blk", "uly"), None),
            P("dp", None),
            P("dp"),
            P("dp"),
            P("dp", None),
            P("dp"),
            P("dp"),
            P("dp"),
            P("dp", None),
            P("dp"),
            P("dp", None),
            P("dp"),
            P("dp"),
            P("dp"),
        ),
        out_specs=(
            P("dp", ("blk", "uly"), None),
            P("dp", ("blk", "uly"), None),
            P("dp", None),
            P("dp"),
            P("dp"),
            P("dp", None),
            P("dp"),
            P("dp"),
            P("dp"),
            P("dp", None),
            P("dp"),
            P("dp", None),
            P("dp"),
            P("dp"),
            P("dp"),
        ),
        check_vma=False,
    )
```

profile of v0, /device:TPU:0, one launch (start us, length us, event | category | flops | bytes accessed | tf_op | source)
XLA Modules:
  0.0 844.3 jit_solution(14480245671128180972)
XLA Ops:
  15.8 21.3 %all-reduce.20 = (bf16[768]{0:T(1024)(128)(2,1)S(1)}, bf16[768]{0:T(1024)(128)(2,1)S(1)}, bf16[768]{0:T(1024)(128)(2,1)S(1)}, bf16[768]{0:T(1024)(128)(2,1)S(1)}...) all-reduce(bf16[768]{0:T(1024)(128)(2,1)S(1)} %dynamic-update-slice, ...), channel_id=1, replica_groups=mesh['dp'=4,'blk'=2,'uly'=4] {'dp'}, use_global_device_ids=true, to_apply=%add.1 | all-reduce | flops 5376 | bytes 21504
  37.1 45.4 %all-gather.7.cloned.1.call-done = bf16[768,2304]{1,0:T(8,128)(2,1)} async-done(((bf16[192,2304]{1,0:T(8,128)(2,1)}), bf16[768,2304]{1,0:T(8,128)(2,1)}) %all-gather.7.cloned.1.call-update) | async-done | bytes 3538960 | tf_op jit(solution)/shard_map/all_gather | solution.py:71
  88.9 23.2 %all_to_all.16 = bf16[1,3,4,49152]{3,1,0,2:T(4,128)(2,1)S(1)} all-to-all(bf16[1,3,4,49152]{3,1,0,2:T(4,128)(2,1)S(1)} %reshape.445), channel_id=1, replica_groups=mesh['dp'=4,'blk'=2,'uly'=4] {'uly'}, dimensions={2} | all-to-all | bytes 2359296 | tf_op jit(solution)/shard_map/all_to_all | solution.py:110
  133.7 25.9 %while.46 = (s32[]{:T(128)}, f32[1,3,1024]{2,1,0:T(4,128)S(1)}, f32[1,3,1024]{2,1,0:T(4,128)S(1)}, s32[1]{0:T(128)}, bf16[1,2048,192]{1,2,0:T(8,128)(2,1)S(1)}, ...) while((s32[]{:T(128)}, f32[1,3,1024]{2,1,0:T(4,128)S(1)}, ...), condition=%wide.region_3.4_spmd.clone, body=%wide.region_0.3_spmd.clone.sunk | while | flops 418399232 | bytes 26901672 | solution.py:149
  134.4 5.8 bitcast_reduce_fusion.4
  140.2 6.4 fusion.125
  147.4 5.8 bitcast_reduce_fusion.4
  153.2 6.3 fusion.125
  159.6 11.6 %while.47 = (s32[]{:T(128)}, f32[1,3,1024,64]{2,3,1,0:T(8,128)S(1)}, s32[1]{0:T(128)}, bf16[1,2048,384]{1,2,0:T(8,128)(2,1)}, bf16[1,1024,3,64]{1,3,2,0:T(8,128)...) while((s32[]{:T(128)}, ...), condition=%wide.region_5.6_spmd.clone, body=%wide.region_4.5_spmd.clone.sunk | while | flops 815138816 | bytes 4339905 | solution.py:165
  182.6 13.4 %all-gather = bf16[4,1,768]{2,1,0:T(2,128)(2,1)S(1)} all-gather(bf16[1,1,768]{2,1,0:T(2,128)(2,1)S(1)} %reshape.415), channel_id=1, replica_groups=mesh['dp'=4,'blk'=2,'uly'=4] {'dp'}, dimensions={0}, use_global_device_ids=true | all-gather | bytes 7680 | tf_op jit(solution)/shard_map/all_gather | solution.py:79
  202.1 52.5 %all-gather.13.cloned.1.call-done = bf16[768,3072]{1,0:T(8,128)(2,1)} async-done(((bf16[192,3072]{1,0:T(8,128)(2,1)}), bf16[768,3072]{1,0:T(8,128)(2,1)}) %all-gather.13.cloned.1.call-update) | async-done | bytes 4718608 | tf_op jit(solution)/shard_map/all_gather | solution.py:78
  254.5 11.5 %multiply_convert_fusion.1 = (bf16[256,3072]{1,0:T(8,128)(2,1)S(1)}, f32[256,3072]{1,0:T(8,128)}, f32[256,3072]{1,0:T(8,128)}) fusion(f32[3072]{0:T(1024)S(1)} %bitcast.252, bf16[768,3072]{1,0:T(8,128)(2,1)} %all-gather.13.cloned.1.call-done, f32[256,768]{1,0:T(8,128)S(1)} %get-tuple-element.738, f32[768]{0:T(1024)S(1)} %convert_element_type.213, ...), kind=kOutput, calls=%fused_computation.57 | convolution fusion | flops 1260847104 | bytes 13389824 | tf_op jit(solution)/shard_map/dot_general | solution.py:188
  266.1 77.8 %all-gather.15.cloned.1.call-done = bf16[3072,768]{1,0:T(8,128)(2,1)} async-done(((bf16[768,768]{1,0:T(8,128)(2,1)}), bf16[3072,768]{1,0:T(8,128)(2,1)}) %all-gather.15.cloned.1.call-update) | async-done | bytes 4718608 | tf_op jit(solution)/shard_map/all_gather | solution.py:80
  368.5 5.0 all-to-all-done.2
  384.5 43.3 %while.48 = (s32[]{:T(128)}, f32[1,1024,3,64]{1,3,2,0:T(8,128)S(1)}, bf16[1,2048,384]{1,2,0:T(8,128)(2,1)}, bf16[1,2048,384]{1,2,0:T(8,128)(2,1)S(1)}, s32[1]{0:...) while((s32[]{:T(128)}, ...), condition=%wide.region_16.17_spmd.clone, body=%wide.region_15.16_spmd.clone.sunk | while | flops 2040399872 | bytes 90185016 | solution.py:279
  387.5 5.2 multiply_convert_fusion.3
  395.4 4.9 fusion.144
  402.2 4.1 fusion.143
  409.0 5.2 multiply_convert_fusion.3
  416.8 4.9 fusion.144
  423.7 4.1 fusion.143
  429.4 5.1 reduce-scatter.8.cloned.1.call-done
  439.0 24.1 %all_to_all.17 = bf16[1,3,4,49152]{3,1,0,2:T(4,128)(2,1)S(1)} all-to-all(bf16[1,3,4,49152]{3,1,0,2:T(4,128)(2,1)S(1)} %copy.87), channel_id=1, replica_groups=mesh['dp'=4,'blk'=2,'uly'=4] {'uly'}, dimensions={2} | all-to-all | bytes 2359296 | tf_op jit(solution)/shard_map/all_to_all | solution.py:288
  470.3 4.0 copy.93
  477.1 5.1 convolution_convert_fusion.1
  487.6 52.8 %reduce-scatter.16.cloned.1.call-done = bf16[192,2304]{1,0:T(8,128)(2,1)} async-done(((bf16[768,2304]{1,0:T(8,128)(2,1)}), bf16[192,2304]{1,0:T(8,128)(2,1)}) %reduce-scatter.16.cloned.1.call-update) | async-done | bytes 884752
  542.7 29.6 %reduce-scatter.10.cloned.1.call-done = bf16[192,768]{1,0:T(8,128)(2,1)} async-done(((bf16[768,768]{1,0:T(8,128)(2,1)}), bf16[192,768]{1,0:T(8,128)(2,1)}) %reduce-scatter.10.cloned.1.call-update) | async-done | bytes 294928 | tf_op jit(solution)/shard_map/reduce_scatter | solution.py:325
  572.3 86.4 %reduce-scatter.12.cloned.1.call-done = bf16[192,3072]{1,0:T(8,128)(2,1)} async-done(((bf16[768,3072]{1,0:T(8,128)(2,1)}), bf16[192,3072]{1,0:T(8,128)(2,1)}) %reduce-scatter.12.cloned.1.call-update) | async-done | bytes 1179664 | tf_op jit(solution)/shard_map/reduce_scatter | solution.py:337
  658.7 88.1 %reduce-scatter.14.cloned.1.call-done = bf16[768,768]{1,0:T(8,128)(2,1)} async-done(((bf16[3072,768]{1,0:T(8,128)(2,1)}), bf16[768,768]{1,0:T(8,128)(2,1)}) %reduce-scatter.14.cloned.1.call-update) | async-done | bytes 1179664 | tf_op jit(solution)/shard_map/reduce_scatter | solution.py:343
  753.2 18.2 %all-reduce.19 = (bf16[768]{0:T(1024)(128)(2,1)S(1)}, bf16[768]{0:T(1024)(128)(2,1)S(1)}, bf16[768]{0:T(1024)(128)(2,1)S(1)}, bf16[768]{0:T(1024)(128)(2,1)S(1)}...) all-reduce(bf16[768]{0:T(1024)(128)(2,1)S(1)} %dynamic-update-slice, ...), channel_id=1, replica_groups=mesh['dp'=4,'blk'=2,'uly'=4] {'dp'}, use_global_device_ids=true, to_apply=%add.7 | all-reduce | flops 9984 | bytes 39936
  772.1 15.1 %all-reduce.17 = (bf16[192]{0:T(256)(128)(2,1)S(1)}, bf16[192]{0:T(256)(128)(2,1)S(1)}, bf16[192]{0:T(256)(128)(2,1)S(1)}, bf16[192]{0:T(256)(128)(2,1)S(1)}, bf...) all-reduce(bf16[192]{0:T(256)(128)(2,1)S(1)} %dynamic-slice.9, ...), channel_id=1, replica_groups=mesh['dp'=4,'blk'=2,'uly'=4] {'blk','uly'}, use_global_device_ids=true, to_apply=%region_22.23 | all-reduce | flops 2304 | bytes 9216 | tf_op jit(solution)/shard_map/psum | solution.py:358
  797.3 33.2 %all-reduce.23.cloned.1.call-done = (bf16[192,2304]{0,1:T(8,128)(2,1)}, bf16[192,768]{1,0:T(8,128)(2,1)}, bf16[192,3072]{1,0:T(8,128)(2,1)}, bf16[768,768]{1,0:T(8,128)(2,1)}) async-done(((bf16[192,2304]{0,1:T(8,128)(2,1)}, bf16[192,768]{1,0:T(8,128)(2,1)}, bf16[192,3072]{1,0:T(8,128)(2,1)}, bf16[768,768]{1,0:T(8,128)(2,1)}), (bf16[192,2304]{0,1:T(8,128)(2,1)}, bf16[192,768]{1,0:T(8,128)(2,1)}, ...) | async-done | bytes 3538960 | tf_op jit(solution)/shard_map/psum | solution.py:357
  (294 shorter events, 162.1 us)
Async XLA Ops:
  7.2 75.3 %all-gather.7.cloned.1.call-start = ((), (), s32[]{:S(2)}) async-start(), calls=%async_computation.9 | async-start | bytes 4423680 | tf_op jit(solution)/shard_map/all_gather | solution.py:71
  7.9 151.7 %all-gather.9.cloned.1.call-start = ((), (), s32[]{:S(2)}) async-start(), calls=%async_computation.10 | async-start | bytes 2359296 | tf_op jit(solution)/shard_map/all_gather | solution.py:151
  123.8 76.0 %all-gather.11.cloned.1.call-start = ((), (), s32[]{:S(2)}) async-start(), calls=%async_computation.11 | async-start | bytes 1474560 | tf_op jit(solution)/shard_map/all_gather | solution.py:74
  124.5 130.0 %all-gather.13.cloned.1.call-start = ((), (), s32[]{:S(2)}) async-start(), calls=%async_computation.12 | async-start | bytes 5898240 | tf_op jit(solution)/shard_map/all_gather | solution.py:78
  125.1 218.8 %all-gather.15.cloned.1.call-start = ((), (), s32[]{:S(2)}) async-start(), calls=%async_computation.13 | async-start | bytes 5898240 | tf_op jit(solution)/shard_map/all_gather | solution.py:80
  133.7 26.0 %copy-start.20 = (f32[1,3,1024,64]{2,3,1,0:T(8,128)S(1)}, f32[1,3,1024,64]{2,3,1,0:T(8,128)}, u32[]{:S(2)}) copy-start(f32[1,3,1024,64]{2,3,1,0:T(8,128)} %custom-call.2) | copy-start | bytes 2359300
  172.8 9.8 %copy-start.45 = (bf16[768]{0:T(1024)(128)(2,1)S(1)}, bf16[768]{0:T(1024)(128)(2,1)}, u32[]{:S(2)}) copy-start(bf16[768]{0:T(1024)(128)(2,1)} %param.33) | copy-start | bytes 4612
  177.9 21.9 %copy-start.23 = (bf16[1,256,768]{2,1,0:T(8,128)(2,1)S(1)}, bf16[1,256,768]{2,1,0:T(8,128)(2,1)}, u32[]{:S(2)}) copy-start(bf16[1,256,768]{2,1,0:T(8,128)(2,1)} %param.22) | copy-start | bytes 1179652
  179.1 17.0 %all-to-all-start.1 = ((bf16[4,2,24576]{2,1,0:T(2,128)(2,1)}), bf16[4,2,24576]{2,1,0:T(2,128)(2,1)S(1)}, u32[]{:S(2)}, u32[]{:S(2)}) async-start(bf16[4,2,24576]{2,1,0:T(2,128)(2,1)} %reshape.461), calls=%async_computation.1 | async-start | bytes 786432 | tf_op jit(solution)/shard_map/all_to_all | solution.py:176
  199.8 54.8 %copy-start.14 = (bf16[1,256,4,192]{1,3,2,0:T(8,128)(2,1)}, bf16[1,256,4,192]{1,3,2,0:T(8,128)(2,1)S(1)}, u32[]{:S(2)}) copy-start(bf16[1,256,4,192]{1,3,2,0:T(8,128)(2,1)S(1)} %copy.77) | copy-start | bytes 1179652
  201.8 153.5 %copy-start.2 = (f32[256,768]{1,0:T(8,128)}, f32[256,768]{1,0:T(8,128)S(1)}, u32[]{:S(2)}) copy-start(f32[256,768]{1,0:T(8,128)S(1)} %get-tuple-element.738) | copy-start | bytes 2359300
  201.8 153.5 %copy-start.28 = (f32[256]{0:T(256)}, f32[256]{0:T(256)S(1)}, u32[]{:S(2)}) copy-start(f32[256]{0:T(256)S(1)} %broadcast_multiply_fusion.6) | copy-start | bytes 3076
  202.1 153.2 %copy-start.35 = (f32[256]{0:T(256)}, f32[256]{0:T(256)S(1)}, u32[]{:S(2)}) copy-start(f32[256]{0:T(256)S(1)} %add_rsqrt_fusion.1) | copy-start | bytes 3076
  266.1 81.8 %copy-start.12 = (bf16[256,3072]{1,0:T(8,128)(2,1)}, bf16[256,3072]{1,0:T(8,128)(2,1)S(1)}, u32[]{:S(2)}) copy-start(bf16[256,3072]{1,0:T(8,128)(2,1)S(1)} %get-tuple-element.725) | copy-start | bytes 4718596
  343.9 6.1 slice-start.2
  343.9 6.1 slice-start.3
  343.9 6.1 copy-start.47
  357.6 9.2 %copy-start.22 = (f32[1,3,1024,64]{2,3,1,0:T(8,128)S(1)}, f32[1,3,1024,64]{2,3,1,0:T(8,128)}, u32[]{:S(2)}) copy-start(f32[1,3,1024,64]{2,3,1,0:T(8,128)} %copy-done.21) | copy-start | bytes 2359300
  363.0 10.4 %all-to-all-start.2 = ((bf16[4,2,24576]{2,1,0:T(2,128)(2,1)}), bf16[4,2,24576]{2,1,0:T(2,128)(2,1)S(1)}, u32[]{:S(2)}, u32[]{:S(2)}) async-start(bf16[4,2,24576]{2,1,0:T(2,128)(2,1)} %reshape.463), calls=%async_computation.2 | async-start | bytes 786432 | tf_op jit(solution)/shard_map/all_to_all | solution.py:226
  366.7 67.8 %reduce-scatter.8.cloned.1.call-start = ((), (), s32[]{:S(2)}) async-start(), calls=%async_computation.14 | async-start | bytes 2359296 | tf_op jit(solution)/shard_map/reduce_scatter | solution.py:280
  427.8 112.6 %reduce-scatter.16.cloned.1.call-start = ((), (), s32[]{:S(2)}) async-start(), calls=%async_computation.18 | async-start | bytes 4423680
  474.3 98.0 %reduce-scatter.10.cloned.1.call-start = ((), (), s32[]{:S(2)}) async-start(), calls=%async_computation.15 | async-start | bytes 1474560 | tf_op jit(solution)/shard_map/reduce_scatter | solution.py:325
  477.1 181.6 %reduce-scatter.12.cloned.1.call-start = ((), (), s32[]{:S(2)}) async-start(), calls=%async_computation.16 | async-start | bytes 5898240 | tf_op jit(solution)/shard_map/reduce_scatter | solution.py:337
  482.3 264.5 %reduce-scatter.14.cloned.1.call-start = ((), (), s32[]{:S(2)}) async-start(), calls=%async_computation.17 | async-start | bytes 5898240 | tf_op jit(solution)/shard_map/reduce_scatter | solution.py:343
  487.5 259.3 %copy-start.17 = (bf16[1,256,768]{2,1,0:T(8,128)(2,1)S(1)}, bf16[1,256,768]{2,1,0:T(8,128)(2,1)}, u32[]{:S(2)}) copy-start(bf16[1,256,768]{2,1,0:T(8,128)(2,1)} %param.24) | copy-start | bytes 1179652
  487.5 262.2 %copy-start.5 = (bf16[1,3,4,256,192]{4,3,2,1,0:T(8,128)(2,1)S(1)}, bf16[1,3,4,256,192]{4,3,2,1,0:T(8,128)(2,1)}, u32[]{:S(2)}) copy-start(bf16[1,3,4,256,192]{4,3,2,1,0:T(8,128)(2,1)} %copy-done.4) | copy-start | bytes 3538948
  487.5 342.9 %all-reduce.23.cloned.1.call-start = ((), (), s32[]{:S(2)}) async-start(), calls=%async_computation.19 | async-start | bytes 7667712 | tf_op jit(solution)/shard_map/psum | solution.py:357
  746.8 6.3 copy-start.37
  746.8 45.5 %copy-start.7 = (f32[256,768]{1,0:T(8,128)S(1)}, f32[256,768]{1,0:T(8,128)}, u32[]{:S(2)}) copy-start(f32[256,768]{1,0:T(8,128)} %copy-done.6) | copy-start | bytes 2359300
  746.8 45.5 %copy-start.31 = (f32[256]{0:T(256)S(1)}, f32[256]{0:T(256)}, u32[]{:S(2)}) copy-start(f32[256]{0:T(256)} %copy-done.30) | copy-start | bytes 3076
  747.5 5.7 copy-start.43
  747.5 5.7 copy-start.44
  (36 other events, 105.1 us)
Sparse Core Ops, SparseCore 0:
  9.6 72.8 all-gather.6
  123.9 7.2 all-gather.8
  132.8 31.6 all-gather.10
  165.8 88.6 all-gather.12
  256.0 87.8 all-gather.14
  427.9 6.5 reduce-scatter.7
  474.5 65.8 reduce-scatter.15
  542.8 29.4 reduce-scatter.9
  574.7 83.9 reduce-scatter.11
  660.9 85.7 reduce-scatter.13
  751.6 78.8 all-reduce.22
where the time goes:
time: 852 us; the launch traced here: 844 us
  waiting for transfers between devices  478 us (56%)
  blocking collectives  118 us (14%)
  matrix products  98.3 us (12%)
  local copies, waits for them, and re-layouts  75.7 us (9%)
  other arithmetic  48.4 us (6%)
  between operations  16.9 us (2%)
    reduce_scatter x1, waiting for transfers between devices, on_device(): lax.psum_scatter(param_grads[9].astype(jnp.bfloat16), 'dp', scatter_dimen...  88.1 us
    reduce_scatter x1, waiting for transfers between devices, on_device(): lax.psum_scatter(param_grads[7].astype(jnp.bfloat16), 'dp', scatter_dimen...  86.4 us
    all_gather x1, waiting for transfers between devices, on_device(): lax.all_gather(shrink_weight, 'dp', axis=0, tiled=True)  77.8 us
    unnamed x12, waiting for transfers between devices  55.3 us
    all_gather x1, waiting for transfers between devices, on_device(): lax.all_gather(expand_weight, 'dp', axis=0, tiled=True)  52.5 us
    all_gather x1, waiting for transfers between devices, on_device(): lax.all_gather(attend_weight, 'dp', axis=0, tiled=True)  45.4 us
    unnamed x2, blocking collectives  39.5 us
    psum x1, waiting for transfers between devices, on_device(): lax.psum(owned_grads[0].astype(jnp.bfloat16), ('blk', 'uly'))  33.2 us
  transfers between devices with their start and end apart: 13, of which 10 were waited for; matrix products, arithmetic and copies ran while one was open for 12% of the time, Pallas kernels for 0%

commit v1 on v0

v1 whole, which is shorter than its diff:
```python
import functools

import jax
import jax.numpy as jnp
from jax import lax
from jax.experimental import pallas as pl
from jax.experimental.pallas import tpu as pltpu
from jax.sharding import PartitionSpec as P

HEADS = 12
HD = 64

EPSILON = 1e-12
MASKED = -1000000000.0
LOG2E = 1.4426950408889634
LN2 = 0.6931471805599453
F32 = jnp.float32
BF16 = jnp.bfloat16


def dot_nn(left, right):
    return lax.dot_general(left, right, (((1,), (0,)), ((), ())), preferred_element_type=F32)


def dot_nt(left, right):
    return lax.dot_general(left, right, (((1,), (1,)), ((), ())), preferred_element_type=F32)


def dot_tn(left, right):
    return lax.dot_general(left, right, (((0,), (0,)), ((), ())), preferred_element_type=F32)


def swap_with(value, axis, offset):
    size = lax.axis_size(axis)
    return lax.ppermute(value, axis, [(i, i ^ offset) for i in range(size)])


def xor_order(pieces, index):
    bit = 1
    while bit < len(pieces):
        flag = (index & bit) != 0
        pieces = [jnp.where(flag, pieces[p ^ bit], pieces[p]) for p in range(len(pieces))]
        bit *= 2
    return pieces


def total(values):
    acc = values[0].astype(F32)
    for value in values[1:]:
        acc = acc + value.astype(F32)
    return acc


def pad_rows(value, rows):
    return jnp.pad(value, ((0, rows - value.shape[0]), (0, 0)))


def head_lanes(width, head, ones_lane=None):
    lane = lax.broadcasted_iota(jnp.int32, (1, width), 1)
    keep = (lane >= head * HD) & (lane < (head + 1) * HD)
    if ones_lane is not None:
        keep = keep | (lane == ones_lane)
    return keep


def attend_forward_kernel(heads, blocks, q_ref, *refs):
    kv_refs = refs[:blocks]
    o_ref, lse_ref, vt_ref = refs[blocks:]
    group = heads * HD
    wide = q_ref.shape[1]
    rows = kv_refs[0].shape[0]

    @pl.when(pl.program_id(0) == 0)
    def _():
        for i in range(blocks):
            vt_ref[:, i * rows : (i + 1) * rows] = kv_refs[i][:, wide : wide + group].T

    q = q_ref[...]
    outs = []
    stats = []
    for head in range(heads):
        q_head = jnp.where(head_lanes(wide, head, group), q, jnp.zeros_like(q))
        scores = [dot_nt(kv_refs[i][:, :wide], q_head) for i in range(blocks)]
        top = jnp.max(scores[0], axis=0, keepdims=True)
        for i in range(1, blocks):
            top = jnp.maximum(top, jnp.max(scores[i], axis=0, keepdims=True))
        norm = jnp.zeros_like(top)
        acc = None
        for i in range(blocks):
            probs = jnp.exp2(scores[i] - top)
            norm = norm + jnp.sum(probs, axis=0, keepdims=True)
            part = dot_nn(
                vt_ref[head * HD : (head + 1) * HD, i * rows : (i + 1) * rows], probs.astype(BF16)
            )
            acc = part if acc is None else acc + part
        outs.append(acc / norm)
        stats.append(top + jnp.log2(norm))
    o_ref[...] = jnp.concatenate(outs, axis=0).T.astype(BF16)
    for head in range(heads):
        lse_ref[head : head + 1, :] = stats[head]


def attend_forward(q, kvs, heads, tile):
    rows, wide = q.shape
    group = heads * HD
    blocks = len(kvs)
    keys = blocks * rows
    whole = pl.BlockSpec(kvs[0].shape, lambda t: (0, 0))
    return pl.pallas_call(
        functools.partial(attend_forward_kernel, heads, blocks),
        grid=(rows // tile,),
        in_specs=[pl.BlockSpec((tile, wide), lambda t: (t, 0))] + [whole] * blocks,
        out_specs=[
            pl.BlockSpec((tile, group), lambda t: (t, 0)),
            pl.BlockSpec((8, tile), lambda t: (0, t)),
        ],
        out_shape=[
            jax.ShapeDtypeStruct((rows, group), BF16),
            jax.ShapeDtypeStruct((8, rows), F32),
        ],
        scratch_shapes=[pltpu.VMEM((group, keys), BF16)],
        compiler_params=pltpu.CompilerParams(vmem_limit_bytes=56 * 2**20),
        cost_estimate=pl.CostEstimate(
            flops=4 * heads * rows * keys * wide,
            transcendentals=heads * rows * keys,
            bytes_accessed=2 * rows * wide * 3 + 2 * keys * (wide + group),
        ),
        name="attend_forward",
    )(q, *kvs)


def attend_backward_kernel(heads, blocks, q_ref, do_ref, o_ref, lse_ref, *refs):
    kv_refs = refs[:blocks]
    dq_ref = refs[blocks]
    dkv_refs = refs[blocks + 1 : 2 * blocks + 1]
    kt_ref = refs[2 * blocks + 1]
    dk_accs = refs[2 * blocks + 2 : 3 * blocks + 2]
    dv_accs = refs[3 * blocks + 2 :]
    group = heads * HD
    wide = q_ref.shape[1]
    rows = kv_refs[0].shape[0]

    @pl.when(pl.program_id(0) == 0)
    def _():
        for i in range(blocks):
            kt_ref[:, i * rows : (i + 1) * rows] = kv_refs[i][:, :group].T
            dk_accs[i][...] = jnp.zeros_like(dk_accs[i])
            dv_accs[i][...] = jnp.zeros_like(dv_accs[i])

    q = q_ref[...]
    dout = do_ref[...]
    products = (dout.astype(F32) * o_ref[...].astype(F32)).T
    dqs = []
    for head in range(heads):
        q_head = jnp.where(head_lanes(wide, head, group), q, jnp.zeros_like(q))
        do_head = jnp.where(head_lanes(group, head), dout, jnp.zeros_like(dout))
        lse = lse_ref[head : head + 1, :]
        delta = jnp.sum(products[head * HD : (head + 1) * HD], axis=0, keepdims=True)
        acc = None
        for i in range(blocks):
            probs = jnp.exp2(dot_nt(kv_refs[i][:, :wide], q_head) - lse)
            dv_accs[i][...] += dot_nn(probs.astype(BF16), do_head)
            grads = dot_nt(kv_refs[i][:, wide : wide + group], do_head)
            grads = (probs * (grads - delta)).astype(BF16)
            dk_accs[i][...] += dot_nn(grads, q_head)
            part = dot_nn(
                kt_ref[head * HD : (head + 1) * HD, i * rows : (i + 1) * rows], grads
            )
            acc = part if acc is None else acc + part
        dqs.append(acc)
    dq_ref[...] = jnp.concatenate(dqs, axis=0).T.astype(BF16)

    @pl.when(pl.program_id(0) == pl.num_programs(0) - 1)
    def _():
        for i in range(blocks):
            dkv_refs[i][:, :group] = (dk_accs[i][:, :group] * LN2).astype(BF16)
            dkv_refs[i][:, wide : wide + group] = dv_accs[i][...].astype(BF16)


def attend_backward(q, kvs, dout, o, lse, heads, tile):
    rows, wide = q.shape
    group = heads * HD
    blocks = len(kvs)
    keys = blocks * rows
    whole = pl.BlockSpec(kvs[0].shape, lambda t: (0, 0))
    out = pl.pallas_call(
        functools.partial(attend_backward_kernel, heads, blocks),
        grid=(rows // tile,),
        in_specs=[
            pl.BlockSpec((tile, wide), lambda t: (t, 0)),
            pl.BlockSpec((tile, group), lambda t: (t, 0)),
            pl.BlockSpec((tile, group), lambda t: (t, 0)),
            pl.BlockSpec((8, tile), lambda t: (0, t)),
        ]
        + [whole] * blocks,
        out_specs=[pl.BlockSpec((tile, group), lambda t: (t, 0))] + [whole] * blocks,
        out_shape=[jax.ShapeDtypeStruct((rows, group), BF16)]
        + [jax.ShapeDtypeStruct(kvs[0].shape, BF16)] * blocks,
        scratch_shapes=[pltpu.VMEM((group, keys), BF16)]
        + [pltpu.VMEM((rows, wide), F32)] * blocks
        + [pltpu.VMEM((rows, group), F32)] * blocks,
        compiler_params=pltpu.CompilerParams(vmem_limit_bytes=56 * 2**20),
        cost_estimate=pl.CostEstimate(
            flops=10 * heads * rows * keys * wide,
            transcendentals=heads * rows * keys,
            bytes_accessed=2 * rows * wide * 4 + 4 * keys * (wide + group),
        ),
        name="attend_backward",
    )(q, dout, o, lse, *kvs)
    return out[0], out[1:]


def feed_kernel(
    x1_ref,
    x1b_ref,
    expand_ref,
    shrink_ref,
    ebias_ref,
    sbias_ref,
    gain_ref,
    shift_ref,
    cot_ref,
    mixed_ref,
    dx1_ref,
    dexpand_ref,
    dshrink_ref,
    debias_ref,
    vec_ref,
    act_ref,
    slope_ref,
    acc_ref,
    d2b_ref,
    x1t_ref,
):
    phase = pl.program_id(0)
    step = pl.program_id(1)
    last = pl.num_programs(1) - 1
    width = x1_ref.shape[1]

    @pl.when(phase == 0)
    def _():
        pre = dot_nn(x1b_ref[...], expand_ref[0]) + ebias_ref[0]
        cdf = 0.5 * (1.0 + lax.erf(pre * 0.7071067811865476))
        pdf = jnp.exp(-0.5 * pre * pre) * 0.3989422804014327
        act = (pre * cdf).astype(BF16)
        act_ref[step] = act
        slope_ref[step] = (cdf + pre * pdf).astype(BF16)
        part = dot_nn(act, shrink_ref[0])

        @pl.when(step == 0)
        def _():
            acc_ref[...] = part
            x1t_ref[...] = x1b_ref[...].T

        @pl.when(step > 0)
        def _():
            acc_ref[...] += part

        @pl.when(step == last)
        def _():
            hidden = x1_ref[...] + (acc_ref[...] + sbias_ref[...])
            center = hidden - jnp.mean(hidden, -1, keepdims=True)
            inverse = lax.rsqrt(jnp.mean(center * center, -1, keepdims=True) + EPSILON)
            normed = center * inverse
            mixed_ref[...] = (normed * gain_ref[...] + shift_ref[...]).astype(BF16)
            grad = cot_ref[...].astype(F32)
            scaled = grad * gain_ref[...]
            dhidden = inverse * (
                scaled
                - jnp.mean(scaled, -1, keepdims=True)
                - normed * jnp.mean(scaled * normed, -1, keepdims=True)
            )
            acc_ref[...] = dhidden
            d2b_ref[...] = dhidden.astype(BF16)
            vec_ref[...] = jnp.zeros_like(vec_ref)
            vec_ref[0:1, :] = jnp.sum(grad * normed, 0, keepdims=True)
            vec_ref[1:2, :] = jnp.sum(grad, 0, keepdims=True)
            vec_ref[2:3, :] = jnp.sum(dhidden, 0, keepdims=True)

    @pl.when(phase == 1)
    def _():
        d2b = d2b_ref[...]
        dpre = (dot_nt(d2b, shrink_ref[0]) * slope_ref[step].astype(F32)).astype(BF16)
        debias_ref[0] = jnp.sum(dpre.astype(F32), 0, keepdims=True)
        dexpand_ref[0] = dot_nn(x1t_ref[...], dpre).astype(BF16)
        dshrink_ref[0] = dot_tn(act_ref[step], d2b).astype(BF16)
        acc_ref[...] += dot_nt(dpre, expand_ref[0])

        @pl.when(step == last)
        def _():
            dx1_ref[...] = acc_ref[...]


def feed_forward_backward(x1, x1b, expand, shrink, ebias, sbias, gain, shift, cot):
    rows, width = x1.shape
    parts, _, block = expand.shape
    full = pl.BlockSpec((rows, width), lambda p, k: (0, 0))
    line = pl.BlockSpec((1, width), lambda p, k: (0, 0))
    return pl.pallas_call(
        feed_kernel,
        grid=(2, parts),
        in_specs=[
            full,
            full,
            pl.BlockSpec((1, width, block), lambda p, k: (k, 0, 0)),
            pl.BlockSpec((1, block, width), lambda p, k: (k, 0, 0)),
            pl.BlockSpec((1, 1, block), lambda p, k: (k, 0, 0)),
            line,
            line,
            line,
            full,
        ],
        out_specs=[
            full,
            full,
            pl.BlockSpec((1, width, block), lambda p, k: (p * k, 0, 0)),
            pl.BlockSpec((1, block, width), lambda p, k: (p * k, 0, 0)),
            pl.BlockSpec((1, 1, block), lambda p, k: (p * k, 0, 0)),
            pl.BlockSpec((8, width), lambda p, k: (0, 0)),
        ],
        out_shape=[
            jax.ShapeDtypeStruct((rows, width), BF16),
            jax.ShapeDtypeStruct((rows, width), F32),
            jax.ShapeDtypeStruct((parts, width, block), BF16),
            jax.ShapeDtypeStruct((parts, block, width), BF16),
            jax.ShapeDtypeStruct((parts, 1, block), F32),
            jax.ShapeDtypeStruct((8, width), F32),
        ],
        scratch_shapes=[
            pltpu.VMEM((parts, rows, block), BF16),
            pltpu.VMEM((parts, rows, block), BF16),
            pltpu.VMEM((rows, width), F32),
            pltpu.VMEM((rows, width), BF16),
            pltpu.VMEM((width, rows), BF16),
        ],
        compiler_params=pltpu.CompilerParams(vmem_limit_bytes=48 * 2**20),
        cost_estimate=pl.CostEstimate(
            flops=12 * rows * width * parts * block,
            transcendentals=2 * rows * parts * block,
            bytes_accessed=12 * width * parts * block,
        ),
        name="feed_forward_backward",
    )(x1, x1b, expand, shrink, ebias, sbias, gain, shift, cot)


def on_device(
    tokens,
    lengths,
    cotangent,
    attend_weight,
    query_bias,
    value_bias,
    mixer_weight,
    mixer_bias,
    attn_gain,
    attn_shift,
    expand_weight,
    expand_bias,
    shrink_weight,
    shrink_bias,
    final_gain,
    final_shift,
):
    uly = lax.axis_size("uly")
    blk = lax.axis_size("blk")
    dp = lax.axis_size("dp")
    u = lax.axis_index("uly")
    b = lax.axis_index("blk")
    z = lax.axis_index("dp")
    width = tokens.shape[-1]
    rows = tokens.shape[0] * tokens.shape[1]
    block_rows = uly * rows
    heads = HEADS // uly
    group = heads * HD
    wide = -(-(group + 1) // 128) * 128
    shard = attend_weight.shape[0]
    hidden = expand_weight.shape[1]
    parts = blk * uly
    unit = hidden // (parts * dp)
    share = shard // blk

    x = tokens.reshape(rows, width)
    x_rows = jnp.concatenate([x] + [swap_with(x, "uly", j) for j in range(1, uly)], 0)

    small = jnp.concatenate(
        [query_bias, value_bias, mixer_bias, attn_gain, attn_shift, shrink_bias]
        + [final_gain, final_shift, expand_bias]
    )
    small_rows = small.shape[0] // (3 * group)
    own_heads = lax.dynamic_slice_in_dim(attend_weight.reshape(shard, 3, uly, group), u, 1, 2)
    own_heads = own_heads.reshape(shard, 3 * group)
    first_piece = jnp.concatenate(
        [
            lax.dynamic_slice_in_dim(own_heads, b * share, share, 0),
            pad_rows(small.reshape(small_rows, 3 * group), 16),
        ]
    )
    first_all = lax.all_gather(first_piece, "dp", axis=0, tiled=False)
    halves = first_all[:, :share]
    halves = xor_order([halves] + [swap_with(halves, "blk", i) for i in range(1, blk)], b)
    attend_own = jnp.stack(halves, 1).reshape(width, 3, group)
    vectors = first_all[:, share : share + small_rows].reshape(dp, -1, shard).astype(F32)
    names = [vectors[:, k].reshape(width) for k in range(8)]
    bias_query, bias_value, bias_mixer, gain_attn, shift_attn, bias_shrink = names[:6]
    gain_final, shift_final = names[6:]
    bias_expand = vectors[:, 8:].reshape(dp, parts, unit).transpose(1, 0, 2)
    bias_expand = jnp.stack(
        xor_order(list(bias_expand.reshape(parts, dp * unit)), b * uly + u), 0
    ).reshape(parts, 1, dp * unit)

    mixer_own = lax.dynamic_slice_in_dim(mixer_weight, b * share, share, 0)
    mixer_all = jnp.stack(
        xor_order([mixer_own] + [swap_with(mixer_own, "dp", j) for j in range(1, dp)], z), 0
    )
    mixer_all = jnp.stack(
        xor_order([mixer_all] + [swap_with(mixer_all, "blk", i) for i in range(1, blk)], b), 1
    ).reshape(width, width)

    part = b * uly + u
    expand_own = lax.dynamic_slice_in_dim(
        expand_weight.reshape(shard, dp, parts, unit), part, 1, 2
    ).reshape(-1, width)
    shrink_own = lax.dynamic_slice_in_dim(shrink_weight.reshape(parts, unit, width), part, 1, 0)
    expand_rows = expand_own.shape[0]
    feed_own = jnp.concatenate([expand_own, shrink_own.reshape(unit, width)], 0)
    feed_all = lax.all_gather(feed_own, "dp", axis=0, tiled=False)
    expand_part = feed_all[:, :expand_rows].reshape(width, dp * unit)
    shrink_part = feed_all[:, expand_rows:].reshape(dp * unit, width)
    expand_two = jnp.stack([expand_part, swap_with(expand_part, "uly", 1)])
    shrink_two = jnp.stack([shrink_part, swap_with(shrink_part, "uly", 2)])
    expand_far = swap_with(expand_two, "uly", 2)
    shrink_far = swap_with(shrink_two, "uly", 1)
    expand_here = jnp.concatenate([expand_two, expand_far], 0)
    shrink_here = jnp.stack([shrink_two[0], shrink_far[0], shrink_two[1], shrink_far[1]], 0)
    expand_full = jnp.concatenate(
        [expand_here] + [swap_with(expand_here, "blk", i) for i in range(1, blk)], 0
    )
    shrink_full = jnp.concatenate(
        [shrink_here] + [swap_with(shrink_here, "blk", i) for i in range(1, blk)], 0
    )

    lane_pad = ((0, 0), (0, wide - group))
    bias_row = jnp.pad(lax.dynamic_slice_in_dim(bias_query, u * group, group, 0), lane_pad[1:])
    ones_lane = (jnp.arange(wide) == group).astype(F32)
    q = dot_nn(x_rows, jnp.pad(attend_own[:, 0], lane_pad)) + bias_row
    q = (q * (0.125 * LOG2E) + ones_lane).astype(BF16)
    kv_weight = jnp.concatenate([jnp.pad(attend_own[:, 1], lane_pad), attend_own[:, 2]], 1)
    kv_bias = jnp.concatenate(
        [jnp.zeros((wide,), F32), lax.dynamic_slice_in_dim(bias_value, u * group, group, 0)]
    )
    kv_ones = jnp.pad(ones_lane, (0, group))
    row_index = jnp.arange(block_rows, dtype=jnp.int32)
    positions = b * block_rows + ((row_index // rows) ^ u) * rows + row_index % rows
    key_mask = jnp.where(positions < lengths[0], 0.0, MASKED)
    kv = (dot_nn(x_rows, kv_weight) + kv_bias + key_mask[:, None] * kv_ones).astype(BF16)
    kvs = [kv] + [swap_with(kv, "blk", i) for i in range(1, blk)]

    o_rows, lse = attend_forward(q, kvs, heads, min(256, block_rows))
    pieces = [o_rows[j * rows : (j + 1) * rows] for j in range(uly)]
    pieces = [pieces[0]] + [swap_with(pieces[j], "uly", j) for j in range(1, uly)]
    mixer_in = jnp.concatenate(xor_order(pieces, u), 1)

    first_sum = x.astype(F32) + (dot_nn(mixer_in, mixer_all) + bias_mixer)
    center = first_sum - jnp.mean(first_sum, -1, keepdims=True)
    first_inv = lax.rsqrt(jnp.mean(center * center, -1, keepdims=True) + EPSILON)
    first_normed = center * first_inv
    first_out = first_normed * gain_attn + shift_attn
    first_low = first_out.astype(BF16)

    mixed, first_grad, expand_grad, shrink_grad, expand_bias_grad, vec_grads = (
        feed_forward_backward(
            first_out,
            first_low,
            expand_full,
            shrink_full,
            bias_expand,
            bias_shrink[None],
            gain_final[None],
            shift_final[None],
            cotangent.reshape(rows, width),
        )
    )

    scaled = first_grad * gain_attn
    attn_grad = first_inv * (
        scaled
        - jnp.mean(scaled, -1, keepdims=True)
        - first_normed * jnp.mean(scaled * first_normed, -1, keepdims=True)
    )
    attn_low = attn_grad.astype(BF16)
    out_grad = dot_nt(attn_low, mixer_all).astype(BF16)
    sends = xor_order([out_grad[:, j * group : (j + 1) * group] for j in range(uly)], u)
    dout_rows = jnp.concatenate(
        [sends[0]] + [swap_with(sends[j], "uly", j) for j in range(1, uly)], 0
    )
    dq, dkvs = attend_backward(q, kvs, dout_rows, o_rows, lse, heads, min(256, block_rows))

    mixer_grad = dot_tn(mixer_in, attn_low).astype(BF16)
    attn_gain_grad = jnp.sum(first_grad * first_normed, 0)
    attn_shift_grad = jnp.sum(first_grad, 0)
    mixer_bias_grad = jnp.sum(attn_grad, 0)
    ebg = jnp.stack(xor_order(list(expand_bias_grad.reshape(parts, dp * unit)), part), 0)
    ebg = ebg.reshape(parts, dp, unit).transpose(1, 0, 2).reshape(dp, parts * unit)
    vec_all = jnp.concatenate(
        [
            v.reshape(dp, shard)
            for v in (
                mixer_bias_grad,
                attn_gain_grad,
                attn_shift_grad,
                vec_grads[2],
                vec_grads[0],
                vec_grads[1],
            )
        ]
        + [ebg],
        1,
    ).astype(BF16)

    mixer_cols = width // blk
    mixer_part_rows = shard // uly
    vec_len = vec_all.shape[1]
    vec_rows = -(-vec_len // mixer_cols)
    vec_rows = -(-vec_rows // 16) * 16
    vec_block = jnp.pad(vec_all, ((0, 0), (0, vec_rows * mixer_cols - vec_len))).reshape(
        dp, vec_rows, mixer_cols
    )
    mixer_view = mixer_grad.reshape(dp, uly, mixer_part_rows, blk, mixer_cols)
    by_blk = xor_order([mixer_view[:, :, :, i] for i in range(blk)], b)
    mixer_parts = []
    for i in range(blk):
        by_uly = xor_order([by_blk[i][:, j] for j in range(uly)], u)
        mixer_parts.append(
            jnp.stack([jnp.concatenate([piece, vec_block], 1) for piece in by_uly], 0)
        )
    mixer_sum = total(
        [mixer_parts[0]] + [swap_with(mixer_parts[i], "blk", i) for i in range(1, blk)]
    ).astype(BF16)
    mixer_sum = total(
        [mixer_sum[0]] + [swap_with(mixer_sum[j], "uly", j) for j in range(1, uly)]
    ).astype(BF16)

    def over_blk(grad):
        return total(
            [grad[:uly]]
            + [swap_with(grad[i * uly : (i + 1) * uly], "blk", i) for i in range(1, blk)]
        ).astype(BF16)

    shrink_sum = over_blk(shrink_grad)
    expand_sum = over_blk(expand_grad)
    shrink_sum = shrink_sum.reshape(2, 2, dp * unit, width)
    expand_sum = expand_sum.reshape(2, 2, width, dp * unit)
    shrink_sum = total([shrink_sum[0], swap_with(shrink_sum[1], "uly", 2)]).astype(BF16)
    expand_sum = total([expand_sum[:, 0], swap_with(expand_sum[:, 1], "uly", 1)]).astype(BF16)
    shrink_sum = total([shrink_sum[0], swap_with(shrink_sum[1], "uly", 1)]).astype(BF16)
    expand_sum = total([expand_sum[0], swap_with(expand_sum[1], "uly", 2)]).astype(BF16)

    mixer_rows = mixer_sum.shape[1] * mixer_cols // width
    packed = jnp.concatenate(
        [
            expand_sum.reshape(dp, expand_rows, width),
            shrink_sum.reshape(dp, unit, width),
            mixer_sum.reshape(dp, mixer_rows, width),
        ],
        1,
    )

    def over_dp(value):
        sends = [lax.dynamic_slice_in_dim(value, z ^ j, 1, 0)[0] for j in range(dp)]
        return total([sends[0]] + [swap_with(sends[j], "dp", j) for j in range(1, dp)])

    owned = over_dp(packed)
    vec_owned = owned[expand_rows + unit :].reshape(-1, mixer_cols)[mixer_part_rows:]
    vec_owned = vec_owned.reshape(-1)[:vec_len]

    def in_plane(value):
        value = value.astype(BF16)
        value = jnp.stack(
            xor_order([value] + [swap_with(value, "uly", j) for j in range(1, uly)], u), 0
        )
        return jnp.stack(
            xor_order([value] + [swap_with(value, "blk", i) for i in range(1, blk)], b), 0
        )

    gathered = in_plane(owned).reshape(parts, -1, width)
    expand_out = gathered[:, :expand_rows].reshape(parts, shard, dp, unit)
    expand_out = expand_out.transpose(1, 2, 0, 3).reshape(shard, hidden).astype(F32)
    shrink_out = gathered[:, expand_rows : expand_rows + unit]
    shrink_out = shrink_out.reshape(parts * unit, width).astype(F32)
    mixer_out = gathered[:, expand_rows + unit :].reshape(blk, uly, -1, mixer_cols)
    mixer_out = mixer_out[:, :, :mixer_part_rows].transpose(1, 2, 0, 3)
    mixer_out = mixer_out.reshape(shard, width).astype(F32)

    own_dkv = total([dkvs[0]] + [swap_with(dkvs[i], "blk", i) for i in range(1, blk)])
    own_dkv = own_dkv.astype(BF16)
    proj_grad = jnp.concatenate(
        [dq * jnp.asarray(0.125, BF16), own_dkv[:, :group], own_dkv[:, wide : wide + group]], 1
    )
    token_parts = dot_nt(proj_grad, attend_own.reshape(width, 3 * group))
    token_low = token_parts.astype(BF16)
    tokens_grad = attn_grad + total(
        [token_parts[:rows]]
        + [swap_with(token_low[j * rows : (j + 1) * rows], "uly", j) for j in range(1, uly)]
    )
    attend_grad = dot_tn(x_rows, proj_grad).astype(BF16)
    attend_grad = attend_grad.reshape(dp, blk, share, 3 * group)
    bias_sum = jnp.sum(proj_grad.astype(F32), 0)[None]
    bias_rows = pad_rows(bias_sum.astype(BF16), 16)
    attend_parts = [
        jnp.concatenate(
            [
                lax.dynamic_slice_in_dim(attend_grad, b ^ i, 1, 1).reshape(-1, 3 * group),
                bias_rows,
            ],
            0,
        )
        for i in range(blk)
    ]
    attend_sum = total(
        [attend_parts[0]] + [swap_with(attend_parts[i], "blk", i) for i in range(1, blk)]
    ).astype(BF16)
    bias_half = jnp.broadcast_to(attend_sum[dp * share :], (dp, 16, 3 * group))
    attend_sum = attend_sum[: dp * share].reshape(dp, share, 3 * group)
    attend_owned = over_dp(jnp.concatenate([attend_sum, bias_half], 1))
    attend_all = in_plane(attend_owned)
    attend_out = attend_all[:, :, :share].reshape(blk, uly, share, 3, group)
    attend_out = attend_out.transpose(0, 2, 3, 1, 4).reshape(shard, 3 * width).astype(F32)
    bias_out = attend_all[0, :, share].astype(F32).reshape(uly, 3, group)
    query_bias_grad = lax.dynamic_slice_in_dim(bias_out[:, 0].reshape(width), z * shard, shard, 0)
    value_bias_grad = lax.dynamic_slice_in_dim(bias_out[:, 2].reshape(width), z * shard, shard, 0)

    vecs = [vec_owned[k * shard : (k + 1) * shard] for k in range(6)]
    return (
        mixed.reshape(tokens.shape),
        tokens_grad.reshape(tokens.shape),
        attend_out,
        query_bias_grad,
        value_bias_grad,
        mixer_out,
        vecs[0],
        vecs[1],
        vecs[2],
        expand_out,
        vec_owned[6 * shard :],
        shrink_out,
        vecs[3],
        vecs[4],
        vecs[5],
    )


def solution(mesh):
    row_spec = P("dp", ("blk", "uly"), None)
    matrix = P("dp", None)
    vector = P("dp")
    return jax.shard_map(
        on_device,
        mesh=mesh,
        in_specs=(
            row_spec,
            vector,
            row_spec,
            matrix,
            vector,
            vector,
            matrix,
            vector,
            vector,
            vector,
            matrix,
            vector,
            matrix,
            vector,
            vector,
            vector,
        ),
        out_specs=(
            row_spec,
            row_spec,
            matrix,
            vector,
            vector,
            matrix,
            vector,
            vector,
            vector,
            matrix,
            vector,
            matrix,
            vector,
            vector,
            vector,
        ),
        check_vma=False,
    )
```

time: 852 us -> 395 us (0.46)
  the two profiles are of different devices: /device:TPU:0 before, /device:TPU:16 now
where the time goes in v1:
time: 395 us; the launch traced here: 389 us
  waiting for transfers between devices  90.7 us (23%)
  local copies, waits for them, and re-layouts  80.4 us (20%)
  Pallas kernels  59.1 us (15%)
  other arithmetic  55.1 us (14%)
  starting transfers between devices  47.8 us (12%)
  blocking collectives  22 us (6%)
  matrix products  17.4 us (4%)
  between operations  16.3 us (4%)
    ppermute x50, waiting for transfers between devices, swap_with(): return lax.ppermute(value, axis, [(i, i ^ offset) for i in range(size)])  90.6 us
    ppermute x50, starting transfers between devices, swap_with(): return lax.ppermute(value, axis, [(i, i ^ offset) for i in range(size)])  47.8 us
    pallas_call x1, Pallas kernels, attend_backward(): pl.pallas_call(functools.partial(attend_backward_kernel, heads, blocks),...  22.7 us
    pallas_call x1, Pallas kernels, feed_forward_backward(): pl.pallas_call(feed_kernel, grid=(2, parts), in_specs=[full, full, pl.Blo...  22.5 us
    all_gather x1, blocking collectives, on_device(): first_all = lax.all_gather(first_piece, 'dp', axis=0, tiled=False)  22 us
    pallas_call x1, Pallas kernels, attend_forward(): pl.pallas_call(functools.partial(attend_forward_kernel, heads, blocks), g...  13.9 us
    convert_element_type x3, local copies, waits for them, and re-layouts, on_device(): expand_out.transpose(1, 2, 0, 3).reshape(shard, hidden).astype(F32)  12.1 us
    unnamed x93, local copies, waits for them, and re-layouts  8.75 us
  transfers between devices with their start and end apart: 51, of which 19 were waited for; matrix products, arithmetic and copies ran while one was open for 30% of the time, Pallas kernels for 9%

profile of v1, /device:TPU:16, one launch (start us, length us, event | category | flops | bytes accessed | tf_op | source)
XLA Modules:
  0.0 388.8 jit_solution(4658780076536619275)
XLA Ops:
  9.9 2.8 collective-permute-start.9
  12.7 2.9 reshape.1252
  21.8 22.0 %all-gather = bf16[448,576]{1,0:T(8,128)(2,1)S(1)} all-gather(bf16[112,576]{1,0:T(8,128)(2,1)S(1)} %copy.156), channel_id=2, replica_groups=mesh['dp'=4,'blk'=2,'uly'=4] {'dp'}, dimensions={0}, use_global_device_ids=true | all-gather | bytes 645120 | tf_op jit(solution)/shard_map/all_gather | solution.py:398
  62.7 6.0 %collective-permute-done.1 = bf16[256,768]{1,0:T(8,128)(2,1)} collective-permute-done((bf16[256,768]{1,0:T(8,128)(2,1)}, bf16[256,768]{1,0:T(8,128)(2,1)}, u32[]{:S(2)}, u32[]{:S(2)}) %collective-permute-start.1) | collective-permute-done | bytes 393248 | tf_op jit(solution)/shard_map/ppermute | solution.py:35
  68.8 3.5 add_convert_fusion.4.refs_0_
  75.9 2.8 fusion.4.q_ref
  90.5 13.9 %attend_forward.1 = (bf16[1024,192]{1,0:T(8,128)(2,1)}, f32[8,1024]{1,0:T(8,128)}) custom-call(bf16[1024,256]{1,0:T(8,128)(2,1)} %fusion.4.q_ref, bf16[1024,448]{1,0:T(8,128)(2,1)} %add_convert_fusion.4.refs_0_, bf16[1024,448]{1,0:T(8,128)(2,1)} %copy.161.refs_1_), custom_call_target="tpu_custom_call" | custom-call | flops 6442450944 | bytes 3407872 | tf_op jit(solution)/shard_map/attend_forward/pallas_call | solution.py:109
  109.1 7.1 %collective-permute-done.13 = bf16[2,768,384]{2,1,0:T(8,128)(2,1)} collective-permute-done((bf16[2,768,384]{2,1,0:T(8,128)(2,1)}, bf16[2,768,384]{2,1,0:T(8,128)(2,1)}, u32[]{:S(2)}, u32[]{:S(2)}) %collective-permute-start.13) | collective-permute-done | bytes 1179680 | tf_op jit(solution)/shard_map/ppermute | solution.py:35
  126.8 3.6 pad_maximum_fusion.expand_ref
  132.7 22.5 %feed_forward_backward.1 = (bf16[256,768]{1,0:T(8,128)(2,1)}, f32[256,768]{1,0:T(8,128)S(1)}, bf16[8,768,384]{2,1,0:T(8,128)(2,1)}, bf16[8,384,768]{2,1,0:T(8,12...) custom-call(f32[256,768]{1,0:T(8,128)S(1)} %get-tuple-element.75.x1_ref, ...), custom_call_target="tpu_custom_call" | custom-call | flops 7247757312 | bytes 28311552 | tf_op jit(solution)/shard_map/feed_forward_backward/pallas_call | solution.py:299
  157.6 2.8 reshape.1270
  176.8 3.5 collective-permute-done.19
  181.1 22.7 %attend_backward.1 = (bf16[1024,192]{1,0:T(8,128)(2,1)}, bf16[1024,448]{1,0:T(8,128)(2,1)}, bf16[1024,448]{1,0:T(8,128)(2,1)}) custom-call(bf16[1024,256]{1,0:T(8,128)(2,1)} %fusion.4.q_ref, bf16[1024,192]{1,0:T(8,128)(2,1)} %pad_maximum_fusion.24.do_ref, bf16[1024,192]{1,0:T(8,128)(2,1)} %get-tuple-element.26.o_ref, f32[8,1024]{1,0:T(8,128)} %get-tuple-element.29.lse_ref, ...), custom_call_target="tpu_custom_call" | custom-call | flops 16106127360 | bytes 5767168 | tf_op jit(solution)/shard_map/attend_backward/pallas_call | solution.py:186
  211.3 4.3 %collective-permute-done.40 = bf16[4,64,384]{2,1,0:T(8,128)(2,1)} collective-permute-done((bf16[4,64,384]{2,1,0:T(8,128)(2,1)S(1)}, bf16[4,64,384]{2,1,0:T(8,128)(2,1)}, u32[]{:S(2)}, u32[]{:S(2)}) %collective-permute-start.40) | collective-permute-done | bytes 196640 | tf_op jit(solution)/shard_map/ppermute | solution.py:35
  218.0 5.0 %collective-permute-done.42 = bf16[4,64,384]{2,1,0:T(8,128)(2,1)S(1)} collective-permute-done((bf16[4,64,384]{2,1,0:T(8,128)(2,1)S(1)}, bf16[4,64,384]{2,1,0:T(8,128)(2,1)S(1)}, u32[]{:S(2)}, u32[]{:S(2)}) %collective-permute-start.42) | collective-permute-done | bytes 196640 | tf_op jit(solution)/shard_map/ppermute | solution.py:35
  226.0 3.3 add_convert_fusion.1
  231.9 3.7 convolution_convert_fusion.1
  239.9 2.9 add_convert_fusion
  244.8 3.6 fusion.112
  248.4 9.1 %collective-permute-done.34 = bf16[2,768,384]{2,1,0:T(8,128)(2,1)} collective-permute-done((bf16[2,768,384]{2,1,0:T(8,128)(2,1)}, bf16[2,768,384]{2,1,0:T(8,128)(2,1)}, u32[]{:S(2)}, u32[]{:S(2)}) %collective-permute-start.34) | collective-permute-done | bytes 1179680 | tf_op jit(solution)/shard_map/ppermute | solution.py:35
  260.9 11.0 %collective-permute-done.37 = bf16[2,384,768]{2,1,0:T(8,128)(2,1)S(1)} collective-permute-done((bf16[2,384,768]{2,1,0:T(8,128)(2,1)S(1)}, bf16[2,384,768]{2,1,0:T(8,128)(2,1)S(1)}, u32[]{:S(2)}, u32[]{:S(2)}) %collective-permute-start.37) | collective-permute-done | bytes 1179680 | tf_op jit(solution)/shard_map/ppermute | solution.py:35
  278.2 3.8 collective-permute-done.35
  293.2 5.5 %collective-permute-done.43 = bf16[224,768]{1,0:T(8,128)(2,1)S(1)} collective-permute-done((bf16[224,768]{1,0:T(8,128)(2,1)S(1)}, bf16[224,768]{1,0:T(8,128)(2,1)S(1)}, u32[]{:S(2)}, u32[]{:S(2)}) %collective-permute-start.43) | collective-permute-done | bytes 344096 | tf_op jit(solution)/shard_map/ppermute | solution.py:35
  300.5 10.0 %collective-permute-done.44 = bf16[224,768]{1,0:T(8,128)(2,1)S(1)} collective-permute-done((bf16[224,768]{1,0:T(8,128)(2,1)S(1)}, bf16[224,768]{1,0:T(8,128)(2,1)S(1)}, u32[]{:S(2)}, u32[]{:S(2)}) %collective-permute-start.44) | collective-permute-done | bytes 344096 | tf_op jit(solution)/shard_map/ppermute | solution.py:35
  311.3 4.9 %collective-permute-done.45 = bf16[224,768]{1,0:T(8,128)(2,1)S(1)} collective-permute-done((bf16[224,768]{1,0:T(8,128)(2,1)S(1)}, bf16[224,768]{1,0:T(8,128)(2,1)S(1)}, u32[]{:S(2)}, u32[]{:S(2)}) %collective-permute-start.45) | collective-permute-done | bytes 344096 | tf_op jit(solution)/shard_map/ppermute | solution.py:35
  324.8 6.2 %collective-permute-done.46 = bf16[224,768]{1,0:T(8,128)(2,1)S(1)} collective-permute-done((bf16[224,768]{1,0:T(8,128)(2,1)S(1)}, bf16[224,768]{1,0:T(8,128)(2,1)S(1)}, u32[]{:S(2)}, u32[]{:S(2)}) %collective-permute-start.46) | collective-permute-done | bytes 344096 | tf_op jit(solution)/shard_map/ppermute | solution.py:35
  332.1 3.2 collective-permute-done.47
  339.0 4.6 %collective-permute-done.24 = bf16[256,768]{1,0:T(8,128)(2,1)} collective-permute-done((bf16[256,768]{1,0:T(8,128)(2,1)}, bf16[256,768]{1,0:T(8,128)(2,1)}, u32[]{:S(2)}, u32[]{:S(2)}) %collective-permute-start.24) | collective-permute-done | bytes 393248 | tf_op jit(solution)/shard_map/ppermute | solution.py:35
  354.1 3.7 reshape.1282
  366.2 4.1 %reshape.1293 = f32[8,192,4,96]{3,2,1,0:T(4,128)S(1)} reshape(f32[8,96,768]{2,1,0:T(8,128)} %get-tuple-element.77) | data formatting | bytes 4718592 | tf_op jit(solution)/shard_map/convert_element_type | solution.py:587
  370.3 3.4 copy.214
  373.7 4.6 %reshape.1290 = f32[192,3072]{1,0:T(8,128)} reshape(f32[192,4,8,96]{3,2,1,0:T(8,128)} %bitcast.229) | data formatting | bytes 4718592 | tf_op jit(solution)/shard_map/convert_element_type | solution.py:587
  (358 shorter events, 159.4 us)
Async XLA Ops:
  7.2 50.3 %all-gather.4.cloned.1.call-start = ((), (), s32[]{:S(2)}) async-start(), calls=%async_computation | async-start | bytes 1474560 | tf_op jit(solution)/shard_map/all_gather | solution.py:426
  8.3 39.7 %collective-permute-start.10 = (bf16[96,768]{1,0:T(8,128)(2,1)S(1)}, bf16[96,768]{1,0:T(8,128)(2,1)S(1)}, u32[]{:S(2)}, u32[]{:S(2)}) collective-permute-start(bf16[96,768]{1,0:T(8,128)(2,1)S(1)} %constant_dynamic-slice_fusion.2), channel_id=1, source_target_pairs={{0,8},{8,0},{16,24},{24,16},{1,9},{9,1},{17,25},{25,17},{2,10},{10... | collective-permute-start | bytes 442376 | tf_op jit(solution)/shard_map/ppermute | solution.py:35
  9.9 39.8 %collective-permute-start.8 = (bf16[96,768]{1,0:T(8,128)(2,1)S(1)}, bf16[96,768]{1,0:T(8,128)(2,1)S(1)}, u32[]{:S(2)}, u32[]{:S(2)}) collective-permute-start(bf16[96,768]{1,0:T(8,128)(2,1)S(1)} %constant_dynamic-slice_fusion.2), channel_id=1, source_target_pairs={{0,24},{8,16},{16,8},{24,0},{1,25},{9,17},{17,9},{25,1},{2,26},{10... | collective-permute-start | bytes 442376 | tf_op jit(solution)/shard_map/ppermute | solution.py:35
  9.9 40.5 %collective-permute-start.9 = (bf16[96,768]{1,0:T(8,128)(2,1)S(1)}, bf16[96,768]{1,0:T(8,128)(2,1)}, u32[]{:S(2)}, u32[]{:S(2)}) collective-permute-start(bf16[96,768]{1,0:T(8,128)(2,1)S(1)} %constant_dynamic-slice_fusion.2), channel_id=1, source_target_pairs={{0,16},{8,24},{16,0},{24,8},{1,17},{9,25},{17,1},{25,9},{2,18},{10... | collective-permute-start | bytes 442376 | tf_op jit(solution)/shard_map/ppermute | solution.py:35
  43.9 18.8 %collective-permute-start = (bf16[256,768]{1,0:T(8,128)(2,1)}, bf16[256,768]{1,0:T(8,128)(2,1)}, u32[]{:S(2)}, u32[]{:S(2)}) collective-permute-start(bf16[256,768]{1,0:T(8,128)(2,1)} %bitcast), channel_id=1, source_target_pairs={{0,1},{1,0},{2,3},{3,2},{4,5},{5,4},{6,7},{7,6},{8,9},{9,8},{10,11... | collective-permute-start | bytes 1179656 | tf_op jit(solution)/shard_map/ppermute | solution.py:35
  48.0 20.8 %collective-permute-start.1 = (bf16[256,768]{1,0:T(8,128)(2,1)}, bf16[256,768]{1,0:T(8,128)(2,1)}, u32[]{:S(2)}, u32[]{:S(2)}) collective-permute-start(bf16[256,768]{1,0:T(8,128)(2,1)} %bitcast), channel_id=1, source_target_pairs={{0,2},{1,3},{2,0},{3,1},{4,6},{5,7},{6,4},{7,5},{8,10},{9,11},{10,... | collective-permute-start | bytes 1179656 | tf_op jit(solution)/shard_map/ppermute | solution.py:35
  49.7 19.0 %collective-permute-start.2 = (bf16[256,768]{1,0:T(8,128)(2,1)}, bf16[256,768]{1,0:T(8,128)(2,1)}, u32[]{:S(2)}, u32[]{:S(2)}) collective-permute-start(bf16[256,768]{1,0:T(8,128)(2,1)} %bitcast), channel_id=1, source_target_pairs={{0,3},{1,2},{2,1},{3,0},{4,7},{5,6},{6,5},{7,4},{8,11},{9,10},{10,... | collective-permute-start | bytes 1179656 | tf_op jit(solution)/shard_map/ppermute | solution.py:35
  58.8 21.8 %collective-permute-start.15 = (bf16[384,768]{1,0:T(8,128)(2,1)S(1)}, bf16[384,768]{1,0:T(8,128)(2,1)}, u32[]{:S(2)}, u32[]{:S(2)}) collective-permute-start(bf16[384,768]{1,0:T(8,128)(2,1)S(1)} %bitcast.234), channel_id=1, source_target_pairs={{0,2},{1,3},{2,0},{3,1},{4,6},{5,7},{6,4},{7,5},{8,10},{9,11},{10,... | collective-permute-start | bytes 1769480 | tf_op jit(solution)/shard_map/ppermute | solution.py:35
  61.2 22.3 %collective-permute-start.12 = (bf16[768,384]{1,0:T(8,128)(2,1)}, bf16[768,384]{1,0:T(8,128)(2,1)S(1)}, u32[]{:S(2)}, u32[]{:S(2)}) collective-permute-start(bf16[768,384]{1,0:T(8,128)(2,1)} %reshape.1256), channel_id=1, source_target_pairs={{0,1},{1,0},{2,3},{3,2},{4,5},{5,4},{6,7},{7,6},{8,9},{9,8},{10,11... | collective-permute-start | bytes 1769480 | tf_op jit(solution)/shard_map/ppermute | solution.py:35
  74.5 13.8 %collective-permute-start.4 = (bf16[1024,448]{0,1:T(8,128)(2,1)}, bf16[1024,448]{0,1:T(8,128)(2,1)}, u32[]{:S(2)}, u32[]{:S(2)}) collective-permute-start(bf16[1024,448]{0,1:T(8,128)(2,1)} %copy.160), channel_id=1, source_target_pairs={{0,4},{4,0},{1,5},{5,1},{2,6},{6,2},{3,7},{7,3},{8,12},{12,8},{9,1... | collective-permute-start | bytes 2752520 | tf_op jit(solution)/shard_map/ppermute | solution.py:35
  82.8 34.9 %collective-permute-start.16 = (bf16[2,384,768]{2,1,0:T(8,128)(2,1)}, bf16[2,384,768]{2,1,0:T(8,128)(2,1)}, u32[]{:S(2)}, u32[]{:S(2)}) collective-permute-start(bf16[2,384,768]{2,1,0:T(8,128)(2,1)} %pad_maximum_fusion.10), channel_id=1, source_target_pairs={{0,1},{1,0},{2,3},{3,2},{4,5},{5,4},{6,7},{7,6},{8,9},{9,8},{10,11... | collective-permute-start | bytes 3538952 | tf_op jit(solution)/shard_map/ppermute | solution.py:35
  84.6 31.5 %collective-permute-start.13 = (bf16[2,768,384]{2,1,0:T(8,128)(2,1)}, bf16[2,768,384]{2,1,0:T(8,128)(2,1)}, u32[]{:S(2)}, u32[]{:S(2)}) collective-permute-start(bf16[2,768,384]{2,1,0:T(8,128)(2,1)} %pad_maximum_fusion.9), channel_id=1, source_target_pairs={{0,2},{1,3},{2,0},{3,1},{4,6},{5,7},{6,4},{7,5},{8,10},{9,11},{10,... | collective-permute-start | bytes 3538952 | tf_op jit(solution)/shard_map/ppermute | solution.py:35
  105.5 15.8 %collective-permute-start.5 = (bf16[256,192]{1,0:T(8,128)(2,1)S(1)}, bf16[256,192]{1,0:T(8,128)(2,1)S(1)}, u32[]{:S(2)}, u32[]{:S(2)}) collective-permute-start(bf16[256,192]{1,0:T(8,128)(2,1)S(1)} %get-tuple-element.139), channel_id=1, source_target_pairs={{0,3},{1,2},{2,1},{3,0},{4,7},{5,6},{6,5},{7,4},{8,11},{9,10},{10,... | collective-permute-start | bytes 294920 | tf_op jit(solution)/shard_map/ppermute | solution.py:35
  106.9 14.4 %collective-permute-start.6 = (bf16[256,192]{1,0:T(8,128)(2,1)S(1)}, bf16[256,192]{1,0:T(8,128)(2,1)S(1)}, u32[]{:S(2)}, u32[]{:S(2)}) collective-permute-start(bf16[256,192]{1,0:T(8,128)(2,1)S(1)} %get-tuple-element.138), channel_id=1, source_target_pairs={{0,2},{1,3},{2,0},{3,1},{4,6},{5,7},{6,4},{7,5},{8,10},{9,11},{10,... | collective-permute-start | bytes 294920 | tf_op jit(solution)/shard_map/ppermute | solution.py:35
  166.1 60.0 %collective-permute-start.33 = (bf16[4,768,384]{2,1,0:T(8,128)(2,1)}, bf16[4,768,384]{2,1,0:T(8,128)(2,1)}, u32[]{:S(2)}, u32[]{:S(2)}) collective-permute-start(bf16[4,768,384]{2,1,0:T(8,128)(2,1)} %slice.308), channel_id=1, source_target_pairs={{0,4},{4,0},{1,5},{5,1},{2,6},{6,2},{3,7},{7,3},{8,12},{12,8},{9,1... | collective-permute-start | bytes 7077896 | tf_op jit(solution)/shard_map/ppermute | solution.py:35
  167.7 72.2 %collective-permute-start.36 = (bf16[4,384,768]{2,1,0:T(8,128)(2,1)}, bf16[4,384,768]{2,1,0:T(8,128)(2,1)}, u32[]{:S(2)}, u32[]{:S(2)}) collective-permute-start(bf16[4,384,768]{2,1,0:T(8,128)(2,1)} %slice.314), channel_id=1, source_target_pairs={{0,4},{4,0},{1,5},{5,1},{2,6},{6,2},{3,7},{7,3},{8,12},{12,8},{9,1... | collective-permute-start | bytes 7077896 | tf_op jit(solution)/shard_map/ppermute | solution.py:35
  176.8 29.3 %collective-permute-start.39 = (bf16[4,4,64,384]{3,2,1,0:T(8,128)(2,1)S(1)}, bf16[4,4,64,384]{3,2,1,0:T(8,128)(2,1)}, u32[]{:S(2)}, u32[]{:S(2)}) collective-permute-start(bf16[4,4,64,384]{3,2,1,0:T(8,128)(2,1)S(1)} %pad_maximum_fusion.13), channel_id=1, source_target_pairs={{0,4},{4,0},{1,5},{5,1},{2,6},{6,2},{3,7},{7,3},{8,12},{12,8},{9,1... | collective-permute-start | bytes 2359304 | tf_op jit(solution)/shard_map/ppermute | solution.py:35
  206.1 18.1 %collective-permute-start.21 = (bf16[1024,448]{0,1:T(8,128)(2,1)}, bf16[1024,448]{0,1:T(8,128)(2,1)}, u32[]{:S(2)}, u32[]{:S(2)}) collective-permute-start(bf16[1024,448]{0,1:T(8,128)(2,1)} %copy.165), channel_id=1, source_target_pairs={{0,4},{4,0},{1,5},{5,1},{2,6},{6,2},{3,7},{7,3},{8,12},{12,8},{9,1... | collective-permute-start | bytes 2752520 | tf_op jit(solution)/shard_map/ppermute | solution.py:35
  230.5 27.0 %collective-permute-start.34 = (bf16[2,768,384]{2,1,0:T(8,128)(2,1)}, bf16[2,768,384]{2,1,0:T(8,128)(2,1)}, u32[]{:S(2)}, u32[]{:S(2)}) collective-permute-start(bf16[2,768,384]{2,1,0:T(8,128)(2,1)} %slice_bitcast_fusion), channel_id=1, source_target_pairs={{0,1},{1,0},{2,3},{3,2},{4,5},{5,4},{6,7},{7,6},{8,9},{9,8},{10,11... | collective-permute-start | bytes 3538952 | tf_op jit(solution)/shard_map/ppermute | solution.py:35
  242.9 29.0 %collective-permute-start.37 = (bf16[2,384,768]{2,1,0:T(8,128)(2,1)S(1)}, bf16[2,384,768]{2,1,0:T(8,128)(2,1)S(1)}, u32[]{:S(2)}, u32[]{:S(2)}) collective-permute-start(bf16[2,384,768]{2,1,0:T(8,128)(2,1)S(1)} %slice.386), channel_id=1, source_target_pairs={{0,2},{1,3},{2,0},{3,1},{4,6},{5,7},{6,4},{7,5},{8,10},{9,11},{10,... | collective-permute-start | bytes 3538952 | tf_op jit(solution)/shard_map/ppermute | solution.py:35
  244.2 29.5 %collective-permute-start.25 = (bf16[400,576]{1,0:T(8,128)(2,1)S(1)}, bf16[400,576]{1,0:T(8,128)(2,1)S(1)}, u32[]{:S(2)}, u32[]{:S(2)}) collective-permute-start(bf16[400,576]{1,0:T(8,128)(2,1)S(1)} %fusion.22), channel_id=1, source_target_pairs={{0,4},{4,0},{1,5},{5,1},{2,6},{6,2},{3,7},{7,3},{8,12},{12,8},{9,1... | collective-permute-start | bytes 1382408 | tf_op jit(solution)/shard_map/ppermute | solution.py:35
  259.2 22.9 %collective-permute-start.35 = (bf16[768,384]{1,0:T(8,128)(2,1)S(1)}, bf16[768,384]{1,0:T(8,128)(2,1)S(1)}, u32[]{:S(2)}, u32[]{:S(2)}) collective-permute-start(bf16[768,384]{1,0:T(8,128)(2,1)S(1)} %slice_bitcast_fusion.4), channel_id=1, source_target_pairs={{0,2},{1,3},{2,0},{3,1},{4,6},{5,7},{6,4},{7,5},{8,10},{9,11},{10,... | collective-permute-start | bytes 1769480 | tf_op jit(solution)/shard_map/ppermute | solution.py:35
  276.8 13.8 %collective-permute-start.28 = (bf16[112,576]{1,0:T(8,128)(2,1)}, bf16[112,576]{1,0:T(8,128)(2,1)}, u32[]{:S(2)}, u32[]{:S(2)}) collective-permute-start(bf16[112,576]{1,0:T(8,128)(2,1)} %get-tuple-element.136), channel_id=1, source_target_pairs={{0,24},{8,16},{16,8},{24,0},{1,25},{9,17},{17,9},{25,1},{2,26},{10... | collective-permute-start | bytes 387080 | tf_op jit(solution)/shard_map/ppermute | solution.py:35
  285.2 13.6 %collective-permute-start.43 = (bf16[224,768]{1,0:T(8,128)(2,1)S(1)}, bf16[224,768]{1,0:T(8,128)(2,1)S(1)}, u32[]{:S(2)}, u32[]{:S(2)}) collective-permute-start(bf16[224,768]{1,0:T(8,128)(2,1)S(1)} %get-tuple-element.89), channel_id=1, source_target_pairs={{0,8},{8,0},{16,24},{24,16},{1,9},{9,1},{17,25},{25,17},{2,10},{10... | collective-permute-start | bytes 1032200 | tf_op jit(solution)/shard_map/ppermute | solution.py:35
  287.3 23.3 %collective-permute-start.44 = (bf16[224,768]{1,0:T(8,128)(2,1)S(1)}, bf16[224,768]{1,0:T(8,128)(2,1)S(1)}, u32[]{:S(2)}, u32[]{:S(2)}) collective-permute-start(bf16[224,768]{1,0:T(8,128)(2,1)S(1)} %get-tuple-element.91), channel_id=1, source_target_pairs={{0,16},{8,24},{16,0},{24,8},{1,17},{9,25},{17,1},{25,9},{2,18},{10... | collective-permute-start | bytes 1032200 | tf_op jit(solution)/shard_map/ppermute | solution.py:35
  287.3 28.9 %collective-permute-start.45 = (bf16[224,768]{1,0:T(8,128)(2,1)S(1)}, bf16[224,768]{1,0:T(8,128)(2,1)S(1)}, u32[]{:S(2)}, u32[]{:S(2)}) collective-permute-start(bf16[224,768]{1,0:T(8,128)(2,1)S(1)} %get-tuple-element.90), channel_id=1, source_target_pairs={{0,24},{8,16},{16,8},{24,0},{1,25},{9,17},{17,9},{25,1},{2,26},{10... | collective-permute-start | bytes 1032200 | tf_op jit(solution)/shard_map/ppermute | solution.py:35
  289.8 49.2 %collective-permute-start.22 = (bf16[256,768]{1,0:T(8,128)(2,1)}, bf16[256,768]{1,0:T(8,128)(2,1)}, u32[]{:S(2)}, u32[]{:S(2)}) collective-permute-start(bf16[256,768]{1,0:T(8,128)(2,1)} %get-tuple-element.82), channel_id=1, source_target_pairs={{0,1},{1,0},{2,3},{3,2},{4,5},{5,4},{6,7},{7,6},{8,9},{9,8},{10,11... | collective-permute-start | bytes 1179656 | tf_op jit(solution)/shard_map/ppermute | solution.py:35
  290.6 48.5 %collective-permute-start.23 = (bf16[256,768]{1,0:T(8,128)(2,1)}, bf16[256,768]{1,0:T(8,128)(2,1)}, u32[]{:S(2)}, u32[]{:S(2)}) collective-permute-start(bf16[256,768]{1,0:T(8,128)(2,1)} %get-tuple-element.84), channel_id=1, source_target_pairs={{0,2},{1,3},{2,0},{3,1},{4,6},{5,7},{6,4},{7,5},{8,10},{9,11},{10,... | collective-permute-start | bytes 1179656 | tf_op jit(solution)/shard_map/ppermute | solution.py:35
  298.8 19.4 %collective-permute-start.29 = (bf16[112,576]{1,0:T(8,128)(2,1)S(1)}, bf16[112,576]{1,0:T(8,128)(2,1)S(1)}, u32[]{:S(2)}, u32[]{:S(2)}) collective-permute-start(bf16[112,576]{1,0:T(8,128)(2,1)S(1)} %fusion.31), channel_id=1, source_target_pairs={{0,3},{1,2},{2,1},{3,0},{4,7},{5,6},{6,5},{7,4},{8,11},{9,10},{10,... | collective-permute-start | bytes 387080 | tf_op jit(solution)/shard_map/ppermute | solution.py:35
  320.0 15.3 %collective-permute-start.47 = (bf16[224,768]{1,0:T(8,128)(2,1)S(1)}, bf16[224,768]{1,0:T(8,128)(2,1)S(1)}, u32[]{:S(2)}, u32[]{:S(2)}) collective-permute-start(bf16[224,768]{1,0:T(8,128)(2,1)S(1)} %get-tuple-element.70), channel_id=1, source_target_pairs={{0,2},{1,3},{2,0},{3,1},{4,6},{5,7},{6,4},{7,5},{8,10},{9,11},{10,... | collective-permute-start | bytes 1032200 | tf_op jit(solution)/shard_map/ppermute | solution.py:35
  322.9 14.7 %collective-permute-start.48 = (bf16[224,768]{1,0:T(8,128)(2,1)S(1)}, bf16[224,768]{1,0:T(8,128)(2,1)S(1)}, u32[]{:S(2)}, u32[]{:S(2)}) collective-permute-start(bf16[224,768]{1,0:T(8,128)(2,1)S(1)} %get-tuple-element.70), channel_id=1, source_target_pairs={{0,1},{1,0},{2,3},{3,2},{4,5},{5,4},{6,7},{7,6},{8,9},{9,8},{10,11... | collective-permute-start | bytes 1032200 | tf_op jit(solution)/shard_map/ppermute | solution.py:35
  339.0 23.2 %collective-permute-start.49 = (bf16[4,224,768]{2,1,0:T(8,128)(2,1)}, bf16[4,224,768]{2,1,0:T(8,128)(2,1)}, u32[]{:S(2)}, u32[]{:S(2)}) collective-permute-start(bf16[4,224,768]{2,1,0:T(8,128)(2,1)} %pad_maximum_fusion.6), channel_id=1, source_target_pairs={{0,4},{4,0},{1,5},{5,1},{2,6},{6,2},{3,7},{7,3},{8,12},{12,8},{9,1... | collective-permute-start | bytes 4128776 | tf_op jit(solution)/shard_map/ppermute | solution.py:35
  (62 other events, 369.5 us)
Sparse Core Ops, SparseCore 0:
  18.1 35.5 all-gather.3

commit v2 on v1

--- a/solution.py
+++ b/solution.py
@@ -343,7 +343,7 @@
     )(x1, x1b, expand, shrink, ebias, sbias, gain, shift, cot)
 
 
-def on_device(
+def general_device(
     tokens,
     lengths,
     cotangent,
@@ -649,6 +649,976 @@
     )
 
 
+def call(kernel, name, scalars, args, in_specs, out_shape, out_specs, scratch, grid, flops, vmem):
+    size = sum(a.size * a.dtype.itemsize for a in args)
+    return pl.pallas_call(
+        kernel,
+        grid_spec=pltpu.PrefetchScalarGridSpec(
+            num_scalar_prefetch=1,
+            grid=grid,
+            in_specs=in_specs,
+            out_specs=out_specs,
+            scratch_shapes=scratch,
+        ),
+        out_shape=out_shape,
+        compiler_params=pltpu.CompilerParams(vmem_limit_bytes=vmem * 2**20),
+        cost_estimate=pl.CostEstimate(flops=flops, bytes_accessed=size, transcendentals=0),
+        name=name,
+    )(scalars, *args)
+
+
+def whole(shape):
+    return pl.BlockSpec(shape, lambda *_: (0,) * len(shape))
+
+
+def one_hot(rows, cols, row_offset=0, col_offset=0):
+    row = lax.broadcasted_iota(jnp.int32, (rows, cols), 0) + row_offset
+    col = lax.broadcasted_iota(jnp.int32, (rows, cols), 1) + col_offset
+    return jnp.where(row == col, 1.0, 0.0).astype(BF16)
+
+
+def fetch_kernel(
+    sizes, idx, attend_ref, small_ref, expand_ref, shrink_ref, mixer_ref, first_ref, feed_ref
+):
+    uly, dp, group, unit = sizes
+    share = attend_ref.shape[1]
+    shard, width = mixer_ref.shape
+    u = idx[1]
+    part = idx[0] * uly + u
+    take = one_hot(width, group, 0, u * group)
+    for c in range(3):
+        cols = dot_nn(attend_ref[0, :, c * width : (c + 1) * width], take)
+        first_ref[:share, c * group : (c + 1) * group] = cols.astype(BF16)
+    first_ref[share:, :] = jnp.zeros_like(first_ref[share:, :])
+    first_ref[share:, :shard] = small_ref[...]
+    take = one_hot(width, unit, 0, part * unit)
+    half = shard // 2
+    for k in range(dp):
+        cols = dot_nn(expand_ref[:, k * width : (k + 1) * width], take).astype(BF16)
+        feed_ref[:half, k * unit : (k + 1) * unit] = cols[:half]
+        feed_ref[:half, (dp + k) * unit : (dp + k + 1) * unit] = cols[half:]
+    feed_ref[half : half + unit, :] = shrink_ref[0]
+    rows = feed_ref.shape[0] - half - unit
+    feed_ref[half + unit :, :] = dot_nn(
+        one_hot(rows, shard, part * rows, 0), mixer_ref[...]
+    ).astype(BF16)
+
+
+def project_kernel(sizes, idx, *refs):
+    uly, blk, dp, group, unit = sizes
+    x_refs, refs = refs[:uly], refs[uly:]
+    mine_refs, refs = refs[:dp], refs[dp:]
+    other_refs, refs = refs[:dp], refs[dp:]
+    w_ref, q_ref, kv_ref, vec_ref, eb_ref = refs
+    b, u, z, length = idx[0], idx[1], idx[2], idx[3]
+    rows, width = x_refs[0].shape
+    wide = q_ref.shape[1]
+    pad = wide - group
+    share = mine_refs[0].shape[0] - 16
+    shard = 2 * share
+    parts = uly * blk
+    w_ref[:, group:wide] = jnp.zeros((width, pad), BF16)
+    w_ref[:, wide + group : 2 * wide] = jnp.zeros((width, pad), BF16)
+    own_vec = jnp.zeros((16, shard), F32)
+    all_vec = jnp.zeros((16, width), F32)
+    for j in range(dp):
+        for ref, core in ((mine_refs[j], b), (other_refs[j], 1 - b)):
+            start = pl.multiple_of((z ^ j) * shard + core * share, share)
+            for c in range(3):
+                w_ref[pl.ds(start, share), c * wide : c * wide + group] = ref[
+                    :share, c * group : (c + 1) * group
+                ]
+        vec = mine_refs[j][share:, :shard]
+        own_vec += jnp.where((z ^ j) == u, 1.0, 0.0) * vec.astype(F32)
+        all_vec += dot_nn(vec, one_hot(shard, width, (z ^ j) * shard, 0))
+    vec_ref[...] = all_vec
+
+    low = all_vec.astype(BF16)
+    part = b * uly + u
+    eb = jnp.zeros((parts, dp * unit), F32)
+    for parity in range(2):
+        col = lax.broadcasted_iota(jnp.int32, (width, dp * unit), 1)
+        row = lax.broadcasted_iota(jnp.int32, (width, dp * unit), 0)
+        source = col + (col // unit) * (shard - unit) + parity * unit
+        lanes = dot_nn(low, jnp.where(row == source, 1.0, 0.0).astype(BF16)).astype(BF16)
+        owner = lax.broadcasted_iota(jnp.int32, (parts, 16), 0) ^ part
+        line = lax.broadcasted_iota(jnp.int32, (parts, 16), 1)
+        wanted = ((owner & 1) == parity) & (line == 8 + (owner >> 1))
+        eb += dot_nn(jnp.where(wanted, 1.0, 0.0).astype(BF16), lanes)
+    eb_ref[...] = eb
+
+    lane = lax.broadcasted_iota(jnp.int32, (1, wide), 1)
+    mark = jnp.where(lane == group, 1.0, 0.0)
+    zeros = jnp.zeros((1, pad), F32)
+    q_bias = jnp.concatenate([own_vec[0:1], zeros], 1)
+    v_bias = own_vec[1:2]
+    for j in range(uly):
+        x = x_refs[j][...]
+        here = slice(j * rows, (j + 1) * rows)
+        q = dot_nn(x, w_ref[:, :wide]) + q_bias
+        q_ref[here, :] = (q * (0.125 * LOG2E) + mark).astype(BF16)
+        first = (b * uly + (u ^ j)) * rows
+        position = lax.broadcasted_iota(jnp.int32, (rows, 1), 0) + first
+        masked = jnp.where(position < length, 0.0, MASKED)
+        k = dot_nn(x, w_ref[:, wide : 2 * wide]) + masked * mark
+        kv_ref[here, :wide] = k.astype(BF16)
+        kv_ref[here, wide:] = (dot_nn(x, w_ref[:, 2 * wide :]) + v_bias).astype(BF16)
+
+
+def attend_kernel(heads, blocks, q_ref, *refs):
+    kv_refs = refs[:blocks]
+    o_refs = refs[blocks:-2]
+    lse_ref, vt_ref = refs[-2:]
+    group = heads * HD
+    wide = q_ref.shape[1]
+    rows = kv_refs[0].shape[0]
+
+    @pl.when(pl.program_id(0) == 0)
+    def _():
+        for i in range(blocks):
+            vt_ref[:, i * rows : (i + 1) * rows] = kv_refs[i][:, wide : wide + group].T
+
+    q = q_ref[...]
+    outs = []
+    for head in range(heads):
+        q_head = jnp.where(head_lanes(wide, head, group), q, jnp.zeros_like(q))
+        scores = [dot_nt(kv_refs[i][:, :wide], q_head) for i in range(blocks)]
+        top = jnp.max(scores[0], axis=0, keepdims=True)
+        for i in range(1, blocks):
+            top = jnp.maximum(top, jnp.max(scores[i], axis=0, keepdims=True))
+        norm = jnp.zeros_like(top)
+        acc = None
+        for i in range(blocks):
+            probs = jnp.exp2(scores[i] - top)
+            norm = norm + jnp.sum(probs, axis=0, keepdims=True)
+            part = dot_nn(
+                vt_ref[head * HD : (head + 1) * HD, i * rows : (i + 1) * rows], probs.astype(BF16)
+            )
+            acc = part if acc is None else acc + part
+        outs.append(acc / norm)
+        lse_ref[head : head + 1, :] = top + jnp.log2(norm)
+    out = jnp.concatenate(outs, axis=0).T.astype(BF16)
+    for j, o_ref in enumerate(o_refs):
+
+        @pl.when(pl.program_id(0) == j)
+        def _(o_ref=o_ref):
+            o_ref[...] = out
+
+
+def attend(q, kvs, heads, pieces):
+    rows, wide = q.shape
+    tile = rows // pieces
+    group = heads * HD
+    blocks = len(kvs)
+    keys = blocks * rows
+    out = pl.pallas_call(
+        functools.partial(attend_kernel, heads, blocks),
+        grid=(pieces,),
+        in_specs=[pl.BlockSpec((tile, wide), lambda t: (t, 0))] + [whole(kvs[0].shape)] * blocks,
+        out_specs=[whole((tile, group))] * pieces + [pl.BlockSpec((8, tile), lambda t: (0, t))],
+        out_shape=[jax.ShapeDtypeStruct((tile, group), BF16)] * pieces
+        + [jax.ShapeDtypeStruct((8, rows), F32)],
+        scratch_shapes=[pltpu.VMEM((group, keys), BF16)],
+        compiler_params=pltpu.CompilerParams(vmem_limit_bytes=48 * 2**20),
+        cost_estimate=pl.CostEstimate(
+            flops=4 * heads * rows * keys * wide,
+            transcendentals=heads * rows * keys,
+            bytes_accessed=2 * rows * wide * 3 + 2 * keys * (wide + group),
+        ),
+        name="attend",
+    )(q, *kvs)
+    return out[:-1], out[-1]
+
+
+def first_norm_kernel(uly, idx, x_ref, *refs):
+    o_refs = refs[:uly]
+    m_ref, vec_ref, x1_ref, x1b_ref, normed_ref, inverse_ref = refs[uly:]
+    group = o_refs[0].shape[1]
+    acc = vec_ref[2:3, :]
+    for j in range(uly):
+        start = pl.multiple_of((idx[1] ^ j) * group, group)
+        acc = acc + dot_nn(o_refs[j][...], m_ref[pl.ds(start, group), :])
+    hidden = x_ref[...].astype(F32) + acc
+    center = hidden - jnp.mean(hidden, -1, keepdims=True)
+    inverse = lax.rsqrt(jnp.mean(center * center, -1, keepdims=True) + EPSILON)
+    normed = center * inverse
+    out = normed * vec_ref[3:4, :] + vec_ref[4:5, :]
+    x1_ref[...] = out
+    x1b_ref[...] = out.astype(BF16)
+    normed_ref[...] = normed
+    inverse_ref[...] = inverse
+
+
+def load_parts(expand_refs, shrink_refs, e_ref, s_ref, e_sem, s_sem, act):
+    unit = s_ref.shape[2]
+    for p in range(len(expand_refs)):
+        act(pltpu.make_async_copy(expand_refs[p], e_ref.at[p], e_sem.at[p]), p)
+        act(
+            pltpu.make_async_copy(shrink_refs[p].at[:, pl.ds(0, unit), :], s_ref.at[p], s_sem.at[p]),
+            p,
+        )
+
+
+def feed_forward_kernel(parts, idx, x1_ref, x1b_ref, eb_ref, vec_ref, cot_ref, *refs):
+    expand_refs, refs = refs[:parts], refs[parts:]
+    shrink_refs, refs = refs[:parts], refs[parts:]
+    mixed_ref, dh_ref, dhb_ref, slope_ref, keep_ref, send_ref, grads_ref, *refs = refs
+    act_ref, acc_ref, low_ref, e_ref, s_ref, e_sem, s_sem = refs
+    phase = pl.program_id(0)
+    step = pl.program_id(1)
+    dp, unit, width = s_ref.shape[1:]
+    z = idx[2]
+
+    @pl.when((phase == 0) & (step == 0))
+    def _():
+        load_parts(
+            expand_refs, shrink_refs, e_ref, s_ref, e_sem, s_sem, lambda copy, p: copy.start()
+        )
+
+    @pl.when(phase == 0)
+    def _():
+        def wait(copy, p):
+            @pl.when(step == p)
+            def _():
+                copy.wait()
+
+        load_parts(expand_refs, shrink_refs, e_ref, s_ref, e_sem, s_sem, wait)
+        pre = dot_nn(x1b_ref[...], e_ref[step]) + eb_ref[pl.ds(step, 1), :]
+        cdf = 0.5 * (1.0 + lax.erf(pre * 0.7071067811865476))
+        pdf = jnp.exp(-0.5 * pre * pre) * 0.3989422804014327
+        act = (pre * cdf).astype(BF16)
+        act_ref[step] = act
+        slope_ref[0] = (cdf + pre * pdf).astype(BF16)
+        part = dot_nn(act, s_ref[step].reshape(dp * unit, width))
+
+        @pl.when(step == 0)
+        def _():
+            acc_ref[...] = part
+
+        @pl.when(step > 0)
+        def _():
+            acc_ref[...] += part
+
+        @pl.when(step == parts - 1)
+        def _():
+            hidden = x1_ref[...] + (acc_ref[...] + vec_ref[5:6, :])
+            gain = vec_ref[6:7, :]
+            center = hidden - jnp.mean(hidden, -1, keepdims=True)
+            inverse = lax.rsqrt(jnp.mean(center * center, -1, keepdims=True) + EPSILON)
+            normed = center * inverse
+            mixed_ref[...] = (normed * gain + vec_ref[7:8, :]).astype(BF16)
+            grad = cot_ref[...].astype(F32)
+            scaled = grad * gain
+            dhidden = inverse * (
+                scaled
+                - jnp.mean(scaled, -1, keepdims=True)
+                - normed * jnp.mean(scaled * normed, -1, keepdims=True)
+            )
+            dh_ref[...] = dhidden
+            low_ref[...] = dhidden.astype(BF16)
+            dhb_ref[...] = dhidden.astype(BF16)
+            grads_ref[...] = jnp.zeros_like(grads_ref)
+            grads_ref[0:1, :] = jnp.sum(dhidden, 0, keepdims=True)
+            grads_ref[1:2, :] = jnp.sum(grad * normed, 0, keepdims=True)
+            grads_ref[2:3, :] = jnp.sum(grad, 0, keepdims=True)
+
+    @pl.when(phase == 1)
+    def _():
+        dshrink = dot_tn(act_ref[step], low_ref[...]).astype(BF16)
+
+        def store(ref):
+            for k in range(dp):
+                start = pl.multiple_of((z ^ k) * unit, unit)
+                ref[0, pl.ds(start, unit), :] = dshrink[k * unit : (k + 1) * unit]
+
+        @pl.when(step < parts // 2)
+        def _():
+            store(keep_ref)
+
+        @pl.when(step >= parts // 2)
+        def _():
+            store(send_ref)
+
+
+def feed_forward(scalars, x1, x1b, eb, vec, cot, expand, shrink):
+    rows, width = x1.shape
+    parts = len(expand)
+    block = expand[0].shape[1]
+    dp = shrink[0].shape[0]
+    unit = block // dp
+    half = parts // 2
+    hbm = pl.BlockSpec(memory_space=pl.ANY)
+    grad = (1, block, width)
+    return call(
+        functools.partial(feed_forward_kernel, parts),
+        "feed_forward",
+        scalars,
+        [x1, x1b, eb, vec, cot, *expand, *shrink],
+        [whole(x1.shape), whole(x1.shape), whole(eb.shape), whole(vec.shape), whole(cot.shape)]
+        + [hbm] * (2 * parts),
+        [
+            jax.ShapeDtypeStruct((rows, width), BF16),
+            jax.ShapeDtypeStruct((rows, width), F32),
+            jax.ShapeDtypeStruct((rows, width), BF16),
+            jax.ShapeDtypeStruct((parts, rows, block), BF16),
+            jax.ShapeDtypeStruct((half, block, width), BF16),
+            jax.ShapeDtypeStruct((half, block, width), BF16),
+            jax.ShapeDtypeStruct((8, width), F32),
+        ],
+        [
+            whole((rows, width)),
+            whole((rows, width)),
+            whole((rows, width)),
+            pl.BlockSpec((1, rows, block), lambda p, k, _: (k * (1 - p) + (parts - 1) * p, 0, 0)),
+            pl.BlockSpec(grad, lambda p, k, _: (jnp.minimum(k, half - 1) * p, 0, 0)),
+            pl.BlockSpec(grad, lambda p, k, _: (jnp.maximum(k - half, 0) * p, 0, 0)),
+            whole((8, width)),
+        ],
+        [
+            pltpu.VMEM((parts, rows, block), BF16),
+            pltpu.VMEM((rows, width), F32),
+            pltpu.VMEM((rows, width), BF16),
+            pltpu.VMEM((parts, width, block), BF16),
+            pltpu.VMEM((parts, dp, unit, width), BF16),
+            pltpu.SemaphoreType.DMA((parts,)),
+            pltpu.SemaphoreType.DMA((parts,)),
+        ],
+        (2, parts),
+        6 * rows * width * parts * block,
+        48,
+    )
+
+
+def feed_backward_kernel(parts, idx, x1b_ref, dh_ref, dhb_ref, slope_ref, *refs):
+    expand_refs, refs = refs[:parts], refs[parts:]
+    shrink_refs, refs = refs[:parts], refs[parts:]
+    dx_ref, keep_ref, send_ref, deb_ref, *refs = refs
+    x1t_ref, acc_ref, e_ref, s_ref, e_sem, s_sem = refs
+    step = pl.program_id(0)
+    dp, unit, width = s_ref.shape[1:]
+    shard = width // dp
+    z = idx[2]
+
+    @pl.when(step == 0)
+    def _():
+        load_parts(
+            expand_refs, shrink_refs, e_ref, s_ref, e_sem, s_sem, lambda copy, p: copy.start()
+        )
+        for k in range(dp):
+            start = pl.multiple_of((z ^ k) * shard, shard)
+            x1t_ref[pl.ds(start, shard), :] = x1b_ref[...].T[k * shard : (k + 1) * shard]
+
+    def wait(copy, p):
+        @pl.when(step == p)
+        def _():
+            copy.wait()
+
+    load_parts(expand_refs, shrink_refs, e_ref, s_ref, e_sem, s_sem, wait)
+    dpre = dot_nt(dhb_ref[...], s_ref[step].reshape(dp * unit, width))
+    dpre = (dpre * slope_ref[0].astype(F32)).astype(BF16)
+    deb_ref[0] = jnp.sum(dpre.astype(F32), 0, keepdims=True)
+    dexpand = dot_nn(x1t_ref[...], dpre).astype(BF16)
+
+    @pl.when(step < parts // 2)
+    def _():
+        keep_ref[0] = dexpand
+
+    @pl.when(step >= parts // 2)
+    def _():
+        send_ref[0] = dexpand
+
+    part = dot_nt(dpre, e_ref[step])
+
+    @pl.when(step == 0)
+    def _():
+        acc_ref[...] = dh_ref[...] + part
+
+    @pl.when(step > 0)
+    def _():
+        acc_ref[...] += part
+
+    @pl.when(step == parts - 1)
+    def _():
+        dx_ref[...] = acc_ref[...]
+
+
+def feed_backward(scalars, x1b, dh, dhb, slope, expand, shrink):
+    rows, width = dh.shape
+    parts = len(expand)
+    block = expand[0].shape[1]
+    dp = shrink[0].shape[0]
+    unit = block // dp
+    half = parts // 2
+    hbm = pl.BlockSpec(memory_space=pl.ANY)
+    grad = (1, width, block)
+    return call(
+        functools.partial(feed_backward_kernel, parts),
+        "feed_backward",
+        scalars,
+        [x1b, dh, dhb, slope, *expand, *shrink],
+        [whole(x1b.shape), whole(dh.shape), whole(dhb.shape)]
+        + [pl.BlockSpec((1, rows, block), lambda k, _: (k, 0, 0))]
+        + [hbm] * (2 * parts),
+        [
+            jax.ShapeDtypeStruct((rows, width), F32),
+            jax.ShapeDtypeStruct((half, width, block), BF16),
+            jax.ShapeDtypeStruct((half, width, block), BF16),
+            jax.ShapeDtypeStruct((parts, 1, block), F32),
+        ],
+        [
+            whole((rows, width)),
+            pl.BlockSpec(grad, lambda k, _: (jnp.minimum(k, half - 1), 0, 0)),
+            pl.BlockSpec(grad, lambda k, _: (jnp.maximum(k - half, 0), 0, 0)),
+            pl.BlockSpec((1, 1, block), lambda k, _: (k, 0, 0)),
+        ],
+        [
+            pltpu.VMEM((width, rows), BF16),
+            pltpu.VMEM((rows, width), F32),
+            pltpu.VMEM((parts, width, block), BF16),
+            pltpu.VMEM((parts, dp, unit, width), BF16),
+            pltpu.SemaphoreType.DMA((parts,)),
+            pltpu.SemaphoreType.DMA((parts,)),
+        ],
+        (parts,),
+        6 * rows * width * parts * block,
+        48,
+    )
+
+
+def norm_backward_kernel(sizes, idx, dx_ref, normed_ref, inverse_ref, m_ref, vec_ref, *refs):
+    uly, dp, unit = sizes
+    grads_ref, deb_ref, *refs = refs
+    o_refs, refs = refs[:uly], refs[uly:]
+    dh_ref, *refs = refs
+    do_refs, refs = refs[:uly], refs[uly:]
+    keep_ref, send_ref, turn_ref = refs
+    b, u, z = idx[0], idx[1], idx[2]
+    group = o_refs[0].shape[1]
+    share = group // 2
+    width = dx_ref.shape[1]
+    parts = deb_ref.shape[0]
+    grad = dx_ref[...]
+    normed = normed_ref[...]
+    scaled = grad * vec_ref[3:4, :]
+    dhidden = inverse_ref[...] * (
+        scaled
+        - jnp.mean(scaled, -1, keepdims=True)
+        - normed * jnp.mean(scaled * normed, -1, keepdims=True)
+    )
+    dh_ref[...] = dhidden
+    low = dhidden.astype(BF16)
+    for j in range(uly):
+        start = pl.multiple_of((u ^ j) * group, group)
+        do_refs[j][...] = dot_nt(low, m_ref[pl.ds(start, group), :]).astype(BF16)
+    line = lax.broadcasted_iota(jnp.int32, (8, width), 0)
+    lines = jnp.zeros((8, width), F32)
+    values = [
+        jnp.sum(dhidden, 0, keepdims=True),
+        jnp.sum(grad * normed, 0, keepdims=True),
+        jnp.sum(grad, 0, keepdims=True),
+        grads_ref[0:1, :],
+        grads_ref[1:2, :],
+        grads_ref[2:3, :],
+    ]
+    for k, value in enumerate(values):
+        lines = jnp.where(line == k, value, lines)
+    lines = lines.astype(BF16)
+    part = b * uly + u
+    owner = lax.broadcasted_iota(jnp.int32, (parts, parts), 1) ^ part
+    order = lax.broadcasted_iota(jnp.int32, (parts, parts), 0)
+    order = jnp.where(order == owner, 1.0, 0.0).astype(BF16)
+    ebs = dot_nn(order, deb_ref[...].astype(BF16)).astype(BF16)
+    for j in range(uly):
+        turn_ref[...] = dot_tn(o_refs[j][...], low).astype(BF16)
+        place = u ^ j ^ z
+        keep_ref[place, :share] = turn_ref[pl.ds(pl.multiple_of(b * share, share), share), :]
+        send_ref[place, :share] = turn_ref[pl.ds(pl.multiple_of((1 - b) * share, share), share), :]
+    for k in range(dp):
+        shard = (z ^ k) * group
+        own = dot_nn(lines, one_hot(width, group, 0, shard)).astype(BF16)
+        ebk = dot_nn(ebs, one_hot(dp * unit, unit, 0, (z ^ k) * unit)).astype(BF16)
+        for ref in (keep_ref, send_ref):
+            ref[k, share:, :] = jnp.zeros_like(ref[k, share:, :])
+            ref[k, share : share + 8, :group] = own
+            ref[k, share + 8 : share + 16, :unit] = ebk
+
+
+def attend_grad_kernel(heads, blocks, pieces, q_ref, lse_ref, *refs):
+    do_refs, refs = refs[:pieces], refs[pieces:]
+    o_refs, refs = refs[:pieces], refs[pieces:]
+    kv_refs, refs = refs[:blocks], refs[blocks:]
+    dq_ref, *refs = refs
+    dkv_refs, refs = refs[:blocks], refs[blocks:]
+    kt_ref, dout_ref, prod_ref, *refs = refs
+    dk_accs, dv_accs = refs[:blocks], refs[blocks:]
+    group = heads * HD
+    wide = q_ref.shape[1]
+    rows = kv_refs[0].shape[0]
+
+    @pl.when(pl.program_id(0) == 0)
+    def _():
+        for i in range(blocks):
+            kt_ref[:, i * rows : (i + 1) * rows] = kv_refs[i][:, :group].T
+            dk_accs[i][...] = jnp.zeros_like(dk_accs[i])
+            dv_accs[i][...] = jnp.zeros_like(dv_accs[i])
+
+    for j in range(pieces):
+
+        @pl.when(pl.program_id(0) == j)
+        def _(j=j):
+            dout_ref[...] = do_refs[j][...]
+            prod_ref[...] = (do_refs[j][...].astype(F32) * o_refs[j][...].astype(F32)).T
+
+    q = q_ref[...]
+    dout = dout_ref[...]
+    dqs = []
+    for head in range(heads):
+        q_head = jnp.where(head_lanes(wide, head, group), q, jnp.zeros_like(q))
+        do_head = jnp.where(head_lanes(group, head), dout, jnp.zeros_like(dout))
+        lse = lse_ref[head : head + 1, :]
+        delta = jnp.sum(prod_ref[head * HD : (head + 1) * HD, :], axis=0, keepdims=True)
+        acc = None
+        for i in range(blocks):
+            probs = jnp.exp2(dot_nt(kv_refs[i][:, :wide], q_head) - lse)
+            dv_accs[i][...] += dot_nn(probs.astype(BF16), do_head)
+            grads = dot_nt(kv_refs[i][:, wide : wide + group], do_head)
+            grads = (probs * (grads - delta)).astype(BF16)
+            dk_accs[i][...] += dot_nn(grads, q_head)
+            part = dot_nn(
+                kt_ref[head * HD : (head + 1) * HD, i * rows : (i + 1) * rows], grads
+            )
+            acc = part if acc is None else acc + part
+        dqs.append(acc)
+    dq_ref[...] = jnp.concatenate(dqs, axis=0).T.astype(BF16)
+
+    @pl.when(pl.program_id(0) == pl.num_programs(0) - 1)
+    def _():
+        for i in range(blocks):
+            dkv_refs[i][:, :group] = (dk_accs[i][:, :group] * LN2).astype(BF16)
+            dkv_refs[i][:, group:wide] = jnp.zeros((rows, wide - group), BF16)
+            dkv_refs[i][:, wide : wide + group] = dv_accs[i][...].astype(BF16)
+
+
+def attend_grad(q, kvs, douts, outs, lse, heads):
+    rows, wide = q.shape
+    group = heads * HD
+    blocks = len(kvs)
+    pieces = len(douts)
+    tile = rows // pieces
+    keys = blocks * rows
+    out = pl.pallas_call(
+        functools.partial(attend_grad_kernel, heads, blocks, pieces),
+        grid=(pieces,),
+        in_specs=[
+            pl.BlockSpec((tile, wide), lambda t: (t, 0)),
+            pl.BlockSpec((8, tile), lambda t: (0, t)),
+        ]
+        + [whole((tile, group))] * (2 * pieces)
+        + [whole(kvs[0].shape)] * blocks,
+        out_specs=[pl.BlockSpec((tile, group), lambda t: (t, 0))]
+        + [whole(kvs[0].shape)] * blocks,
+        out_shape=[jax.ShapeDtypeStruct((rows, group), BF16)]
+        + [jax.ShapeDtypeStruct(kvs[0].shape, BF16)] * blocks,
+        scratch_shapes=[
+            pltpu.VMEM((group, keys), BF16),
+            pltpu.VMEM((tile, group), BF16),
+            pltpu.VMEM((group, tile), F32),
+        ]
+        + [pltpu.VMEM((rows, wide), F32)] * blocks
+        + [pltpu.VMEM((rows, group), F32)] * blocks,
+        compiler_params=pltpu.CompilerParams(vmem_limit_bytes=48 * 2**20),
+        cost_estimate=pl.CostEstimate(
+            flops=10 * heads * rows * keys * wide,
+            transcendentals=heads * rows * keys,
+            bytes_accessed=2 * rows * wide * 4 + 4 * keys * (wide + group),
+        ),
+        name="attend_grad",
+    )(q, lse, *douts, *outs, *kvs)
+    return out[0], out[1:]
+
+
+def project_grad_kernel(sizes, idx, dq_ref, own_ref, got_ref, *refs):
+    uly, dp, group = sizes
+    x_refs, refs = refs[:uly], refs[uly:]
+    dproj_ref, keep_ref, send_ref = refs
+    b, z = idx[0], idx[2]
+    rows, width = x_refs[0].shape
+    wide = own_ref.shape[1] - group
+    share = keep_ref.shape[1] - 16
+    dproj_ref[:, :group] = dq_ref[...] * jnp.asarray(0.125, BF16)
+    dproj_ref[:, group:wide] = jnp.zeros((uly * rows, wide - group), BF16)
+    dproj_ref[:, wide:] = (own_ref[...].astype(F32) + got_ref[...].astype(F32)).astype(BF16)
+    sums = jnp.sum(dproj_ref[...].astype(F32), 0, keepdims=True).astype(BF16)
+    grad = None
+    for j in range(uly):
+        part = dot_tn(x_refs[j][...], dproj_ref[j * rows : (j + 1) * rows, :])
+        grad = part if grad is None else grad + part
+    grad = grad.astype(BF16)
+    for ref, mine in ((keep_ref, True), (send_ref, False)):
+        for c in range(3):
+            lanes = slice(c * wide, c * wide + group)
+            into = slice(c * group, (c + 1) * group)
+            for s in range(dp):
+                for core in range(2):
+                    start = (s * 2 + core) * share
+
+                    @pl.when((b == core) == mine)
+                    def _(start=start, s=s, ref=ref, lanes=lanes, into=into):
+                        ref[s ^ z, :share, into] = grad[start : start + share, lanes]
+
+                ref[s, share:, into] = jnp.broadcast_to(sums[:, lanes], (16, group))
+
+
+def token_grad_kernel(uly, idx, dproj_ref, w_ref, dh_ref, *out_refs):
+    rows = dh_ref.shape[0]
+    for j in reversed(range(uly)):
+        part = dot_nt(dproj_ref[j * rows : (j + 1) * rows, :], w_ref[...])
+        if j == 0:
+            part = part + dh_ref[...]
+        out_refs[j][...] = part.astype(out_refs[j].dtype)
+
+
+def finish_feed_kernel(sizes, idx, *refs):
+    uly, dp, unit = sizes
+    pieces, (expand_ref, shrink_ref) = refs[:-2], refs[-2:]
+    shard = expand_ref.shape[0]
+    width = shrink_ref.shape[1]
+    half = shard // 2
+    part = idx[0] * uly + idx[1]
+    outs = [None] * dp
+    for p, ref in enumerate(pieces):
+        start = pl.multiple_of((part ^ p) * unit, unit)
+        shrink_ref[pl.ds(start, unit), :] = ref[half:, :].astype(F32)
+        put = one_hot(unit, width, (part ^ p) * unit, 0)
+        for k in range(dp):
+            for h in range(2):
+                lanes = slice((h * dp + k) * unit, (h * dp + k + 1) * unit)
+                value = dot_nn(ref[:half, lanes], put)
+                rows = slice(h * half, (h + 1) * half)
+                cols = slice(k * width, (k + 1) * width)
+                if p == 0:
+                    expand_ref[rows, cols] = value
+                else:
+                    expand_ref[rows, cols] += value
+
+
+def finish_attend_kernel(uly, idx, *refs):
+    mine, refs = refs[:uly], refs[uly:]
+    other, refs = refs[:uly], refs[uly:]
+    out_ref, bias_ref = refs
+    b, u, z = idx[0], idx[1], idx[2]
+    share = mine[0].shape[0] - 16
+    group = mine[0].shape[1] // 3
+    width = uly * group
+    for group_refs, core in ((mine, b), (other, 1 - b)):
+        start = pl.multiple_of(core * share, share)
+        for c in range(3):
+            acc = None
+            for j in range(uly):
+                put = one_hot(group, width, (u ^ j) * group, 0)
+                value = dot_nn(group_refs[j][:share, c * group : (c + 1) * group], put)
+                acc = value if acc is None else acc + value
+            out_ref[pl.ds(start, share), c * width : (c + 1) * width] = acc
+    bias = jnp.zeros((8, 3 * group), F32)
+    for j in range(uly):
+        lines = mine[j][share : share + 16, :].astype(F32)[:8]
+        bias += jnp.where((u ^ j) == z, 1.0, 0.0) * lines
+    bias_ref[...] = bias
+
+
+def on_device(*args):
+    (
+        tokens,
+        lengths,
+        cotangent,
+        attend_weight,
+        query_bias,
+        value_bias,
+        mixer_weight,
+        mixer_bias,
+        attn_gain,
+        attn_shift,
+        expand_weight,
+        expand_bias,
+        shrink_weight,
+        shrink_bias,
+        final_gain,
+        final_shift,
+    ) = args
+    uly = lax.axis_size("uly")
+    blk = lax.axis_size("blk")
+    dp = lax.axis_size("dp")
+    width = tokens.shape[-1]
+    rows = tokens.shape[0] * tokens.shape[1]
+    heads = HEADS // uly
+    group = heads * HD
+    wide = -(-(group + 1) // 128) * 128
+    shard = attend_weight.shape[0]
+    hidden = expand_weight.shape[1]
+    parts = blk * uly
+    unit = hidden // (parts * dp)
+    share = shard // blk
+    if not (blk == 2 and uly == 4 and shard == group and unit * 2 == shard and share % 16 == 0):
+        return general_device(*args)
+    u = lax.axis_index("uly")
+    b = lax.axis_index("blk")
+    z = lax.axis_index("dp")
+    mixer_rows = shard // parts
+    feed_rows = shard // 2 + unit + mixer_rows
+    block_rows = uly * rows
+    cols = 2 * wide + group
+
+    x = tokens.reshape(rows, width)
+    xs = [x] + [swap_with(x, "uly", j) for j in range(1, uly)]
+    scalars = jnp.stack([b, u, z, lengths[0]]).astype(jnp.int32)
+    small = jnp.stack(
+        [query_bias, value_bias, mixer_bias, attn_gain, attn_shift, shrink_bias]
+        + [final_gain, final_shift]
+        + [expand_bias[k * shard : (k + 1) * shard] for k in range(hidden // dp // shard)]
+        + [jnp.zeros_like(query_bias)] * (8 - hidden // dp // shard)
+    )
+    first, feed = call(
+        functools.partial(fetch_kernel, (uly, dp, group, unit)),
+        "fetch",
+        scalars,
+        [
+            attend_weight.reshape(blk, share, 3 * width),
+            small,
+            expand_weight,
+            shrink_weight.reshape(parts, unit, width),
+            mixer_weight,
+        ],
+        [
+            pl.BlockSpec((1, share, 3 * width), lambda t, s: (s[0], 0, 0)),
+            whole(small.shape),
+            whole(expand_weight.shape),
+            pl.BlockSpec((1, unit, width), lambda t, s: (s[0] * uly + s[1], 0, 0)),
+            whole(mixer_weight.shape),
+        ],
+        [
+            jax.ShapeDtypeStruct((share + 16, 3 * group), BF16),
+            jax.ShapeDtypeStruct((feed_rows, width), BF16),
+        ],
+        [whole((share + 16, 3 * group)), whole((feed_rows, width))],
+        [],
+        (1,),
+        10**9,
+        32,
+    )
+    mine = [first] + [swap_with(first, "dp", j) for j in range(1, dp)]
+    other = [swap_with(piece, "blk", 1) for piece in mine]
+
+    feed_all = lax.all_gather(feed, "dp", axis=0, tiled=False)
+    half = shard // 2
+    halves = feed_all[:, :half].reshape(dp, half, 2, dp * unit).transpose(0, 2, 1, 3)
+    expand = [halves.reshape(width, dp * unit)]
+    shrink = [feed_all[:, half:]]
+    expand.append(swap_with(expand[0], "uly", 1))
+    shrink_y = swap_with(shrink[0], "uly", 2)
+    expand.append(swap_with(expand[0], "uly", 2))
+    shrink.append(swap_with(shrink[0], "uly", 1))
+    expand.append(swap_with(expand[1], "uly", 2))
+    shrink += [shrink_y, swap_with(shrink_y, "uly", 1)]
+    expand += [swap_with(piece, "blk", 1) for piece in expand]
+    shrink += [swap_with(piece, "blk", 1) for piece in shrink]
+    mixer_all = jnp.stack(xor_order([piece[:, unit:] for piece in shrink], b * uly + u), 1)
+    mixer_all = mixer_all.reshape(width, width)
+
+    w_own, q, kv, vec, eb = call(
+        functools.partial(project_kernel, (uly, blk, dp, group, unit)),
+        "project",
+        scalars,
+        [*xs, *mine, *other],
+        [whole((rows, width))] * uly + [whole(first.shape)] * (2 * dp),
+        [
+            jax.ShapeDtypeStruct((width, cols), BF16),
+            jax.ShapeDtypeStruct((block_rows, wide), BF16),
+            jax.ShapeDtypeStruct((block_rows, wide + group), BF16),
+            jax.ShapeDtypeStruct((16, width), F32),
+            jax.ShapeDtypeStruct((parts, dp * unit), F32),
+        ],
+        [
+            whole((width, cols)),
+            whole((block_rows, wide)),
+            whole((block_rows, wide + group)),
+            whole((16, width)),
+            whole((parts, dp * unit)),
+        ],
+        [],
+        (1,),
+        2 * block_rows * width * cols,
+        48,
+    )
+    kvs = [kv, swap_with(kv, "blk", 1)]
+    outs, lse = attend(q, kvs, heads, uly)
+    o_cols = [outs[0]] + [swap_with(outs[j], "uly", j) for j in range(1, uly)]
+
+    square = (rows, width)
+    x1, x1b, normed, inverse = call(
+        functools.partial(first_norm_kernel, uly),
+        "first_norm",
+        scalars,
+        [x, *o_cols, mixer_all, vec],
+        [whole(square)] + [whole((rows, group))] * uly + [whole((width, width)), whole(vec.shape)],
+        [
+            jax.ShapeDtypeStruct(square, F32),
+            jax.ShapeDtypeStruct(square, BF16),
+            jax.ShapeDtypeStruct(square, F32),
+            jax.ShapeDtypeStruct((rows, 1), F32),
+        ],
+        [whole(square), whole(square), whole(square), whole((rows, 1))],
+        [],
+        (1,),
+        2 * rows * width * width,
+        32,
+    )
+    mixed, dh2, dh2b, slope, s_keep, s_send, sums2 = feed_forward(
+        scalars, x1, x1b, eb, vec, cotangent.reshape(square), expand, shrink
+    )
+    s_got = swap_with(s_send, "blk", 1)
+    dx1, e_keep, e_send, deb = feed_backward(scalars, x1b, dh2, dh2b, slope, expand, shrink)
+    e_got = swap_with(e_send, "blk", 1)
+    block = (dp, share + 16, width)
+    dh1, *rest = call(
+        functools.partial(norm_backward_kernel, (uly, dp, unit)),
+        "norm_backward",
+        scalars,
+        [dx1, normed, inverse, mixer_all, vec, sums2, deb.reshape(parts, dp * unit), *o_cols],
+        [whole(square), whole(square), whole((rows, 1)), whole((width, width))]
+        + [whole(vec.shape), whole(sums2.shape), whole((parts, dp * unit))]
+        + [whole((rows, group))] * uly,
+        [jax.ShapeDtypeStruct(square, F32)]
+        + [jax.ShapeDtypeStruct((rows, group), BF16)] * uly
+        + [jax.ShapeDtypeStruct(block, BF16)] * 2,
+        [whole(square)] + [whole((rows, group))] * uly + [whole(block)] * 2,
+        [pltpu.VMEM((group, width), BF16)],
+        (1,),
+        4 * rows * width * width,
+        48,
+    )
+    douts = [rest[0]] + [swap_with(rest[j], "uly", j) for j in range(1, uly)]
+    m_keep, m_send = rest[uly:]
+    m_got = swap_with(m_send, "blk", 1)
+    dq, dkvs = attend_grad(q, kvs, douts, outs, lse, heads)
+
+    def add(*values):
+        return total(values).astype(BF16)
+
+    s_y = swap_with(add(s_keep[2:], s_got[2:]), "uly", 2)
+    s_x = swap_with(add(s_keep[1], s_got[1], s_y[1]), "uly", 1)
+    e_x = swap_with(
+        jnp.stack([add(e_keep[1], e_got[1]), add(e_keep[3], e_got[3])]), "uly", 1
+    )
+    e_y = swap_with(add(e_keep[2], e_got[2], e_x[1]), "uly", 2)
+
+    def feed_piece(j):
+        at = slice(j * unit, (j + 1) * unit)
+        low = [slice(j * shard + h * half, j * shard + (h + 1) * half) for h in range(2)]
+        sides = [add(e_keep[0, r], e_got[0, r], e_x[0, r], e_y[r]) for r in low]
+        bottom = add(s_keep[0, at], s_got[0, at], s_y[0, at], s_x[at])
+        return jnp.concatenate([jnp.concatenate(sides, 1), bottom], 0)
+
+    def over_dp(pieces):
+        return add(pieces[0], *[swap_with(pieces[j], "dp", j) for j in range(1, dp)])
+
+    owned = over_dp([feed_piece(j) for j in range(dp)])
+    plane = [owned] + [swap_with(owned, "uly", j) for j in range(1, uly)]
+    plane += [swap_with(piece, "blk", 1) for piece in plane]
+    expand_out, shrink_out = call(
+        functools.partial(finish_feed_kernel, (uly, dp, unit)),
+        "finish_feed",
+        scalars,
+        plane,
+        [whole(owned.shape)] * parts,
+        [
+            jax.ShapeDtypeStruct((shard, hidden), F32),
+            jax.ShapeDtypeStruct((hidden // dp, width), F32),
+        ],
+        [whole((shard, hidden)), whole((hidden // dp, width))],
+        [],
+        (1,),
+        10**9,
+        48,
+    )
+
+    m_own = over_dp([add(m_keep[j], m_got[j]) for j in range(dp)])
+    m_all = [m_own] + [swap_with(m_own, "uly", j) for j in range(1, uly)]
+    m_all = [value.astype(F32) for value in m_all]
+    m_all = (m_all[0] + m_all[1]) + (m_all[2] + m_all[3])
+    m_half = m_all[:share].astype(BF16)
+    mixer_out = jnp.concatenate(xor_order([m_half, swap_with(m_half, "blk", 1)], b), 0)
+    vecs = [m_all[share + k, :shard] for k in range(6)]
+    eb_out = m_all[share + 8 : share + 8 + parts, :unit].reshape(-1)
+
+    dproj, a_keep, a_send = call(
+        functools.partial(project_grad_kernel, (uly, dp, group)),
+        "project_grad",
+        scalars,
+        [dq, dkvs[0], swap_with(dkvs[1], "blk", 1), *xs],
+        [whole(dq.shape), whole(kv.shape), whole(kv.shape)] + [whole(square)] * uly,
+        [
+            jax.ShapeDtypeStruct((block_rows, cols), BF16),
+            jax.ShapeDtypeStruct((dp, share + 16, 3 * group), BF16),
+            jax.ShapeDtypeStruct((dp, share + 16, 3 * group), BF16),
+        ],
+        [whole((block_rows, cols))] + [whole((dp, share + 16, 3 * group))] * 2,
+        [],
+        (1,),
+        2 * block_rows * width * cols,
+        48,
+    )
+    a_got = swap_with(a_send, "blk", 1)
+    token_parts = call(
+        functools.partial(token_grad_kernel, uly),
+        "token_grad",
+        scalars,
+        [dproj, w_own, dh1],
+        [whole((block_rows, cols)), whole((width, cols)), whole(square)],
+        [jax.ShapeDtypeStruct(square, F32)] + [jax.ShapeDtypeStruct(square, BF16)] * (uly - 1),
+        [whole(square)] * uly,
+        [],
+        (1,),
+        2 * block_rows * width * cols,
+        48,
+    )
+    tokens_grad = total(
+        [token_parts[0]] + [swap_with(token_parts[j], "uly", j) for j in range(1, uly)]
+    )
+    a_own = over_dp([add(a_keep[j], a_got[j]) for j in range(dp)])
+    a_mine = [a_own] + [swap_with(a_own, "uly", j) for j in range(1, uly)]
+    a_other = [swap_with(piece, "blk", 1) for piece in a_mine]
+    attend_out, biases = call(
+        functools.partial(finish_attend_kernel, uly),
+        "finish_attend",
+        scalars,
+        [*a_mine, *a_other],
+        [whole(a_own.shape)] * (2 * uly),
+        [jax.ShapeDtypeStruct((shard, 3 * width), F32), jax.ShapeDtypeStruct((8, 3 * group), F32)],
+        [whole((shard, 3 * width)), whole((8, 3 * group))],
+        [],
+        (1,),
+        10**9,
+        48,
+    )
+    return (
+        mixed.reshape(tokens.shape),
+        tokens_grad.reshape(tokens.shape),
+        attend_out,
+        biases[0, :group],
+        biases[0, 2 * group :],
+        mixer_out.astype(F32),
+        vecs[0],
+        vecs[1],
+        vecs[2],
+        expand_out,
+        eb_out,
+        shrink_out,
+        vecs[3],
+        vecs[4],
+        vecs[5],
+    )
+
+
 def solution(mesh):
     row_spec = P("dp", ("blk", "uly"), None)
     matrix = P("dp", None)

time: 395 us -> 399 us (1.010)
  the two profiles are of different devices: /device:TPU:16 before, /device:TPU:0 now
where the time goes in v2:
time: 399 us; the launch traced here: 396 us
  waiting for transfers between devices  163 us (41%)
  Pallas kernels  90 us (23%)
  starting transfers between devices  65.9 us (17%)
  local copies, waits for them, and re-layouts  32.5 us (8%)
  other arithmetic  28.6 us (7%)
  between operations  15.2 us (4%)
    ppermute x70, waiting for transfers between devices, swap_with(): return lax.ppermute(value, axis, [(i, i ^ offset) for i in range(size)])  130 us
    ppermute x70, starting transfers between devices, swap_with(): return lax.ppermute(value, axis, [(i, i ^ offset) for i in range(size)])  65.8 us
    pallas_call x10, Pallas kernels, call(): pl.pallas_call(kernel, grid_spec=pltpu.PrefetchScalarGridSpec(num_scalar_...  57.6 us
    all_gather x1, waiting for transfers between devices, on_device(): feed_all = lax.all_gather(feed, 'dp', axis=0, tiled=False)  33.8 us
    pallas_call x1, Pallas kernels, attend_grad(): pl.pallas_call(functools.partial(attend_grad_kernel, heads, blocks, piece...  21 us
    convert_element_type x12, other arithmetic, add(): return total(values).astype(BF16)  19.4 us
    unnamed x61, local copies, waits for them, and re-layouts  14.8 us
    pallas_call x1, Pallas kernels, attend(): pl.pallas_call(functools.partial(attend_kernel, heads, blocks), grid=(pie...  11.4 us
  transfers between devices with their start and end apart: 71, of which 22 were waited for; matrix products, arithmetic and copies ran while one was open for 10% of the time, Pallas kernels for 13%

profile of v2, /device:TPU:0, one launch (start us, length us, event | category | flops | bytes accessed | tf_op | source)
XLA Modules:
  0.0 395.6 jit_solution(10567743017999054078)
XLA Ops:
  21.4 4.7 %collective-permute-start.5 = (bf16[112,576]{1,0:T(8,128)(2,1)S(1)}, bf16[112,576]{1,0:T(8,128)(2,1)S(1)}, u32[]{:S(2)}, u32[]{:S(2)}) collective-permute-start(bf16[112,576]{1,0:T(8,128)(2,1)S(1)} %get-tuple-element.63.refs_4_), channel_id=1, source_target_pairs={{0,24},{8,16},{16,8},{24,0},{1,25},{9,17},{17,9},{25,1},{2,26},{10... | collective-permute-start | bytes 387080 | tf_op jit(solution)/shard_map/ppermute | solution.py:35
  26.7 33.8 %all-gather.3.cloned.1.call-done = bf16[864,768]{1,0:T(8,128)(2,1)} async-done(((bf16[216,768]{1,0:T(8,128)(2,1)}), bf16[864,768]{1,0:T(8,128)(2,1)}) %all-gather.3.cloned.1.call-update) | async-done | bytes 1327120 | tf_op jit(solution)/shard_map/all_gather | solution.py:1411
  71.7 5.3 %collective-permute-done.2.refs_3_ = bf16[256,768]{1,0:T(8,128)(2,1)S(1)} collective-permute-done((bf16[256,768]{1,0:T(8,128)(2,1)S(1)}, bf16[256,768]{1,0:T(8,128)(2,1)S(1)}, u32[]{:S(2)}, u32[]{:S(2)}) %collective-permute-start.2) | collective-permute-done | bytes 393248 | tf_op jit(solution)/shard_map/ppermute | solution.py:35
  77.0 21.1 %collective-permute-done.1.refs_2_ = bf16[256,768]{1,0:T(8,128)(2,1)S(1)} collective-permute-done((bf16[256,768]{1,0:T(8,128)(2,1)S(1)}, bf16[256,768]{1,0:T(8,128)(2,1)S(1)}, u32[]{:S(2)}, u32[]{:S(2)}) %collective-permute-start.1) | collective-permute-done | bytes 393248 | tf_op jit(solution)/shard_map/ppermute | solution.py:35
  98.1 2.7 project.1
  110.4 13.2 %collective-permute-done.18.refs_9_ = bf16[4,120,768]{2,1,0:T(8,128)(2,1)} collective-permute-done((bf16[4,120,768]{2,1,0:T(8,128)(2,1)}, bf16[4,120,768]{2,1,0:T(8,128)(2,1)}, u32[]{:S(2)}, u32[]{:S(2)}) %collective-permute-start.18) | collective-permute-done | bytes 737312 | tf_op jit(solution)/shard_map/ppermute | solution.py:35
  124.1 15.3 %collective-permute-done.15.refs_11_ = bf16[4,120,768]{2,1,0:T(8,128)(2,1)} collective-permute-done((bf16[4,120,768]{2,1,0:T(8,128)(2,1)}, bf16[4,120,768]{2,1,0:T(8,128)(2,1)}, u32[]{:S(2)}, u32[]{:S(2)}) %collective-permute-start.15) | collective-permute-done | bytes 737312 | tf_op jit(solution)/shard_map/ppermute | solution.py:35
  140.9 10.8 %collective-permute-done.21.refs_1_ = bf16[768,384]{1,0:T(8,128)(2,1)} collective-permute-done((bf16[768,384]{1,0:T(8,128)(2,1)S(1)}, bf16[768,384]{1,0:T(8,128)(2,1)}, u32[]{:S(2)}, u32[]{:S(2)}) %collective-permute-start.21) | collective-permute-done | bytes 589856 | tf_op jit(solution)/shard_map/ppermute | solution.py:35
  154.2 11.4 %attend.1 = (bf16[256,192]{1,0:T(8,128)(2,1)S(1)}, bf16[256,192]{1,0:T(8,128)(2,1)S(1)}, bf16[256,192]{1,0:T(8,128)(2,1)S(1)}, bf16[256,192]{1,0:T(8,128)(2,1)S(1)}, f32[8,1024]{1,0:T(8,128)S(1)}) custom-call(bf16[1024,256]{1,0:T(8,128)(2,1)S(1)} %copy-done.27, bf16[1024,448]{1,0:T(8,128)(2,1)S(1)} %get-tuple-element.65.refs_0_.refs_8_, ...), custom_call_target="tpu_custom_call" | custom-call | flops 6442450944 | bytes 3407872 | tf_op jit(solution)/shard_map/attend/pallas_call | solution.py:814
  172.9 4.2 %collective-permute-done.12.refs_2_.refs_4_ = bf16[256,192]{1,0:T(8,128)(2,1)S(1)} collective-permute-done((bf16[256,192]{1,0:T(8,128)(2,1)S(1)}, bf16[256,192]{1,0:T(8,128)(2,1)S(1)}, u32[]{:S(2)}, u32[]{:S(2)}) %collective-permute-start.12) | collective-permute-done | bytes 98336 | tf_op jit(solution)/shard_map/ppermute | solution.py:35
  179.4 3.6 collective-permute-done.13.refs_3_.refs_5_
  185.3 17.0 %feed_forward.1 = (bf16[256,768]{1,0:T(8,128)(2,1)}, f32[256,768]{1,0:T(8,128)}, bf16[256,768]{1,0:T(8,128)(2,1)S(1)}, bf16[8,256,384]{2,1,0:T(8,128)(2,1)}, bf1...) custom-call(s32[4]{0:T(128)S(1)} %pad_add_fusion.idx, f32[256,768]{1,0:T(8,128)} %copy-done.21, ...), custom_call_target="tpu_custom_call" | custom-call | flops 3623878656 | bytes 12251136 | tf_op jit(solution)/shard_map/feed_forward/pallas_call | solution.py:654
  202.3 16.0 %feed_backward.1 = (f32[256,768]{1,0:T(8,128)}, bf16[4,768,384]{2,1,0:T(8,128)(2,1)}, bf16[4,768,384]{2,1,0:T(8,128)(2,1)}, f32[8,1,384]{2,1,0:T(1,128)S(1)}) custom-call(s32[4]{0:T(128)S(1)} %pad_add_fusion.idx, bf16[256,768]{1,0:T(8,128)(2,1)S(1)} %get-tuple-element.73.x1b_ref, f32[256,768]{1,0:T(8,128)} %get-tuple-element.77.dh_ref, ...), custom_call_target="tpu_custom_call" | custom-call | flops 3623878656 | bytes 13762560 | tf_op jit(solution)/shard_map/feed_backward/pallas_call | solution.py:654
  220.0 3.1 norm_backward.1
  226.6 2.7 collective-permute-done.28.refs_1_
  229.3 2.9 collective-permute-done.29.refs_2_
  232.3 21.0 %attend_grad.1 = (bf16[1024,192]{1,0:T(8,128)(2,1)S(1)}, bf16[1024,448]{1,0:T(8,128)(2,1)S(1)}, bf16[1024,448]{1,0:T(8,128)(2,1)S(1)}) custom-call(bf16[1024,256]{1,0:T(8,128)(2,1)S(1)} %copy-done.28, f32[8,1024]{1,0:T(8,128)S(1)} %get-tuple-element.76.lse_ref, bf16[256,192]{1,0:T(8,128)(2,1)S(1)} %get-tuple-element.85.refs_0_, ...), custom_call_target="tpu_custom_call" | custom-call | flops 16106127360 | bytes 5767168 | tf_op jit(solution)/shard_map/attend_grad/pallas_call | solution.py:1209
  261.0 2.6 add_convert_fusion
  268.2 5.6 %collective-permute-done.49 = bf16[112,768]{1,0:T(8,128)(2,1)S(1)} collective-permute-done((bf16[112,768]{1,0:T(8,128)(2,1)S(1)}, bf16[112,768]{1,0:T(8,128)(2,1)S(1)}, u32[]{:S(2)}, u32[]{:S(2)}) %collective-permute-start.49) | collective-permute-done | bytes 172064 | tf_op jit(solution)/shard_map/ppermute | solution.py:35
  273.9 9.6 %collective-permute-done.48 = bf16[112,768]{1,0:T(8,128)(2,1)S(1)} collective-permute-done((bf16[112,768]{1,0:T(8,128)(2,1)S(1)}, bf16[112,768]{1,0:T(8,128)(2,1)S(1)}, u32[]{:S(2)}, u32[]{:S(2)}) %collective-permute-start.48) | collective-permute-done | bytes 172064 | tf_op jit(solution)/shard_map/ppermute | solution.py:35
  293.2 4.7 %project_grad.1 = (bf16[1024,704]{1,0:T(8,128)(2,1)}, bf16[4,112,576]{2,1,0:T(8,128)(2,1)S(1)}, bf16[4,112,576]{2,1,0:T(8,128)(2,1)}) custom-call(s32[4]{0:T(128)S(1)} %pad_add_fusion.idx, bf16[1024,192]{1,0:T(8,128)(2,1)S(1)} %copy-done.8, bf16[1024,448]{1,0:T(8,128)(2,1)S(1)} %get-tuple-element.90.own_ref, bf16[1024,448]{1,0:T(8,128)(2,1)S(1)} %copy.39.got_ref, ...), custom_call_target="tpu_custom_call" | custom-call | flops 1107296256 | bytes 3801088 | tf_op jit(solution)/shard_map/project_grad/pallas_call | solution.py:654
  299.3 2.5 token_grad.1
  315.1 9.7 %collective-permute-done.56 = bf16[768,384]{1,0:T(8,128)(2,1)S(1)} collective-permute-done((bf16[768,384]{1,0:T(8,128)(2,1)}, bf16[768,384]{1,0:T(8,128)(2,1)S(1)}, u32[]{:S(2)}, u32[]{:S(2)}) %collective-permute-start.56) | collective-permute-done | bytes 589856 | tf_op jit(solution)/shard_map/ppermute | solution.py:35
  326.7 2.5 collective-permute-start.38
  334.7 6.0 %collective-permute-start.61 = (bf16[192,768]{1,0:T(8,128)(2,1)S(1)}, bf16[192,768]{1,0:T(8,128)(2,1)S(1)}, u32[]{:S(2)}, u32[]{:S(2)}) collective-permute-start(bf16[192,768]{1,0:T(8,128)(2,1)S(1)} %pad_maximum_fusion.2), channel_id=1, source_target_pairs={{0,16},{8,24},{16,0},{24,8},{1,17},{9,25},{17,1},{25,9},{2,18},{10... | collective-permute-start | bytes 884744 | tf_op jit(solution)/shard_map/ppermute | solution.py:35
  341.8 4.2 %collective-permute-start.62 = (bf16[192,768]{1,0:T(8,128)(2,1)S(1)}, bf16[192,768]{1,0:T(8,128)(2,1)S(1)}, u32[]{:S(2)}, u32[]{:S(2)}) collective-permute-start(bf16[192,768]{1,0:T(8,128)(2,1)S(1)} %pad_maximum_fusion.3), channel_id=1, source_target_pairs={{0,24},{8,16},{16,8},{24,0},{1,25},{9,17},{17,9},{25,1},{2,26},{10... | collective-permute-start | bytes 884744 | tf_op jit(solution)/shard_map/ppermute | solution.py:35
  347.0 2.6 collective-permute-start.34
  350.0 8.6 %collective-permute-done.41.refs_3_ = bf16[112,576]{1,0:T(8,128)(2,1)S(1)} collective-permute-done((bf16[112,576]{1,0:T(8,128)(2,1)S(1)}, bf16[112,576]{1,0:T(8,128)(2,1)S(1)}, u32[]{:S(2)}, u32[]{:S(2)}) %collective-permute-start.41) | collective-permute-done | bytes 129056 | tf_op jit(solution)/shard_map/ppermute | solution.py:35
  369.7 3.8 collective-permute-done.65.refs_3_
  373.5 5.9 %collective-permute-done.64.refs_2_ = bf16[192,768]{1,0:T(8,128)(2,1)S(1)} collective-permute-done((bf16[192,768]{1,0:T(8,128)(2,1)S(1)}, bf16[192,768]{1,0:T(8,128)(2,1)S(1)}, u32[]{:S(2)}, u32[]{:S(2)}) %collective-permute-start.64) | collective-permute-done | bytes 294944 | tf_op jit(solution)/shard_map/ppermute | solution.py:35
  379.9 2.9 finish_attend.1
  383.4 5.4 %finish_feed.1 = (f32[192,3072]{1,0:T(8,128)}, f32[768,768]{1,0:T(8,128)}) custom-call(s32[4]{0:T(128)S(1)} %pad_add_fusion.idx, bf16[192,768]{1,0:T(8,128)(2,1)S(1)} %add_convert_fusion.5.refs_0_, bf16[192,768]{1,0:T(8,128)(2,1)S(1)} %collective-permute-done.63.refs_1_, bf16[192,768]{1,0:T(8,128)(2,1)S(1)} %collective-permute-done.64.refs_2_, ...), custom_call_target="tpu_custom_call" | custom-call | flops 1000000000 | bytes 2359296 | tf_op jit(solution)/shard_map/finish_feed/pallas_call | solution.py:654
  (242 shorter events, 115.2 us)
Async XLA Ops:
  7.2 53.4 %all-gather.3.cloned.1.call-start = ((), (), s32[]{:S(2)}) async-start(), calls=%async_computation | async-start | bytes 1658880 | tf_op jit(solution)/shard_map/all_gather | solution.py:1411
  20.9 43.2 %collective-permute-start.6 = (bf16[112,576]{1,0:T(8,128)(2,1)S(1)}, bf16[112,576]{1,0:T(8,128)(2,1)S(1)}, u32[]{:S(2)}, u32[]{:S(2)}) collective-permute-start(bf16[112,576]{1,0:T(8,128)(2,1)S(1)} %get-tuple-element.63.refs_4_), channel_id=1, source_target_pairs={{0,4},{4,0},{1,5},{5,1},{2,6},{6,2},{3,7},{7,3},{8,12},{12,8},{9,1... | collective-permute-start | bytes 387080 | tf_op jit(solution)/shard_map/ppermute | solution.py:35
  21.4 44.1 %collective-permute-start.5 = (bf16[112,576]{1,0:T(8,128)(2,1)S(1)}, bf16[112,576]{1,0:T(8,128)(2,1)S(1)}, u32[]{:S(2)}, u32[]{:S(2)}) collective-permute-start(bf16[112,576]{1,0:T(8,128)(2,1)S(1)} %get-tuple-element.63.refs_4_), channel_id=1, source_target_pairs={{0,24},{8,16},{16,8},{24,0},{1,25},{9,17},{17,9},{25,1},{2,26},{10... | collective-permute-start | bytes 387080 | tf_op jit(solution)/shard_map/ppermute | solution.py:35
  26.1 41.0 %collective-permute-start.4 = (bf16[112,576]{1,0:T(8,128)(2,1)S(1)}, bf16[112,576]{1,0:T(8,128)(2,1)S(1)}, u32[]{:S(2)}, u32[]{:S(2)}) collective-permute-start(bf16[112,576]{1,0:T(8,128)(2,1)S(1)} %get-tuple-element.63.refs_4_), channel_id=1, source_target_pairs={{0,16},{8,24},{16,0},{24,8},{1,17},{9,25},{17,1},{25,9},{2,18},{10... | collective-permute-start | bytes 387080 | tf_op jit(solution)/shard_map/ppermute | solution.py:35
  26.1 41.5 %collective-permute-start.3 = (bf16[112,576]{1,0:T(8,128)(2,1)S(1)}, bf16[112,576]{1,0:T(8,128)(2,1)S(1)}, u32[]{:S(2)}, u32[]{:S(2)}) collective-permute-start(bf16[112,576]{1,0:T(8,128)(2,1)S(1)} %get-tuple-element.63.refs_4_), channel_id=1, source_target_pairs={{0,8},{8,0},{16,24},{24,16},{1,9},{9,1},{17,25},{25,17},{2,10},{10... | collective-permute-start | bytes 387080 | tf_op jit(solution)/shard_map/ppermute | solution.py:35
  62.6 42.9 %collective-permute-start.14 = (bf16[4,120,768]{2,1,0:T(8,128)(2,1)}, bf16[4,120,768]{2,1,0:T(8,128)(2,1)}, u32[]{:S(2)}, u32[]{:S(2)}) collective-permute-start(bf16[4,120,768]{2,1,0:T(8,128)(2,1)} %slice.402.refs_8_), channel_id=1, source_target_pairs={{0,2},{1,3},{2,0},{3,1},{4,6},{5,7},{6,4},{7,5},{8,10},{9,11},{10,... | collective-permute-start | bytes 2211848 | tf_op jit(solution)/shard_map/ppermute | solution.py:35
  65.6 32.5 %collective-permute-start.1 = (bf16[256,768]{1,0:T(8,128)(2,1)S(1)}, bf16[256,768]{1,0:T(8,128)(2,1)S(1)}, u32[]{:S(2)}, u32[]{:S(2)}) collective-permute-start(bf16[256,768]{1,0:T(8,128)(2,1)S(1)} %bitcast.123), channel_id=1, source_target_pairs={{0,2},{1,3},{2,0},{3,1},{4,6},{5,7},{6,4},{7,5},{8,10},{9,11},{10,... | collective-permute-start | bytes 1179656 | tf_op jit(solution)/shard_map/ppermute | solution.py:35
  67.1 31.0 %collective-permute-start = (bf16[256,768]{1,0:T(8,128)(2,1)S(1)}, bf16[256,768]{1,0:T(8,128)(2,1)S(1)}, u32[]{:S(2)}, u32[]{:S(2)}) collective-permute-start(bf16[256,768]{1,0:T(8,128)(2,1)S(1)} %bitcast.124), channel_id=1, source_target_pairs={{0,1},{1,0},{2,3},{3,2},{4,5},{5,4},{6,7},{7,6},{8,9},{9,8},{10,11... | collective-permute-start | bytes 1179656 | tf_op jit(solution)/shard_map/ppermute | solution.py:35
  104.0 19.6 %collective-permute-start.18 = (bf16[4,120,768]{2,1,0:T(8,128)(2,1)}, bf16[4,120,768]{2,1,0:T(8,128)(2,1)}, u32[]{:S(2)}, u32[]{:S(2)}) collective-permute-start(bf16[4,120,768]{2,1,0:T(8,128)(2,1)} %slice.402.refs_8_), channel_id=1, source_target_pairs={{0,1},{1,0},{2,3},{3,2},{4,5},{5,4},{6,7},{7,6},{8,9},{9,8},{10,11... | collective-permute-start | bytes 2211848 | tf_op jit(solution)/shard_map/ppermute | solution.py:35
  105.5 33.9 %collective-permute-start.15 = (bf16[4,120,768]{2,1,0:T(8,128)(2,1)}, bf16[4,120,768]{2,1,0:T(8,128)(2,1)}, u32[]{:S(2)}, u32[]{:S(2)}) collective-permute-start(bf16[4,120,768]{2,1,0:T(8,128)(2,1)} %collective-permute-done.14.refs_10_), channel_id=1, source_target_pairs={{0,1},{1,0},{2,3},{3,2},{4,5},{5,4},{6,7},{7,6},{8,9},{9,8},{10,11... | collective-permute-start | bytes 2211848 | tf_op jit(solution)/shard_map/ppermute | solution.py:35
  108.9 42.7 %collective-permute-start.21 = (bf16[768,384]{1,0:T(8,128)(2,1)S(1)}, bf16[768,384]{1,0:T(8,128)(2,1)}, u32[]{:S(2)}, u32[]{:S(2)}) collective-permute-start(bf16[768,384]{1,0:T(8,128)(2,1)S(1)} %bitcast.118), channel_id=1, source_target_pairs={{0,1},{1,0},{2,3},{3,2},{4,5},{5,4},{6,7},{7,6},{8,9},{9,8},{10,11... | collective-permute-start | bytes 1769480 | tf_op jit(solution)/shard_map/ppermute | solution.py:35
  110.4 55.2 %collective-permute-start.20 = (bf16[4,120,768]{2,1,0:T(8,128)(2,1)}, bf16[4,120,768]{2,1,0:T(8,128)(2,1)}, u32[]{:S(2)}, u32[]{:S(2)}) collective-permute-start(bf16[4,120,768]{2,1,0:T(8,128)(2,1)} %slice.402.refs_8_), channel_id=1, source_target_pairs={{0,4},{4,0},{1,5},{5,1},{2,6},{6,2},{3,7},{7,3},{8,12},{12,8},{9,1... | collective-permute-start | bytes 2211848 | tf_op jit(solution)/shard_map/ppermute | solution.py:35
  123.6 43.6 %collective-permute-start.19 = (bf16[4,120,768]{2,1,0:T(8,128)(2,1)}, bf16[4,120,768]{2,1,0:T(8,128)(2,1)}, u32[]{:S(2)}, u32[]{:S(2)}) collective-permute-start(bf16[4,120,768]{2,1,0:T(8,128)(2,1)} %collective-permute-done.18.refs_9_), channel_id=1, source_target_pairs={{0,4},{4,0},{1,5},{5,1},{2,6},{6,2},{3,7},{7,3},{8,12},{12,8},{9,1... | collective-permute-start | bytes 2211848 | tf_op jit(solution)/shard_map/ppermute | solution.py:35
  123.6 44.1 %collective-permute-start.17 = (bf16[4,120,768]{2,1,0:T(8,128)(2,1)}, bf16[4,120,768]{2,1,0:T(8,128)(2,1)}, u32[]{:S(2)}, u32[]{:S(2)}) collective-permute-start(bf16[4,120,768]{2,1,0:T(8,128)(2,1)} %collective-permute-done.14.refs_10_), channel_id=1, source_target_pairs={{0,4},{4,0},{1,5},{5,1},{2,6},{6,2},{3,7},{7,3},{8,12},{12,8},{9,1... | collective-permute-start | bytes 2211848 | tf_op jit(solution)/shard_map/ppermute | solution.py:35
  139.4 28.4 %collective-permute-start.16 = (bf16[4,120,768]{2,1,0:T(8,128)(2,1)}, bf16[4,120,768]{2,1,0:T(8,128)(2,1)}, u32[]{:S(2)}, u32[]{:S(2)}) collective-permute-start(bf16[4,120,768]{2,1,0:T(8,128)(2,1)} %collective-permute-done.15.refs_11_), channel_id=1, source_target_pairs={{0,4},{4,0},{1,5},{5,1},{2,6},{6,2},{3,7},{7,3},{8,12},{12,8},{9,1... | collective-permute-start | bytes 2211848 | tf_op jit(solution)/shard_map/ppermute | solution.py:35
  167.2 18.1 %collective-permute-start.24 = (bf16[768,384]{1,0:T(8,128)(2,1)S(1)}, bf16[768,384]{1,0:T(8,128)(2,1)S(1)}, u32[]{:S(2)}, u32[]{:S(2)}) collective-permute-start(bf16[768,384]{1,0:T(8,128)(2,1)S(1)} %bitcast.119), channel_id=1, source_target_pairs={{0,4},{4,0},{1,5},{5,1},{2,6},{6,2},{3,7},{7,3},{8,12},{12,8},{9,1... | collective-permute-start | bytes 1769480 | tf_op jit(solution)/shard_map/ppermute | solution.py:35
  167.2 18.1 %collective-permute-start.25 = (bf16[768,384]{1,0:T(8,128)(2,1)}, bf16[768,384]{1,0:T(8,128)(2,1)S(1)}, u32[]{:S(2)}, u32[]{:S(2)}) collective-permute-start(bf16[768,384]{1,0:T(8,128)(2,1)} %collective-permute-done.21.refs_1_), channel_id=1, source_target_pairs={{0,4},{4,0},{1,5},{5,1},{2,6},{6,2},{3,7},{7,3},{8,12},{12,8},{9,1... | collective-permute-start | bytes 1769480 | tf_op jit(solution)/shard_map/ppermute | solution.py:35
  167.7 17.6 %collective-permute-start.26 = (bf16[768,384]{1,0:T(8,128)(2,1)S(1)}, bf16[768,384]{1,0:T(8,128)(2,1)S(1)}, u32[]{:S(2)}, u32[]{:S(2)}) collective-permute-start(bf16[768,384]{1,0:T(8,128)(2,1)S(1)} %copy-done.6), channel_id=1, source_target_pairs={{0,4},{4,0},{1,5},{5,1},{2,6},{6,2},{3,7},{7,3},{8,12},{12,8},{9,1... | collective-permute-start | bytes 1769480 | tf_op jit(solution)/shard_map/ppermute | solution.py:35
  167.8 17.5 %collective-permute-start.27 = (bf16[768,384]{1,0:T(8,128)(2,1)S(1)}, bf16[768,384]{1,0:T(8,128)(2,1)S(1)}, u32[]{:S(2)}, u32[]{:S(2)}) collective-permute-start(bf16[768,384]{1,0:T(8,128)(2,1)S(1)} %collective-permute-done.23.refs_3_), channel_id=1, source_target_pairs={{0,4},{4,0},{1,5},{5,1},{2,6},{6,2},{3,7},{7,3},{8,12},{12,8},{9,1... | collective-permute-start | bytes 1769480 | tf_op jit(solution)/shard_map/ppermute | solution.py:35
  218.3 38.3 %collective-permute-start.54 = (bf16[4,768,384]{2,1,0:T(8,128)(2,1)}, bf16[4,768,384]{2,1,0:T(8,128)(2,1)}, u32[]{:S(2)}, u32[]{:S(2)}) collective-permute-start(bf16[4,768,384]{2,1,0:T(8,128)(2,1)} %get-tuple-element.106), channel_id=1, source_target_pairs={{0,4},{4,0},{1,5},{5,1},{2,6},{6,2},{3,7},{7,3},{8,12},{12,8},{9,1... | collective-permute-start | bytes 7077896 | tf_op jit(solution)/shard_map/ppermute | solution.py:35
  218.4 42.6 %collective-permute-start.57 = (bf16[4,384,768]{2,1,0:T(8,128)(2,1)}, bf16[4,384,768]{2,1,0:T(8,128)(2,1)}, u32[]{:S(2)}, u32[]{:S(2)}) collective-permute-start(bf16[4,384,768]{2,1,0:T(8,128)(2,1)} %get-tuple-element.108), channel_id=1, source_target_pairs={{0,4},{4,0},{1,5},{5,1},{2,6},{6,2},{3,7},{7,3},{8,12},{12,8},{9,1... | collective-permute-start | bytes 7077896 | tf_op jit(solution)/shard_map/ppermute | solution.py:35
  229.3 26.0 %collective-permute-start.46 = (bf16[4,112,768]{2,1,0:T(8,128)(2,1)}, bf16[4,112,768]{2,1,0:T(8,128)(2,1)}, u32[]{:S(2)}, u32[]{:S(2)}) collective-permute-start(bf16[4,112,768]{2,1,0:T(8,128)(2,1)} %get-tuple-element.104), channel_id=1, source_target_pairs={{0,4},{4,0},{1,5},{5,1},{2,6},{6,2},{3,7},{7,3},{8,12},{12,8},{9,1... | collective-permute-start | bytes 2064392 | tf_op jit(solution)/shard_map/ppermute | solution.py:35
  255.3 32.2 %collective-permute-start.31 = (bf16[1024,448]{0,1:T(8,128)(2,1)}, bf16[1024,448]{0,1:T(8,128)(2,1)}, u32[]{:S(2)}, u32[]{:S(2)}) collective-permute-start(bf16[1024,448]{0,1:T(8,128)(2,1)} %copy.38), channel_id=1, source_target_pairs={{0,4},{4,0},{1,5},{5,1},{2,6},{6,2},{3,7},{7,3},{8,12},{12,8},{9,1... | collective-permute-start | bytes 2752520 | tf_op jit(solution)/shard_map/ppermute | solution.py:35
  259.8 45.0 %collective-permute-start.55 = (bf16[2,768,384]{2,1,0:T(8,128)(2,1)}, bf16[2,768,384]{2,1,0:T(8,128)(2,1)}, u32[]{:S(2)}, u32[]{:S(2)}) collective-permute-start(bf16[2,768,384]{2,1,0:T(8,128)(2,1)} %pad_maximum_fusion), channel_id=1, source_target_pairs={{0,1},{1,0},{2,3},{3,2},{4,5},{5,4},{6,7},{7,6},{8,9},{9,8},{10,11... | collective-permute-start | bytes 3538952 | tf_op jit(solution)/shard_map/ppermute | solution.py:35
  263.6 44.9 %collective-permute-start.58 = (bf16[2,384,768]{2,1,0:T(8,128)(2,1)}, bf16[2,384,768]{2,1,0:T(8,128)(2,1)}, u32[]{:S(2)}, u32[]{:S(2)}) collective-permute-start(bf16[2,384,768]{2,1,0:T(8,128)(2,1)} %add_convert_fusion), channel_id=1, source_target_pairs={{0,2},{1,3},{2,0},{3,1},{4,6},{5,7},{6,4},{7,5},{8,10},{9,11},{10,... | collective-permute-start | bytes 3538952 | tf_op jit(solution)/shard_map/ppermute | solution.py:35
  301.8 45.2 %collective-permute-start.32 = (bf16[256,768]{1,0:T(8,128)(2,1)}, bf16[256,768]{1,0:T(8,128)(2,1)}, u32[]{:S(2)}, u32[]{:S(2)}) collective-permute-start(bf16[256,768]{1,0:T(8,128)(2,1)} %get-tuple-element.96), channel_id=1, source_target_pairs={{0,1},{1,0},{2,3},{3,2},{4,5},{5,4},{6,7},{7,6},{8,9},{9,8},{10,11... | collective-permute-start | bytes 1179656 | tf_op jit(solution)/shard_map/ppermute | solution.py:35
  302.7 46.8 %collective-permute-start.33 = (bf16[256,768]{1,0:T(8,128)(2,1)}, bf16[256,768]{1,0:T(8,128)(2,1)}, u32[]{:S(2)}, u32[]{:S(2)}) collective-permute-start(bf16[256,768]{1,0:T(8,128)(2,1)} %get-tuple-element.97), channel_id=1, source_target_pairs={{0,2},{1,3},{2,0},{3,1},{4,6},{5,7},{6,4},{7,5},{8,10},{9,11},{10,... | collective-permute-start | bytes 1179656 | tf_op jit(solution)/shard_map/ppermute | solution.py:35
  307.3 17.5 %collective-permute-start.56 = (bf16[768,384]{1,0:T(8,128)(2,1)}, bf16[768,384]{1,0:T(8,128)(2,1)S(1)}, u32[]{:S(2)}, u32[]{:S(2)}) collective-permute-start(bf16[768,384]{1,0:T(8,128)(2,1)} %fusion), channel_id=1, source_target_pairs={{0,2},{1,3},{2,0},{3,1},{4,6},{5,7},{6,4},{7,5},{8,10},{9,11},{10,... | collective-permute-start | bytes 1769480 | tf_op jit(solution)/shard_map/ppermute | solution.py:35
  314.0 18.6 %collective-permute-start.53 = (bf16[96,768]{1,0:T(8,128)(2,1)}, bf16[96,768]{1,0:T(8,128)(2,1)S(1)}, u32[]{:S(2)}, u32[]{:S(2)}) collective-permute-start(bf16[96,768]{1,0:T(8,128)(2,1)} %slice.564), channel_id=1, source_target_pairs={{0,4},{4,0},{1,5},{5,1},{2,6},{6,2},{3,7},{7,3},{8,12},{12,8},{9,1... | collective-permute-start | bytes 442376 | tf_op jit(solution)/shard_map/ppermute | solution.py:35
  333.3 25.3 %collective-permute-start.60 = (bf16[192,768]{1,0:T(8,128)(2,1)S(1)}, bf16[192,768]{1,0:T(8,128)(2,1)S(1)}, u32[]{:S(2)}, u32[]{:S(2)}) collective-permute-start(bf16[192,768]{1,0:T(8,128)(2,1)S(1)} %pad_maximum_fusion.1), channel_id=1, source_target_pairs={{0,8},{8,0},{16,24},{24,16},{1,9},{9,1},{17,25},{25,17},{2,10},{10... | collective-permute-start | bytes 884744 | tf_op jit(solution)/shard_map/ppermute | solution.py:35
  334.7 26.5 %collective-permute-start.61 = (bf16[192,768]{1,0:T(8,128)(2,1)S(1)}, bf16[192,768]{1,0:T(8,128)(2,1)S(1)}, u32[]{:S(2)}, u32[]{:S(2)}) collective-permute-start(bf16[192,768]{1,0:T(8,128)(2,1)S(1)} %pad_maximum_fusion.2), channel_id=1, source_target_pairs={{0,16},{8,24},{16,0},{24,8},{1,17},{9,25},{17,1},{25,9},{2,18},{10... | collective-permute-start | bytes 884744 | tf_op jit(solution)/shard_map/ppermute | solution.py:35
  341.8 20.5 %collective-permute-start.62 = (bf16[192,768]{1,0:T(8,128)(2,1)S(1)}, bf16[192,768]{1,0:T(8,128)(2,1)S(1)}, u32[]{:S(2)}, u32[]{:S(2)}) collective-permute-start(bf16[192,768]{1,0:T(8,128)(2,1)S(1)} %pad_maximum_fusion.3), channel_id=1, source_target_pairs={{0,24},{8,16},{16,8},{24,0},{1,25},{9,17},{17,9},{25,1},{2,26},{10... | collective-permute-start | bytes 884744 | tf_op jit(solution)/shard_map/ppermute | solution.py:35
  (69 other events, 602.8 us)
Sparse Core Ops, SparseCore 0:
  21.0 39.4 all-gather.2

commit v3 on v2

--- a/solution.py
+++ b/solution.py
@@ -650,7 +650,6 @@
 
 
 def call(kernel, name, scalars, args, in_specs, out_shape, out_specs, scratch, grid, flops, vmem):
-    size = sum(a.size * a.dtype.itemsize for a in args)
     return pl.pallas_call(
         kernel,
         grid_spec=pltpu.PrefetchScalarGridSpec(
@@ -662,13 +661,21 @@
         ),
         out_shape=out_shape,
         compiler_params=pltpu.CompilerParams(vmem_limit_bytes=vmem * 2**20),
-        cost_estimate=pl.CostEstimate(flops=flops, bytes_accessed=size, transcendentals=0),
+        cost_estimate=pl.CostEstimate(flops=flops, bytes_accessed=1, transcendentals=0),
         name=name,
     )(scalars, *args)
 
 
 def whole(shape):
     return pl.BlockSpec(shape, lambda *_: (0,) * len(shape))
+
+
+def after(value, *deps):
+    return lax.optimization_barrier((value, *deps))[0]
+
+
+def slot(offset):
+    return (offset & 1) * 2 + (offset >> 1)
 
 
 def one_hot(rows, cols, row_offset=0, col_offset=0):
@@ -677,10 +684,9 @@
     return jnp.where(row == col, 1.0, 0.0).astype(BF16)
 
 
-def fetch_kernel(
-    sizes, idx, attend_ref, small_ref, expand_ref, shrink_ref, mixer_ref, first_ref, feed_ref
-):
+def fetch_kernel(sizes, idx, attend_ref, expand_ref, shrink_ref, mixer_ref, *refs):
     uly, dp, group, unit = sizes
+    vec_refs, (first_ref, feed_ref) = refs[:-2], refs[-2:]
     share = attend_ref.shape[1]
     shard, width = mixer_ref.shape
     u = idx[1]
@@ -690,18 +696,23 @@
         cols = dot_nn(attend_ref[0, :, c * width : (c + 1) * width], take)
         first_ref[:share, c * group : (c + 1) * group] = cols.astype(BF16)
     first_ref[share:, :] = jnp.zeros_like(first_ref[share:, :])
-    first_ref[share:, :shard] = small_ref[...]
+    rows = share // dp
+    mixer = dot_nn(one_hot(rows, shard, part * rows, 0), mixer_ref[...]).astype(BF16)
+    for k in range(dp):
+        here = slice(k * rows, (k + 1) * rows)
+        first_ref[here, 3 * group :] = mixer[:, k * group : (k + 1) * group]
+    line = share
+    for ref in vec_refs:
+        for k in range(ref.shape[0] // shard):
+            first_ref[line : line + 1, :shard] = ref[k * shard : (k + 1) * shard].reshape(1, shard)
+            line += 1
     take = one_hot(width, unit, 0, part * unit)
     half = shard // 2
     for k in range(dp):
         cols = dot_nn(expand_ref[:, k * width : (k + 1) * width], take).astype(BF16)
         feed_ref[:half, k * unit : (k + 1) * unit] = cols[:half]
         feed_ref[:half, (dp + k) * unit : (dp + k + 1) * unit] = cols[half:]
-    feed_ref[half : half + unit, :] = shrink_ref[0]
-    rows = feed_ref.shape[0] - half - unit
-    feed_ref[half + unit :, :] = dot_nn(
-        one_hot(rows, shard, part * rows, 0), mixer_ref[...]
-    ).astype(BF16)
+    feed_ref[half:, :] = shrink_ref[0]
 
 
 def project_kernel(sizes, idx, *refs):
@@ -709,7 +720,7 @@
     x_refs, refs = refs[:uly], refs[uly:]
     mine_refs, refs = refs[:dp], refs[dp:]
     other_refs, refs = refs[:dp], refs[dp:]
-    w_ref, q_ref, kv_ref, vec_ref, eb_ref = refs
+    w_ref, q_ref, kv_ref, vec_ref, eb_ref, mixer_ref = refs
     b, u, z, length = idx[0], idx[1], idx[2], idx[3]
     rows, width = x_refs[0].shape
     wide = q_ref.shape[1]
@@ -717,11 +728,16 @@
     share = mine_refs[0].shape[0] - 16
     shard = 2 * share
     parts = uly * blk
-    w_ref[:, group:wide] = jnp.zeros((width, pad), BF16)
-    w_ref[:, wide + group : 2 * wide] = jnp.zeros((width, pad), BF16)
+    for c in range(3):
+        w_ref[:, c * wide + group : (c + 1) * wide] = jnp.zeros((width, pad), BF16)
     own_vec = jnp.zeros((16, shard), F32)
     all_vec = jnp.zeros((16, width), F32)
+    lines = share // dp
     for j in range(dp):
+        for k in range(dp):
+            mixer_ref[j * lines : (j + 1) * lines, k * group : (k + 1) * group] = mine_refs[j][
+                k * lines : (k + 1) * lines, 3 * group :
+            ]
         for ref, core in ((mine_refs[j], b), (other_refs[j], 1 - b)):
             start = pl.multiple_of((z ^ j) * shard + core * share, share)
             for c in range(3):
@@ -751,7 +767,7 @@
     mark = jnp.where(lane == group, 1.0, 0.0)
     zeros = jnp.zeros((1, pad), F32)
     q_bias = jnp.concatenate([own_vec[0:1], zeros], 1)
-    v_bias = own_vec[1:2]
+    v_bias = jnp.concatenate([own_vec[1:2], zeros], 1)
     for j in range(uly):
         x = x_refs[j][...]
         here = slice(j * rows, (j + 1) * rows)
@@ -819,7 +835,7 @@
         out_shape=[jax.ShapeDtypeStruct((tile, group), BF16)] * pieces
         + [jax.ShapeDtypeStruct((8, rows), F32)],
         scratch_shapes=[pltpu.VMEM((group, keys), BF16)],
-        compiler_params=pltpu.CompilerParams(vmem_limit_bytes=48 * 2**20),
+        compiler_params=pltpu.CompilerParams(vmem_limit_bytes=16 * 2**20),
         cost_estimate=pl.CostEstimate(
             flops=4 * heads * rows * keys * wide,
             transcendentals=heads * rows * keys,
@@ -849,245 +865,305 @@
     inverse_ref[...] = inverse
 
 
-def load_parts(expand_refs, shrink_refs, e_ref, s_ref, e_sem, s_sem, act):
-    unit = s_ref.shape[2]
-    for p in range(len(expand_refs)):
-        act(pltpu.make_async_copy(expand_refs[p], e_ref.at[p], e_sem.at[p]), p)
-        act(
-            pltpu.make_async_copy(shrink_refs[p].at[:, pl.ds(0, unit), :], s_ref.at[p], s_sem.at[p]),
-            p,
-        )
-
-
-def feed_forward_kernel(parts, idx, x1_ref, x1b_ref, eb_ref, vec_ref, cot_ref, *refs):
-    expand_refs, refs = refs[:parts], refs[parts:]
-    shrink_refs, refs = refs[:parts], refs[parts:]
-    mixed_ref, dh_ref, dhb_ref, slope_ref, keep_ref, send_ref, grads_ref, *refs = refs
-    act_ref, acc_ref, low_ref, e_ref, s_ref, e_sem, s_sem = refs
-    phase = pl.program_id(0)
-    step = pl.program_id(1)
+def rest_kernel(sizes, idx, expand_ref, shrink_ref, out_ref):
+    uly, dp, unit = sizes
+    width = shrink_ref.shape[1]
+    half = expand_ref.shape[0] // 2
+    for j in range(1, uly):
+        part = idx[0] * uly + (idx[1] ^ j)
+        take = one_hot(width, unit, 0, part * unit)
+        for k in range(dp):
+            cols = dot_nn(expand_ref[:, k * width : (k + 1) * width], take).astype(BF16)
+            out_ref[j - 1, :half, k * unit : (k + 1) * unit] = cols[:half]
+            out_ref[j - 1, :half, (dp + k) * unit : (dp + k + 1) * unit] = cols[half:]
+        start = pl.multiple_of(part * unit, unit)
+        out_ref[j - 1, half:, :] = shrink_ref[pl.ds(start, unit), :]
+
+
+def mixer_kernel(sizes, idx, *refs):
+    uly, dp = sizes
+    pieces, (m_ref, turn_ref) = refs[:-2], refs[-2:]
+    lines = pieces[0].shape[0] // dp
+    b, u, z = idx[0], idx[1], idx[2]
+    shard = 2 * uly * lines
+    for k in range(dp):
+        for p, ref in enumerate(pieces):
+            part = (b * uly + u) ^ p
+            turn_ref[pl.ds(pl.multiple_of(part * lines, 8), lines), :] = ref[
+                k * lines : (k + 1) * lines, :
+            ].astype(F32)
+        start = pl.multiple_of((z ^ k) * shard, shard)
+        m_ref[pl.ds(start, shard), :] = turn_ref[...].astype(BF16)
+
+
+def load_parts(pieces, z, e_ref, s_ref, sem, act, only=None):
     dp, unit, width = s_ref.shape[1:]
-    z = idx[2]
-
-    @pl.when((phase == 0) & (step == 0))
+    shard = width // dp
+    half = shard // 2
+    block = dp * unit
+    for j, row in enumerate(pieces):
+        if only is not None and j != only:
+            continue
+        for k, piece in enumerate(row):
+            for h in range(2):
+                start = pl.multiple_of((z ^ k) * shard + h * half, half)
+                act(
+                    pltpu.make_async_copy(
+                        piece.at[pl.ds(0, half), pl.ds(h * block, block)],
+                        e_ref.at[j, pl.ds(start, half), :],
+                        sem.at[j, 3 * k + h],
+                    )
+                )
+            act(
+                pltpu.make_async_copy(
+                    piece.at[pl.ds(half, unit), :], s_ref.at[j, z ^ k], sem.at[j, 3 * k + 2]
+                )
+            )
+
+
+def by_part(uly, dp, refs):
+    own, rest, *far = refs
+    return [
+        [own if j == 0 else rest.at[j - 1]] + [far[(k - 1) * uly + j] for k in range(1, dp)]
+        for j in range(uly)
+    ]
+
+
+def weights_ready(pieces, z, e_ref, s_ref, sem):
+    step = pl.program_id(0)
+
+    @pl.when(step == 0)
     def _():
-        load_parts(
-            expand_refs, shrink_refs, e_ref, s_ref, e_sem, s_sem, lambda copy, p: copy.start()
-        )
-
-    @pl.when(phase == 0)
+        load_parts(pieces, z, e_ref, s_ref, sem, lambda copy: copy.start())
+
+    for j in range(len(pieces)):
+
+        @pl.when(step == j)
+        def _(j=j):
+            load_parts(pieces, z, e_ref, s_ref, sem, lambda copy: copy.wait(), j)
+
+
+def feed_forward_kernel(uly, idx, mine_ref, other_ref, eb_ref, *refs):
+    act_ref, slope_ref, y_ref, send_ref, acc_ref, x_ref, e_ref, s_ref, sem = refs[-9:]
+    step = pl.program_id(0)
+    dp, unit, width = s_ref.shape[1:]
+    rows = mine_ref.shape[0]
+    weights_ready(by_part(uly, dp, refs[:-9]), idx[2], e_ref, s_ref, sem)
+
+    @pl.when(step == 0)
     def _():
-        def wait(copy, p):
-            @pl.when(step == p)
-            def _():
-                copy.wait()
-
-        load_parts(expand_refs, shrink_refs, e_ref, s_ref, e_sem, s_sem, wait)
-        pre = dot_nn(x1b_ref[...], e_ref[step]) + eb_ref[pl.ds(step, 1), :]
-        cdf = 0.5 * (1.0 + lax.erf(pre * 0.7071067811865476))
-        pdf = jnp.exp(-0.5 * pre * pre) * 0.3989422804014327
-        act = (pre * cdf).astype(BF16)
-        act_ref[step] = act
-        slope_ref[0] = (cdf + pre * pdf).astype(BF16)
-        part = dot_nn(act, s_ref[step].reshape(dp * unit, width))
-
-        @pl.when(step == 0)
-        def _():
-            acc_ref[...] = part
-
-        @pl.when(step > 0)
-        def _():
-            acc_ref[...] += part
-
-        @pl.when(step == parts - 1)
-        def _():
-            hidden = x1_ref[...] + (acc_ref[...] + vec_ref[5:6, :])
-            gain = vec_ref[6:7, :]
-            center = hidden - jnp.mean(hidden, -1, keepdims=True)
-            inverse = lax.rsqrt(jnp.mean(center * center, -1, keepdims=True) + EPSILON)
-            normed = center * inverse
-            mixed_ref[...] = (normed * gain + vec_ref[7:8, :]).astype(BF16)
-            grad = cot_ref[...].astype(F32)
-            scaled = grad * gain
-            dhidden = inverse * (
-                scaled
-                - jnp.mean(scaled, -1, keepdims=True)
-                - normed * jnp.mean(scaled * normed, -1, keepdims=True)
-            )
-            dh_ref[...] = dhidden
-            low_ref[...] = dhidden.astype(BF16)
-            dhb_ref[...] = dhidden.astype(BF16)
-            grads_ref[...] = jnp.zeros_like(grads_ref)
-            grads_ref[0:1, :] = jnp.sum(dhidden, 0, keepdims=True)
-            grads_ref[1:2, :] = jnp.sum(grad * normed, 0, keepdims=True)
-            grads_ref[2:3, :] = jnp.sum(grad, 0, keepdims=True)
-
-    @pl.when(phase == 1)
+        x_ref[:rows] = mine_ref[...]
+        x_ref[rows:] = other_ref[...]
+        acc_ref[...] = jnp.zeros_like(acc_ref)
+
+    pre = dot_nn(x_ref[...], e_ref[step]) + eb_ref[pl.ds(step, 1), :]
+    cdf = 0.5 * (1.0 + lax.erf(pre * 0.7071067811865476))
+    pdf = jnp.exp(-0.5 * pre * pre) * 0.3989422804014327
+    act = (pre * cdf).astype(BF16)
+    act_ref[0] = act
+    slope_ref[0] = (cdf + pre * pdf).astype(BF16)
+    acc_ref[...] += dot_nn(act, s_ref[step].reshape(dp * unit, width))
+
+    @pl.when(step == uly - 1)
     def _():
-        dshrink = dot_tn(act_ref[step], low_ref[...]).astype(BF16)
-
-        def store(ref):
-            for k in range(dp):
-                start = pl.multiple_of((z ^ k) * unit, unit)
-                ref[0, pl.ds(start, unit), :] = dshrink[k * unit : (k + 1) * unit]
-
-        @pl.when(step < parts // 2)
-        def _():
-            store(keep_ref)
-
-        @pl.when(step >= parts // 2)
-        def _():
-            store(send_ref)
-
-
-def feed_forward(scalars, x1, x1b, eb, vec, cot, expand, shrink):
-    rows, width = x1.shape
-    parts = len(expand)
-    block = expand[0].shape[1]
-    dp = shrink[0].shape[0]
-    unit = block // dp
-    half = parts // 2
+        y_ref[...] = acc_ref[:rows]
+        send_ref[...] = acc_ref[rows:].astype(BF16)
+
+
+def weight_scratch(uly, dp, unit, width):
+    return [
+        pltpu.VMEM((uly, width, dp * unit), BF16),
+        pltpu.VMEM((uly, dp, unit, width), BF16),
+        pltpu.SemaphoreType.DMA((uly, 3 * dp)),
+    ]
+
+
+def feed_forward(scalars, sizes, mine, other, eb, weights):
+    uly, dp, unit = sizes
+    rows, width = mine.shape
+    block = dp * unit
     hbm = pl.BlockSpec(memory_space=pl.ANY)
-    grad = (1, block, width)
     return call(
-        functools.partial(feed_forward_kernel, parts),
+        functools.partial(feed_forward_kernel, uly),
         "feed_forward",
         scalars,
-        [x1, x1b, eb, vec, cot, *expand, *shrink],
-        [whole(x1.shape), whole(x1.shape), whole(eb.shape), whole(vec.shape), whole(cot.shape)]
-        + [hbm] * (2 * parts),
+        [mine, other, eb, *weights],
+        [whole(mine.shape), whole(mine.shape), whole(eb.shape)] + [hbm] * len(weights),
         [
-            jax.ShapeDtypeStruct((rows, width), BF16),
+            jax.ShapeDtypeStruct((uly, 2 * rows, block), BF16),
+            jax.ShapeDtypeStruct((uly, 2 * rows, block), BF16),
             jax.ShapeDtypeStruct((rows, width), F32),
             jax.ShapeDtypeStruct((rows, width), BF16),
-            jax.ShapeDtypeStruct((parts, rows, block), BF16),
-            jax.ShapeDtypeStruct((half, block, width), BF16),
-            jax.ShapeDtypeStruct((half, block, width), BF16),
-            jax.ShapeDtypeStruct((8, width), F32),
         ],
         [
+            pl.BlockSpec((1, 2 * rows, block), lambda k, _: (k, 0, 0)),
+            pl.BlockSpec((1, 2 * rows, block), lambda k, _: (k, 0, 0)),
             whole((rows, width)),
             whole((rows, width)),
+        ],
+        [pltpu.VMEM((2 * rows, width), F32), pltpu.VMEM((2 * rows, width), BF16)]
+        + weight_scratch(uly, dp, unit, width),
+        (uly,),
+        8 * rows * width * uly * block,
+        16,
+    )
+
+
+def final_norm_kernel(idx, x1_ref, y_ref, got_ref, vec_ref, cot_ref, *refs):
+    mixed_ref, dh_ref, low_ref, sums_ref = refs
+    hidden = x1_ref[...] + (y_ref[...] + got_ref[...].astype(F32) + vec_ref[5:6, :])
+    gain = vec_ref[6:7, :]
+    center = hidden - jnp.mean(hidden, -1, keepdims=True)
+    inverse = lax.rsqrt(jnp.mean(center * center, -1, keepdims=True) + EPSILON)
+    normed = center * inverse
+    mixed_ref[...] = (normed * gain + vec_ref[7:8, :]).astype(BF16)
+    grad = cot_ref[...].astype(F32)
+    scaled = grad * gain
+    dhidden = inverse * (
+        scaled
+        - jnp.mean(scaled, -1, keepdims=True)
+        - normed * jnp.mean(scaled * normed, -1, keepdims=True)
+    )
+    dh_ref[...] = dhidden
+    low_ref[...] = dhidden.astype(BF16)
+    sums_ref[...] = jnp.zeros_like(sums_ref)
+    sums_ref[0:1, :] = jnp.sum(dhidden, 0, keepdims=True)
+    sums_ref[1:2, :] = jnp.sum(grad * normed, 0, keepdims=True)
+    sums_ref[2:3, :] = jnp.sum(grad, 0, keepdims=True)
+
+
+def store_halves(step, uly, value, z, dp, near_x, far_x, near_y, far_y):
+    rows = value.shape[0] // dp
+    place = [pl.multiple_of(((z ^ k) >> 1) * rows, rows) for k in range(dp)]
+    for odd, near, far, close in (
+        (0, near_x, far_x, step % 2 == 0),
+        (1, near_y, far_y, step < uly // 2),
+    ):
+        for ref, wanted in ((near, close), (far, jnp.logical_not(close))):
+            for k in range(dp):
+
+                @pl.when(wanted & (((z ^ k) & 1) == odd))
+                def _(ref=ref, k=k):
+                    ref[0, pl.ds(place[k], rows), :] = value[k * rows : (k + 1) * rows]
+
+
+def half_specs(uly, rows, cols):
+    shape = jax.ShapeDtypeStruct((uly // 2, rows, cols), BF16)
+    block = (1, rows, cols)
+    return [shape] * 4, [
+        pl.BlockSpec(block, lambda k, _: (k // 2, 0, 0)),
+        pl.BlockSpec(block, lambda k, _: (k // 2, 0, 0)),
+        pl.BlockSpec(block, lambda k, _: (jnp.minimum(k, 1), 0, 0)),
+        pl.BlockSpec(block, lambda k, _: (jnp.maximum(k - 2, 0), 0, 0)),
+    ]
+
+
+def shrink_grad_kernel(sizes, idx, d_mine, d_other, act_ref, *refs):
+    uly, dp = sizes
+    out_refs, d_ref = refs[:-1], refs[-1]
+    step = pl.program_id(0)
+    rows = d_mine.shape[0]
+
+    @pl.when(step == 0)
+    def _():
+        d_ref[:rows] = d_mine[...]
+        d_ref[rows:] = d_other[...]
+
+    value = dot_tn(act_ref[0], d_ref[...]).astype(BF16)
+    store_halves(step, uly, value, idx[2], dp, *out_refs)
+
+
+def shrink_grad(scalars, sizes, ds, act):
+    uly, dp, unit = sizes
+    rows, width = ds[0].shape
+    block = dp * unit
+    shapes, specs = half_specs(uly, block // 2, width)
+    return call(
+        functools.partial(shrink_grad_kernel, (uly, dp)),
+        "shrink_grad",
+        scalars,
+        [*ds, act],
+        [whole((rows, width))] * 2 + [pl.BlockSpec((1, 2 * rows, block), lambda k, _: (k, 0, 0))],
+        shapes,
+        specs,
+        [pltpu.VMEM((2 * rows, width), BF16)],
+        (uly,),
+        4 * rows * width * uly * block,
+        16,
+    )
+
+
+def feed_backward_kernel(uly, idx, x_mine, x_other, d_mine, d_other, slope_ref, *refs):
+    half_refs, (deb_ref, dx_ref, send_ref) = refs[-14:-10], refs[-10:-7]
+    acc_ref, xt_ref, d_ref, turn_ref, e_ref, s_ref, sem = refs[-7:]
+    step = pl.program_id(0)
+    dp, unit, width = s_ref.shape[1:]
+    rows = x_mine.shape[0]
+    weights_ready(by_part(uly, dp, refs[:-14]), idx[2], e_ref, s_ref, sem)
+
+    @pl.when(step == 0)
+    def _():
+        xt_ref[:, :rows] = x_mine[...].T
+        xt_ref[:, rows:] = x_other[...].T
+        d_ref[:rows] = d_mine[...]
+        d_ref[rows:] = d_other[...]
+        acc_ref[...] = jnp.zeros_like(acc_ref)
+
+    dpre = dot_nt(d_ref[...], s_ref[step].reshape(dp * unit, width))
+    dpre = (dpre * slope_ref[0].astype(F32)).astype(BF16)
+    deb_ref[0] = jnp.sum(dpre.astype(F32), 0, keepdims=True)
+    dexpand = dot_nn(xt_ref[...], dpre).astype(BF16)
+    store_halves(step, uly, dexpand, idx[2], dp, *half_refs)
+    acc_ref[...] += dot_nt(dpre, e_ref[step])
+
+    @pl.when(step == uly - 1)
+    def _():
+        dx_ref[...] = acc_ref[:rows]
+        send_ref[...] = acc_ref[rows:].astype(BF16)
+
+
+def feed_backward(scalars, sizes, xs, ds, slope, weights):
+    uly, dp, unit = sizes
+    rows, width = xs[0].shape
+    block = dp * unit
+    hbm = pl.BlockSpec(memory_space=pl.ANY)
+    shapes, specs = half_specs(uly, width // 2, block)
+    return call(
+        functools.partial(feed_backward_kernel, uly),
+        "feed_backward",
+        scalars,
+        [*xs, *ds, slope, *weights],
+        [whole((rows, width))] * 4
+        + [pl.BlockSpec((1, 2 * rows, block), lambda k, _: (k, 0, 0))]
+        + [hbm] * len(weights),
+        shapes
+        + [
+            jax.ShapeDtypeStruct((uly, 1, block), F32),
+            jax.ShapeDtypeStruct((rows, width), F32),
+            jax.ShapeDtypeStruct((rows, width), BF16),
+        ],
+        specs
+        + [
+            pl.BlockSpec((1, 1, block), lambda k, _: (k, 0, 0)),
             whole((rows, width)),
-            pl.BlockSpec((1, rows, block), lambda p, k, _: (k * (1 - p) + (parts - 1) * p, 0, 0)),
-            pl.BlockSpec(grad, lambda p, k, _: (jnp.minimum(k, half - 1) * p, 0, 0)),
-            pl.BlockSpec(grad, lambda p, k, _: (jnp.maximum(k - half, 0) * p, 0, 0)),
-            whole((8, width)),
+            whole((rows, width)),
         ],
         [
-            pltpu.VMEM((parts, rows, block), BF16),
-            pltpu.VMEM((rows, width), F32),
-            pltpu.VMEM((rows, width), BF16),
-            pltpu.VMEM((parts, width, block), BF16),
-            pltpu.VMEM((parts, dp, unit, width), BF16),
-            pltpu.SemaphoreType.DMA((parts,)),
-            pltpu.SemaphoreType.DMA((parts,)),
-        ],
-        (2, parts),
-        6 * rows * width * parts * block,
-        48,
-    )
-
-
-def feed_backward_kernel(parts, idx, x1b_ref, dh_ref, dhb_ref, slope_ref, *refs):
-    expand_refs, refs = refs[:parts], refs[parts:]
-    shrink_refs, refs = refs[:parts], refs[parts:]
-    dx_ref, keep_ref, send_ref, deb_ref, *refs = refs
-    x1t_ref, acc_ref, e_ref, s_ref, e_sem, s_sem = refs
-    step = pl.program_id(0)
-    dp, unit, width = s_ref.shape[1:]
-    shard = width // dp
-    z = idx[2]
-
-    @pl.when(step == 0)
-    def _():
-        load_parts(
-            expand_refs, shrink_refs, e_ref, s_ref, e_sem, s_sem, lambda copy, p: copy.start()
-        )
-        for k in range(dp):
-            start = pl.multiple_of((z ^ k) * shard, shard)
-            x1t_ref[pl.ds(start, shard), :] = x1b_ref[...].T[k * shard : (k + 1) * shard]
-
-    def wait(copy, p):
-        @pl.when(step == p)
-        def _():
-            copy.wait()
-
-    load_parts(expand_refs, shrink_refs, e_ref, s_ref, e_sem, s_sem, wait)
-    dpre = dot_nt(dhb_ref[...], s_ref[step].reshape(dp * unit, width))
-    dpre = (dpre * slope_ref[0].astype(F32)).astype(BF16)
-    deb_ref[0] = jnp.sum(dpre.astype(F32), 0, keepdims=True)
-    dexpand = dot_nn(x1t_ref[...], dpre).astype(BF16)
-
-    @pl.when(step < parts // 2)
-    def _():
-        keep_ref[0] = dexpand
-
-    @pl.when(step >= parts // 2)
-    def _():
-        send_ref[0] = dexpand
-
-    part = dot_nt(dpre, e_ref[step])
-
-    @pl.when(step == 0)
-    def _():
-        acc_ref[...] = dh_ref[...] + part
-
-    @pl.when(step > 0)
-    def _():
-        acc_ref[...] += part
-
-    @pl.when(step == parts - 1)
-    def _():
-        dx_ref[...] = acc_ref[...]
-
-
-def feed_backward(scalars, x1b, dh, dhb, slope, expand, shrink):
-    rows, width = dh.shape
-    parts = len(expand)
-    block = expand[0].shape[1]
-    dp = shrink[0].shape[0]
-    unit = block // dp
-    half = parts // 2
-    hbm = pl.BlockSpec(memory_space=pl.ANY)
-    grad = (1, width, block)
-    return call(
-        functools.partial(feed_backward_kernel, parts),
-        "feed_backward",
-        scalars,
-        [x1b, dh, dhb, slope, *expand, *shrink],
-        [whole(x1b.shape), whole(dh.shape), whole(dhb.shape)]
-        + [pl.BlockSpec((1, rows, block), lambda k, _: (k, 0, 0))]
-        + [hbm] * (2 * parts),
-        [
-            jax.ShapeDtypeStruct((rows, width), F32),
-            jax.ShapeDtypeStruct((half, width, block), BF16),
-            jax.ShapeDtypeStruct((half, width, block), BF16),
-            jax.ShapeDtypeStruct((parts, 1, block), F32),
-        ],
-        [
-            whole((rows, width)),
-            pl.BlockSpec(grad, lambda k, _: (jnp.minimum(k, half - 1), 0, 0)),
-            pl.BlockSpec(grad, lambda k, _: (jnp.maximum(k - half, 0), 0, 0)),
-            pl.BlockSpec((1, 1, block), lambda k, _: (k, 0, 0)),
-        ],
-        [
-            pltpu.VMEM((width, rows), BF16),
-            pltpu.VMEM((rows, width), F32),
-            pltpu.VMEM((parts, width, block), BF16),
-            pltpu.VMEM((parts, dp, unit, width), BF16),
-            pltpu.SemaphoreType.DMA((parts,)),
-            pltpu.SemaphoreType.DMA((parts,)),
-        ],
-        (parts,),
-        6 * rows * width * parts * block,
-        48,
-    )
-
-
-def norm_backward_kernel(sizes, idx, dx_ref, normed_ref, inverse_ref, m_ref, vec_ref, *refs):
+            pltpu.VMEM((2 * rows, width), F32),
+            pltpu.VMEM((width, 2 * rows), BF16),
+            pltpu.VMEM((2 * rows, width), BF16),
+            pltpu.VMEM((16, 128), BF16),
+        ]
+        + weight_scratch(uly, dp, unit, width),
+        (uly,),
+        12 * rows * width * uly * block,
+        16,
+    )
+
+
+def norm_backward_kernel(sizes, idx, dh2_ref, dx_ref, got_ref, normed_ref, inverse_ref, *refs):
     uly, dp, unit = sizes
-    grads_ref, deb_ref, *refs = refs
+    m_ref, vec_ref, grads_ref, deb_ref, *refs = refs
     o_refs, refs = refs[:uly], refs[uly:]
     dh_ref, *refs = refs
     do_refs, refs = refs[:uly], refs[uly:]
@@ -1096,8 +1172,8 @@
     group = o_refs[0].shape[1]
     share = group // 2
     width = dx_ref.shape[1]
-    parts = deb_ref.shape[0]
-    grad = dx_ref[...]
+    parts = 2 * uly
+    grad = dh2_ref[...] + dx_ref[...] + got_ref[...].astype(F32)
     normed = normed_ref[...]
     scaled = grad * vec_ref[3:4, :]
     dhidden = inverse_ref[...] * (
@@ -1123,14 +1199,13 @@
     for k, value in enumerate(values):
         lines = jnp.where(line == k, value, lines)
     lines = lines.astype(BF16)
-    part = b * uly + u
-    owner = lax.broadcasted_iota(jnp.int32, (parts, parts), 1) ^ part
-    order = lax.broadcasted_iota(jnp.int32, (parts, parts), 0)
+    owner = (lax.broadcasted_iota(jnp.int32, (parts, uly), 1) ^ u) + b * uly
+    order = lax.broadcasted_iota(jnp.int32, (parts, uly), 0)
     order = jnp.where(order == owner, 1.0, 0.0).astype(BF16)
     ebs = dot_nn(order, deb_ref[...].astype(BF16)).astype(BF16)
     for j in range(uly):
         turn_ref[...] = dot_tn(o_refs[j][...], low).astype(BF16)
-        place = u ^ j ^ z
+        place = slot(u ^ j ^ z)
         keep_ref[place, :share] = turn_ref[pl.ds(pl.multiple_of(b * share, share), share), :]
         send_ref[place, :share] = turn_ref[pl.ds(pl.multiple_of((1 - b) * share, share), share), :]
     for k in range(dp):
@@ -1138,15 +1213,16 @@
         own = dot_nn(lines, one_hot(width, group, 0, shard)).astype(BF16)
         ebk = dot_nn(ebs, one_hot(dp * unit, unit, 0, (z ^ k) * unit)).astype(BF16)
         for ref in (keep_ref, send_ref):
-            ref[k, share:, :] = jnp.zeros_like(ref[k, share:, :])
-            ref[k, share : share + 8, :group] = own
-            ref[k, share + 8 : share + 16, :unit] = ebk
-
-
-def attend_grad_kernel(heads, blocks, pieces, q_ref, lse_ref, *refs):
+            ref[slot(k), share:, :] = jnp.zeros_like(ref[slot(k), share:, :])
+            ref[slot(k), share : share + 8, :group] = own
+            ref[slot(k), share + 8 : share + 16, :unit] = ebk
+
+
+def attend_grad_kernel(heads, blocks, pieces, started, q_ref, lse_ref, *refs):
     do_refs, refs = refs[:pieces], refs[pieces:]
     o_refs, refs = refs[:pieces], refs[pieces:]
     kv_refs, refs = refs[:blocks], refs[blocks:]
+    so_far, refs = refs[: blocks * started], refs[blocks * started :]
     dq_ref, *refs = refs
     dkv_refs, refs = refs[:blocks], refs[blocks:]
     kt_ref, dout_ref, prod_ref, *refs = refs
@@ -1159,8 +1235,12 @@
     def _():
         for i in range(blocks):
             kt_ref[:, i * rows : (i + 1) * rows] = kv_refs[i][:, :group].T
-            dk_accs[i][...] = jnp.zeros_like(dk_accs[i])
-            dv_accs[i][...] = jnp.zeros_like(dv_accs[i])
+            if started:
+                dk_accs[i][...] = so_far[i][:, :wide].astype(F32) * LOG2E
+                dv_accs[i][...] = so_far[i][:, wide : wide + group].astype(F32)
+            else:
+                dk_accs[i][...] = jnp.zeros_like(dk_accs[i])
+                dv_accs[i][...] = jnp.zeros_like(dv_accs[i])
 
     for j in range(pieces):
 
@@ -1197,27 +1277,29 @@
             dkv_refs[i][:, :group] = (dk_accs[i][:, :group] * LN2).astype(BF16)
             dkv_refs[i][:, group:wide] = jnp.zeros((rows, wide - group), BF16)
             dkv_refs[i][:, wide : wide + group] = dv_accs[i][...].astype(BF16)
-
-
-def attend_grad(q, kvs, douts, outs, lse, heads):
-    rows, wide = q.shape
+            dkv_refs[i][:, wide + group :] = jnp.zeros((rows, wide - group), BF16)
+
+
+def attend_grad(q, kvs, douts, outs, lse, heads, at, so_far):
+    rows, wide = kvs[0].shape[0], q.shape[1]
     group = heads * HD
     blocks = len(kvs)
     pieces = len(douts)
-    tile = rows // pieces
+    tile = douts[0].shape[0]
     keys = blocks * rows
+    started = 1 if so_far else 0
     out = pl.pallas_call(
-        functools.partial(attend_grad_kernel, heads, blocks, pieces),
+        functools.partial(attend_grad_kernel, heads, blocks, pieces, started),
         grid=(pieces,),
         in_specs=[
-            pl.BlockSpec((tile, wide), lambda t: (t, 0)),
-            pl.BlockSpec((8, tile), lambda t: (0, t)),
+            pl.BlockSpec((tile, wide), lambda t: (t + at, 0)),
+            pl.BlockSpec((8, tile), lambda t: (0, t + at)),
         ]
         + [whole((tile, group))] * (2 * pieces)
-        + [whole(kvs[0].shape)] * blocks,
+        + [whole(kvs[0].shape)] * (blocks + blocks * started),
         out_specs=[pl.BlockSpec((tile, group), lambda t: (t, 0))]
         + [whole(kvs[0].shape)] * blocks,
-        out_shape=[jax.ShapeDtypeStruct((rows, group), BF16)]
+        out_shape=[jax.ShapeDtypeStruct((pieces * tile, group), BF16)]
         + [jax.ShapeDtypeStruct(kvs[0].shape, BF16)] * blocks,
         scratch_shapes=[
             pltpu.VMEM((group, keys), BF16),
@@ -1226,26 +1308,29 @@
         ]
         + [pltpu.VMEM((rows, wide), F32)] * blocks
         + [pltpu.VMEM((rows, group), F32)] * blocks,
-        compiler_params=pltpu.CompilerParams(vmem_limit_bytes=48 * 2**20),
+        compiler_params=pltpu.CompilerParams(vmem_limit_bytes=16 * 2**20),
         cost_estimate=pl.CostEstimate(
-            flops=10 * heads * rows * keys * wide,
-            transcendentals=heads * rows * keys,
+            flops=10 * heads * pieces * tile * keys * wide,
+            transcendentals=heads * pieces * tile * keys,
             bytes_accessed=2 * rows * wide * 4 + 4 * keys * (wide + group),
         ),
         name="attend_grad",
-    )(q, lse, *douts, *outs, *kvs)
+    )(q, lse, *douts, *outs, *kvs, *so_far)
     return out[0], out[1:]
 
 
-def project_grad_kernel(sizes, idx, dq_ref, own_ref, got_ref, *refs):
+def project_grad_kernel(sizes, idx, *refs):
     uly, dp, group = sizes
+    dq_refs, (own_ref, got_ref, *refs) = refs[:uly], refs[uly:]
     x_refs, refs = refs[:uly], refs[uly:]
     dproj_ref, keep_ref, send_ref = refs
     b, z = idx[0], idx[2]
     rows, width = x_refs[0].shape
-    wide = own_ref.shape[1] - group
+    wide = own_ref.shape[1] // 2
     share = keep_ref.shape[1] - 16
-    dproj_ref[:, :group] = dq_ref[...] * jnp.asarray(0.125, BF16)
+    for k, ref in enumerate(dq_refs):
+        here = slice(k * ref.shape[0], (k + 1) * ref.shape[0])
+        dproj_ref[here, :group] = ref[...] * jnp.asarray(0.125, BF16)
     dproj_ref[:, group:wide] = jnp.zeros((uly * rows, wide - group), BF16)
     dproj_ref[:, wide:] = (own_ref[...].astype(F32) + got_ref[...].astype(F32)).astype(BF16)
     sums = jnp.sum(dproj_ref[...].astype(F32), 0, keepdims=True).astype(BF16)
@@ -1264,7 +1349,7 @@
 
                     @pl.when((b == core) == mine)
                     def _(start=start, s=s, ref=ref, lanes=lanes, into=into):
-                        ref[s ^ z, :share, into] = grad[start : start + share, lanes]
+                        ref[slot(s ^ z), :share, into] = grad[start : start + share, lanes]
 
                 ref[s, share:, into] = jnp.broadcast_to(sums[:, lanes], (16, group))
 
@@ -1278,28 +1363,35 @@
         out_refs[j][...] = part.astype(out_refs[j].dtype)
 
 
-def finish_feed_kernel(sizes, idx, *refs):
+def finish_shrink_kernel(idx, *refs):
+    pieces, out_ref = refs[:-1], refs[-1]
+    for p, ref in enumerate(pieces):
+
+        @pl.when(pl.program_id(0) == p)
+        def _(ref=ref):
+            out_ref[...] = ref[...].astype(F32)
+
+
+def finish_expand_kernel(sizes, idx, *refs):
     uly, dp, unit = sizes
-    pieces, (expand_ref, shrink_ref) = refs[:-2], refs[-2:]
-    shard = expand_ref.shape[0]
-    width = shrink_ref.shape[1]
-    half = shard // 2
+    pieces, (out_ref, turn_ref) = refs[:-2], refs[-2:]
+    width = turn_ref.shape[0]
     part = idx[0] * uly + idx[1]
-    outs = [None] * dp
-    for p, ref in enumerate(pieces):
-        start = pl.multiple_of((part ^ p) * unit, unit)
-        shrink_ref[pl.ds(start, unit), :] = ref[half:, :].astype(F32)
-        put = one_hot(unit, width, (part ^ p) * unit, 0)
-        for k in range(dp):
-            for h in range(2):
-                lanes = slice((h * dp + k) * unit, (h * dp + k + 1) * unit)
-                value = dot_nn(ref[:half, lanes], put)
-                rows = slice(h * half, (h + 1) * half)
-                cols = slice(k * width, (k + 1) * width)
-                if p == 0:
-                    expand_ref[rows, cols] = value
-                else:
-                    expand_ref[rows, cols] += value
+    step = pl.program_id(0)
+
+    @pl.when(step == 0)
+    def _():
+        col = lax.broadcasted_iota(jnp.int32, (width, width), 1)
+        row = lax.broadcasted_iota(jnp.int32, (width, width), 0)
+        source = col + ((col // unit) ^ part) * unit - (col // unit) * unit
+        turn_ref[...] = jnp.where(row == source, 1.0, 0.0).astype(BF16)
+
+    for k in range(dp):
+
+        @pl.when(step == k)
+        def _(k=k):
+            line = jnp.concatenate([ref[:, k * unit : (k + 1) * unit] for ref in pieces], 1)
+            out_ref[...] = dot_nn(line, turn_ref[...])
 
 
 def finish_attend_kernel(uly, idx, *refs):
@@ -1358,100 +1450,120 @@
     parts = blk * uly
     unit = hidden // (parts * dp)
     share = shard // blk
-    if not (blk == 2 and uly == 4 and shard == group and unit * 2 == shard and share % 16 == 0):
+    if not (blk == 2 and uly == 4 and dp == 4 and shard == group and unit * 2 == shard and share % 16 == 0):
         return general_device(*args)
     u = lax.axis_index("uly")
     b = lax.axis_index("blk")
     z = lax.axis_index("dp")
-    mixer_rows = shard // parts
-    feed_rows = shard // 2 + unit + mixer_rows
+    mixer_rows = share // dp
+    feed_rows = shard // 2 + unit
     block_rows = uly * rows
-    cols = 2 * wide + group
+    cols = 3 * wide
 
     x = tokens.reshape(rows, width)
-    xs = [x] + [swap_with(x, "uly", j) for j in range(1, uly)]
+    xs = [x, swap_with(x, "uly", 1), swap_with(x, "uly", 2)]
+    xs.append(swap_with(after(x, *xs[1:]), "uly", 3))
     scalars = jnp.stack([b, u, z, lengths[0]]).astype(jnp.int32)
-    small = jnp.stack(
-        [query_bias, value_bias, mixer_bias, attn_gain, attn_shift, shrink_bias]
-        + [final_gain, final_shift]
-        + [expand_bias[k * shard : (k + 1) * shard] for k in range(hidden // dp // shard)]
-        + [jnp.zeros_like(query_bias)] * (8 - hidden // dp // shard)
-    )
+    vectors = [query_bias, value_bias, mixer_bias, attn_gain, attn_shift, shrink_bias]
+    vectors += [final_gain, final_shift, expand_bias]
     first, feed = call(
         functools.partial(fetch_kernel, (uly, dp, group, unit)),
         "fetch",
         scalars,
         [
             attend_weight.reshape(blk, share, 3 * width),
-            small,
             expand_weight,
             shrink_weight.reshape(parts, unit, width),
             mixer_weight,
+            *vectors,
         ],
         [
             pl.BlockSpec((1, share, 3 * width), lambda t, s: (s[0], 0, 0)),
-            whole(small.shape),
             whole(expand_weight.shape),
             pl.BlockSpec((1, unit, width), lambda t, s: (s[0] * uly + s[1], 0, 0)),
             whole(mixer_weight.shape),
+            *[whole(vector.shape) for vector in vectors],
         ],
         [
-            jax.ShapeDtypeStruct((share + 16, 3 * group), BF16),
+            jax.ShapeDtypeStruct((share + 16, width), BF16),
             jax.ShapeDtypeStruct((feed_rows, width), BF16),
         ],
-        [whole((share + 16, 3 * group)), whole((feed_rows, width))],
+        [whole((share + 16, width)), whole((feed_rows, width))],
         [],
         (1,),
         10**9,
-        32,
-    )
-    mine = [first] + [swap_with(first, "dp", j) for j in range(1, dp)]
+        58,
+    )
+    feeds = [None, swap_with(feed, "dp", 1)]
+    mine = [first, None, swap_with(first, "dp", 2), swap_with(first, "dp", 3)]
+    mine[1] = swap_with(after(first, *xs[1:3]), "dp", 1)
+    feeds.append(swap_with(after(feed, *mine[1:]), "dp", 2))
     other = [swap_with(piece, "blk", 1) for piece in mine]
-
-    feed_all = lax.all_gather(feed, "dp", axis=0, tiled=False)
-    half = shard // 2
-    halves = feed_all[:, :half].reshape(dp, half, 2, dp * unit).transpose(0, 2, 1, 3)
-    expand = [halves.reshape(width, dp * unit)]
-    shrink = [feed_all[:, half:]]
-    expand.append(swap_with(expand[0], "uly", 1))
-    shrink_y = swap_with(shrink[0], "uly", 2)
-    expand.append(swap_with(expand[0], "uly", 2))
-    shrink.append(swap_with(shrink[0], "uly", 1))
-    expand.append(swap_with(expand[1], "uly", 2))
-    shrink += [shrink_y, swap_with(shrink_y, "uly", 1)]
-    expand += [swap_with(piece, "blk", 1) for piece in expand]
-    shrink += [swap_with(piece, "blk", 1) for piece in shrink]
-    mixer_all = jnp.stack(xor_order([piece[:, unit:] for piece in shrink], b * uly + u), 1)
-    mixer_all = mixer_all.reshape(width, width)
-
-    w_own, q, kv, vec, eb = call(
+    rest = call(
+        functools.partial(rest_kernel, (uly, dp, unit)),
+        "fetch_rest",
+        scalars,
+        [expand_weight, shrink_weight],
+        [whole(expand_weight.shape), whole(shrink_weight.shape)],
+        jax.ShapeDtypeStruct((uly - 1, shard // 2 + unit, width), BF16),
+        whole((uly - 1, shard // 2 + unit, width)),
+        [],
+        (1,),
+        10**9,
+        16,
+    )
+
+    w_own, q, kv, vec, eb, mixer_mine = call(
         functools.partial(project_kernel, (uly, blk, dp, group, unit)),
         "project",
         scalars,
-        [*xs, *mine, *other],
+        [*after(xs, feeds[1]), *mine, *other],
         [whole((rows, width))] * uly + [whole(first.shape)] * (2 * dp),
         [
             jax.ShapeDtypeStruct((width, cols), BF16),
             jax.ShapeDtypeStruct((block_rows, wide), BF16),
-            jax.ShapeDtypeStruct((block_rows, wide + group), BF16),
+            jax.ShapeDtypeStruct((block_rows, 2 * wide), BF16),
             jax.ShapeDtypeStruct((16, width), F32),
             jax.ShapeDtypeStruct((parts, dp * unit), F32),
+            jax.ShapeDtypeStruct((dp * mixer_rows, width), BF16),
         ],
         [
             whole((width, cols)),
             whole((block_rows, wide)),
-            whole((block_rows, wide + group)),
+            whole((block_rows, 2 * wide)),
             whole((16, width)),
             whole((parts, dp * unit)),
+            whole((dp * mixer_rows, width)),
         ],
         [],
         (1,),
         2 * block_rows * width * cols,
-        48,
+        16,
     )
     kvs = [kv, swap_with(kv, "blk", 1)]
-    outs, lse = attend(q, kvs, heads, uly)
-    o_cols = [outs[0]] + [swap_with(outs[j], "uly", j) for j in range(1, uly)]
+
+    mixer_plane = [swap_with(mixer_mine, "uly", j) for j in range(1, uly)]
+    plane_one = [swap_with(feeds[1], "uly", j) for j in range(1, uly)]
+    outs, lse = attend(after(q, rest, *mixer_plane), kvs, heads, uly)
+    o_cols = after(outs, *plane_one)
+    o_cols = [o_cols[0]] + [swap_with(o_cols[j], "uly", j) for j in range(1, uly)]
+    feeds.append(swap_with(after(feed, feeds[2], *plane_one), "dp", 3))
+    plane_two = [swap_with(after(feeds[2], *o_cols[1:]), "uly", j) for j in range(1, uly)]
+    mixer_parts = [mixer_mine, *mixer_plane]
+    mixer_parts += [swap_with(piece, "blk", 1) for piece in mixer_parts]
+    mixer_all = call(
+        functools.partial(mixer_kernel, (uly, dp)),
+        "mixer_weight",
+        scalars,
+        mixer_parts,
+        [whole(mixer_mine.shape)] * parts,
+        jax.ShapeDtypeStruct((width, width), BF16),
+        whole((width, width)),
+        [pltpu.VMEM((shard, width), F32)],
+        (1,),
+        10**6,
+        16,
+    )
 
     square = (rows, width)
     x1, x1b, normed, inverse = call(
@@ -1470,22 +1582,51 @@
         [],
         (1,),
         2 * rows * width * width,
-        32,
-    )
-    mixed, dh2, dh2b, slope, s_keep, s_send, sums2 = feed_forward(
-        scalars, x1, x1b, eb, vec, cotangent.reshape(square), expand, shrink
-    )
-    s_got = swap_with(s_send, "blk", 1)
-    dx1, e_keep, e_send, deb = feed_backward(scalars, x1b, dh2, dh2b, slope, expand, shrink)
-    e_got = swap_with(e_send, "blk", 1)
+        16,
+    )
+    sizes = (uly, dp, unit)
+    plane_three = [swap_with(after(feeds[3], *plane_two), "uly", j) for j in range(1, uly)]
+    far = [feeds[1], *plane_one, feeds[2], *plane_two, feeds[3], *plane_three]
+    weights = [feed, rest, *far]
+    x1b_other = swap_with(x1b, "blk", 1)
+    act, slope, y_own, y_send = feed_forward(scalars, sizes, x1b, x1b_other, eb, weights)
+    mixed, dh2, dh2b, sums2 = call(
+        final_norm_kernel,
+        "final_norm",
+        scalars,
+        [x1, y_own, swap_with(y_send, "blk", 1), vec, cotangent.reshape(square)],
+        [whole(square)] * 3 + [whole(vec.shape), whole(square)],
+        [
+            jax.ShapeDtypeStruct(square, BF16),
+            jax.ShapeDtypeStruct(square, F32),
+            jax.ShapeDtypeStruct(square, BF16),
+            jax.ShapeDtypeStruct((8, width), F32),
+        ],
+        [whole(square)] * 3 + [whole((8, width))],
+        [],
+        (1,),
+        10**6,
+        16,
+    )
+    dh2b_other = swap_with(dh2b, "blk", 1)
+    ds = [dh2b, dh2b_other]
+    s_near_x, s_far_x, s_near_y, s_far_y = shrink_grad(scalars, sizes, ds, act)
+    s_x = swap_with(s_far_x, "uly", 1)
+    s_y = swap_with(s_far_y, "uly", 2)
+    e_near_x, e_far_x, e_near_y, e_far_y, deb, dx_own, dx_send = feed_backward(
+        scalars, sizes, [x1b, x1b_other], after(ds, s_far_x), slope, weights
+    )
     block = (dp, share + 16, width)
-    dh1, *rest = call(
-        functools.partial(norm_backward_kernel, (uly, dp, unit)),
+    dh1, *rest_out = call(
+        functools.partial(norm_backward_kernel, sizes),
         "norm_backward",
         scalars,
-        [dx1, normed, inverse, mixer_all, vec, sums2, deb.reshape(parts, dp * unit), *o_cols],
-        [whole(square), whole(square), whole((rows, 1)), whole((width, width))]
-        + [whole(vec.shape), whole(sums2.shape), whole((parts, dp * unit))]
+        [dh2, dx_own, swap_with(after(dx_send, s_x, s_y), "blk", 1), normed, inverse, mixer_all]
+        + [vec, sums2]
+        + [deb.reshape(uly, dp * unit), *o_cols],
+        [whole(square)] * 4
+        + [whole((rows, 1)), whole((width, width)), whole(vec.shape), whole(sums2.shape)]
+        + [whole((uly, dp * unit))]
         + [whole((rows, group))] * uly,
         [jax.ShapeDtypeStruct(square, F32)]
         + [jax.ShapeDtypeStruct((rows, group), BF16)] * uly
@@ -1494,68 +1635,67 @@
         [pltpu.VMEM((group, width), BF16)],
         (1,),
         4 * rows * width * width,
-        48,
-    )
-    douts = [rest[0]] + [swap_with(rest[j], "uly", j) for j in range(1, uly)]
-    m_keep, m_send = rest[uly:]
-    m_got = swap_with(m_send, "blk", 1)
-    dq, dkvs = attend_grad(q, kvs, douts, outs, lse, heads)
+        16,
+    )
+    douts = [rest_out[0]] + [swap_with(rest_out[j], "uly", j) for j in range(1, uly)]
+    m_keep, m_send = rest_out[uly:]
 
     def add(*values):
         return total(values).astype(BF16)
 
-    s_y = swap_with(add(s_keep[2:], s_got[2:]), "uly", 2)
-    s_x = swap_with(add(s_keep[1], s_got[1], s_y[1]), "uly", 1)
-    e_x = swap_with(
-        jnp.stack([add(e_keep[1], e_got[1]), add(e_keep[3], e_got[3])]), "uly", 1
-    )
-    e_y = swap_with(add(e_keep[2], e_got[2], e_x[1]), "uly", 2)
-
-    def feed_piece(j):
-        at = slice(j * unit, (j + 1) * unit)
-        low = [slice(j * shard + h * half, j * shard + (h + 1) * half) for h in range(2)]
-        sides = [add(e_keep[0, r], e_got[0, r], e_x[0, r], e_y[r]) for r in low]
-        bottom = add(s_keep[0, at], s_got[0, at], s_y[0, at], s_x[at])
-        return jnp.concatenate([jnp.concatenate(sides, 1), bottom], 0)
-
-    def over_dp(pieces):
-        return add(pieces[0], *[swap_with(pieces[j], "dp", j) for j in range(1, dp)])
-
-    owned = over_dp([feed_piece(j) for j in range(dp)])
-    plane = [owned] + [swap_with(owned, "uly", j) for j in range(1, uly)]
-    plane += [swap_with(piece, "blk", 1) for piece in plane]
-    expand_out, shrink_out = call(
-        functools.partial(finish_feed_kernel, (uly, dp, unit)),
-        "finish_feed",
-        scalars,
-        plane,
-        [whole(owned.shape)] * parts,
-        [
-            jax.ShapeDtypeStruct((shard, hidden), F32),
-            jax.ShapeDtypeStruct((hidden // dp, width), F32),
-        ],
-        [whole((shard, hidden)), whole((hidden // dp, width))],
-        [],
-        (1,),
-        10**9,
-        48,
-    )
-
-    m_own = over_dp([add(m_keep[j], m_got[j]) for j in range(dp)])
-    m_all = [m_own] + [swap_with(m_own, "uly", j) for j in range(1, uly)]
-    m_all = [value.astype(F32) for value in m_all]
-    m_all = (m_all[0] + m_all[1]) + (m_all[2] + m_all[3])
-    m_half = m_all[:share].astype(BF16)
-    mixer_out = jnp.concatenate(xor_order([m_half, swap_with(m_half, "blk", 1)], b), 0)
-    vecs = [m_all[share + k, :shard] for k in range(6)]
-    eb_out = m_all[share + 8 : share + 8 + parts, :unit].reshape(-1)
-
+    def quarter(j, so_far, *deps):
+        dout = after(douts[j], *deps)
+        return attend_grad(q, kvs, [dout], [outs[j]], lse, heads, j, so_far)
+
+    s_near_x, s_near_y, m_send = after((s_near_x, s_near_y, m_send), dh1)
+    s_next_x = add(s_near_x[1], s_x[1])
+    s_next_y = add(s_near_y[1], s_y[1])
+    s_xy = swap_with(after(s_next_x, *douts[1:]), "uly", 2)
+    s_yx = swap_with(after(s_next_y, *douts[1:]), "uly", 1)
+    m_got = swap_with(after(m_send, *douts[1:]), "blk", 1)
+    dq_0, dkvs = quarter(0, [], s_next_x, s_next_y, *douts[1:])
+
+    s_xy, s_yx, m_got, e_far_x, e_far_y = after((s_xy, s_yx, m_got, e_far_x, e_far_y), dq_0)
+    pair = (2, unit, width)
+    s_near = add(s_near_x[0], s_x[0], s_xy).reshape(pair)
+    s_far = add(s_near_y[0], s_y[0], s_yx).reshape(pair)
+    m_near, m_far = add(m_keep[:2], m_got[:2]), add(m_keep[2:], m_got[2:])
+    e_x = swap_with(e_far_x, "uly", 1)
+    e_y = swap_with(e_far_y, "uly", 2)
+    s_one = swap_with(s_far, "dp", 1)
+    m_one = swap_with(m_far, "dp", 1)
+    dq_1, dkvs = quarter(1, dkvs, s_near, s_far, m_near, m_far)
+
+    dq_2, dkvs = quarter(2, dkvs)
+
+    e_x, e_y, s_one, m_one = after((e_x, e_y, s_one, m_one), dq_2)
+    e_next_x = add(e_near_x[1], e_x[1])
+    e_next_y = add(e_near_y[1], e_y[1])
+    e_xy = swap_with(e_next_x, "uly", 2)
+    e_yx = swap_with(e_next_y, "uly", 1)
+    s_next = add(s_near[1], s_one[1])
+    m_next = add(m_near[1], m_one[1])
+    s_two = swap_with(s_next, "dp", 2)
+    m_two = swap_with(m_next, "dp", 2)
+    dq_3, dkvs = quarter(3, dkvs, e_next_x, e_next_y, s_next, m_next)
+
+    dkv_got = swap_with(after(dkvs[1], e_xy, e_yx, s_two, m_two), "blk", 1)
+    e_xy, e_yx, s_two, m_two = after((e_xy, e_yx, s_two, m_two), dq_3)
+    pair = (2, shard, dp * unit)
+    e_near = add(e_near_x[0], e_x[0], e_xy).reshape(pair)
+    e_far = add(e_near_y[0], e_y[0], e_yx).reshape(pair)
+    e_one = swap_with(e_far, "dp", 1)
+    s_own = add(s_near[0], s_one[0], s_two)
+    m_own = add(m_near[0], m_one[0], m_two)
+    s_plane = [s_own] + [swap_with(s_own, "uly", j) for j in range(1, uly)]
+    dkv_got = after(dkv_got, e_near, e_far, s_own, m_own)
+    dqs = [dq_0, dq_1, dq_2, dq_3]
     dproj, a_keep, a_send = call(
         functools.partial(project_grad_kernel, (uly, dp, group)),
         "project_grad",
         scalars,
-        [dq, dkvs[0], swap_with(dkvs[1], "blk", 1), *xs],
-        [whole(dq.shape), whole(kv.shape), whole(kv.shape)] + [whole(square)] * uly,
+        [*dqs, dkvs[0], dkv_got, *xs],
+        [whole(dq_0.shape)] * uly + [whole(kv.shape)] * 2 + [whole(square)] * uly,
         [
             jax.ShapeDtypeStruct((block_rows, cols), BF16),
             jax.ShapeDtypeStruct((dp, share + 16, 3 * group), BF16),
@@ -1565,9 +1705,10 @@
         [],
         (1,),
         2 * block_rows * width * cols,
-        48,
-    )
-    a_got = swap_with(a_send, "blk", 1)
+        16,
+    )
+    a_got = swap_with(after(a_send, *s_plane), "blk", 1)
+    m_plane = [m_own] + [swap_with(after(m_own, *s_plane, dproj), "uly", j) for j in range(1, uly)]
     token_parts = call(
         functools.partial(token_grad_kernel, uly),
         "token_grad",
@@ -1579,27 +1720,78 @@
         [],
         (1,),
         2 * block_rows * width * cols,
-        48,
-    )
-    tokens_grad = total(
-        [token_parts[0]] + [swap_with(token_parts[j], "uly", j) for j in range(1, uly)]
-    )
-    a_own = over_dp([add(a_keep[j], a_got[j]) for j in range(dp)])
-    a_mine = [a_own] + [swap_with(a_own, "uly", j) for j in range(1, uly)]
-    a_other = [swap_with(piece, "blk", 1) for piece in a_mine]
+        16,
+    )
+
+    def in_plane(own, *deps):
+        own = after(own, *deps)
+        return [own] + [swap_with(own, "uly", j) for j in range(1, uly)]
+
+    def both_cores(pieces, *deps):
+        return pieces + [swap_with(after(piece, *deps), "blk", 1) for piece in pieces]
+
+    a_got, e_one = after((a_got, e_one), token_parts[0])
+    a_near, a_far = add(a_keep[:2], a_got[:2]), add(a_keep[2:], a_got[2:])
+    a_one = swap_with(a_far, "dp", 1)
+    e_next = add(e_near[1], e_one[1])
+    e_two = swap_with(e_next, "dp", 2)
+    token_parts = after(token_parts, a_near, a_far, e_next, *m_plane)
+    token_got = [swap_with(token_parts[j], "uly", j) for j in range(1, uly)]
+    a_next = add(a_near[1], a_one[1])
+    a_two = swap_with(a_next, "dp", 2)
+    s_plane = both_cores(s_plane, a_near)
+    shrink_out = call(
+        finish_shrink_kernel,
+        "finish_shrink",
+        scalars,
+        s_plane,
+        [whole(s_own.shape)] * parts,
+        jax.ShapeDtypeStruct((hidden // dp, width), F32),
+        pl.BlockSpec((unit, width), lambda t, s: ((s[0] * uly + s[1]) ^ t, 0)),
+        [],
+        (parts,),
+        10**6,
+        16,
+    )
+    e_own = add(e_near[0], e_one[0], e_two)
+    e_plane = in_plane(e_own, shrink_out, *token_got)
+    tokens_grad = total([token_parts[0], *token_got])
+    a_own = add(a_near[0], a_one[0], a_two)
+    a_plane = in_plane(a_own, *token_got)
+    e_plane = both_cores(e_plane)
+    expand_out = call(
+        functools.partial(finish_expand_kernel, sizes),
+        "finish_expand",
+        scalars,
+        e_plane,
+        [whole(e_own.shape)] * parts,
+        jax.ShapeDtypeStruct((shard, hidden), F32),
+        pl.BlockSpec((shard, width), lambda t, s: (0, t)),
+        [pltpu.VMEM((width, width), BF16)],
+        (dp,),
+        10**9,
+        16,
+    )
+    a_plane = both_cores(a_plane, expand_out)
     attend_out, biases = call(
         functools.partial(finish_attend_kernel, uly),
         "finish_attend",
         scalars,
-        [*a_mine, *a_other],
-        [whole(a_own.shape)] * (2 * uly),
+        a_plane,
+        [whole(a_own.shape)] * parts,
         [jax.ShapeDtypeStruct((shard, 3 * width), F32), jax.ShapeDtypeStruct((8, 3 * group), F32)],
         [whole((shard, 3 * width)), whole((8, 3 * group))],
         [],
         (1,),
         10**9,
-        48,
-    )
+        16,
+    )
+    m_all = [value.astype(F32) for value in m_plane]
+    m_all = (m_all[0] + m_all[1]) + (m_all[2] + m_all[3])
+    m_half = m_all[:share].astype(BF16)
+    mixer_out = jnp.concatenate(xor_order([m_half, swap_with(m_half, "blk", 1)], b), 0)
+    vecs = [m_all[share + k, :shard] for k in range(6)]
+    eb_out = m_all[share + 8 : share + 8 + parts, :unit].reshape(-1)
     return (
         mixed.reshape(tokens.shape),
         tokens_grad.reshape(tokens.shape),

time: 399 us -> 284 us (0.71)
  waiting for transfers between devices: 163 us -> 88.2 us
  local copies, waits for them, and re-layouts: 32.5 us -> 10.7 us
  other arithmetic: 28.6 us -> 11.7 us
  between operations: 15.2 us -> 2.38 us
  starting transfers between devices: 65.9 us -> 73.8 us
    ppermute x70 -> x87, waiting for transfers between devices: 130 us -> 88.2 us  [swap_with(): return lax.ppermute(value, axis, [(i, i ^ offset) for i in range(size)])]
    all_gather x1 -> x0, waiting for transfers between devices: 33.8 us -> none  [on_device(): feed_all = lax.all_gather(feed, 'dp', axis=0, tiled=False)]
    convert_element_type x12 -> x17, other arithmetic: 19.4 us -> 8.06 us  [add(): return total(values).astype(BF16)]
    ppermute x70 -> x87, starting transfers between devices: 65.8 us -> 73.8 us  [swap_with(): return lax.ppermute(value, axis, [(i, i ^ offset) for i in range(size)])]
    unnamed x61 -> x81, local copies, waits for them, and re-layouts: 14.8 us -> 8.17 us
    another operation x15 -> x0, local copies, waits for them, and re-layouts: 5.42 us -> none  [the longest x14 5.34 us: on_device(): jnp.stack([query_bias, value_bias, mixer_bias, attn_gain, attn_shift, shr...]
    slice x3 -> x0, local copies, waits for them, and re-layouts: 4.06 us -> none  [the longest x1 2.06 us: on_device(): shrink = [feed_all[:, half:]]]
    pallas_call x10 -> x15, Pallas kernels: 57.6 us -> 59 us  [call(): pl.pallas_call(kernel, grid_spec=pltpu.PrefetchScalarGridSpec(num_scalar_...]
  transfers between devices with their start and end apart: 71 -> 87, of which waited for: 22 -> 37; matrix products, arithmetic and copies ran while one was open for 10% -> 4% of each run, Pallas kernels for 13% -> 25%
where the time goes in v3:
time: 284 us; the launch traced here: 278 us
  Pallas kernels  91.4 us (32%)
  waiting for transfers between devices  88.2 us (31%)
  starting transfers between devices  73.8 us (26%)
  other arithmetic  11.7 us (4%)
  local copies, waits for them, and re-layouts  10.7 us (4%)
    ppermute x87, waiting for transfers between devices, swap_with(): return lax.ppermute(value, axis, [(i, i ^ offset) for i in range(size)])  88.2 us
    ppermute x87, starting transfers between devices, swap_with(): return lax.ppermute(value, axis, [(i, i ^ offset) for i in range(size)])  73.8 us
    pallas_call x15, Pallas kernels, call(): pl.pallas_call(kernel, grid_spec=pltpu.PrefetchScalarGridSpec(num_scalar_...  59 us
    pallas_call x4, Pallas kernels, attend_grad(): pl.pallas_call(functools.partial(attend_grad_kernel, heads, blocks, piece...  20.5 us
    pallas_call x1, Pallas kernels, attend(): pl.pallas_call(functools.partial(attend_kernel, heads, blocks), grid=(pie...  11.9 us
    unnamed x81, local copies, waits for them, and re-layouts  8.17 us
    convert_element_type x17, other arithmetic, add(): return total(values).astype(BF16)  8.06 us
  transfers between devices with their start and end apart: 87, of which 37 were waited for; matrix products, arithmetic and copies ran while one was open for 4% of the time, Pallas kernels for 25%

profile of v3, /device:TPU:0, one launch (start us, length us, event | category | flops | bytes accessed | tf_op | source)
XLA Modules:
  0.0 278.1 jit_solution(8397228790288340864)
XLA Ops:
  0.6 3.0 %collective-permute-start.1 = (bf16[256,768]{1,0:T(8,128)(2,1)}, bf16[256,768]{1,0:T(8,128)(2,1)S(1)}, u32[]{:S(2)}, u32[]{:S(2)}) collective-permute-start(bf16[256,768]{1,0:T(8,128)(2,1)} %bitcast.71), channel_id=1, source_target_pairs={{0,2},{1,3},{2,0},{3,1},{4,6},{5,7},{6,4},{7,5},{8,10},{9,11},{10,... | collective-permute-start | bytes 1179656 | tf_op jit(solution)/shard_map/ppermute | solution.py:35
  6.4 3.8 %fetch.1 = (bf16[112,768]{1,0:T(8,128)(2,1)}, bf16[192,768]{1,0:T(8,128)(2,1)}) custom-call(s32[4]{0:T(128)} %pad_add_fusion.idx, bf16[2,96,2304]{2,1,0:T(8,128)(2,1)} %bitcast.90, bf16[192,3072]{1,0:T(8,128)(2,1)} %expand_ref.3, bf16[8,96,768]{2,1,0:T(8,128)(2,1)} %bitcast.79, bf16[192,768]{1,0:T(8,128)(2,1)} %mixer_ref.1, bf16[192]{0:T(256)(128)(2,1)} %refs_0_.1, ...), custom_call_target="tpu_custom_call" | custom-call | flops 1000000000 | bytes 1 | tf_op jit(solution)/shard_map/fetch/pallas_call | solution.py:653
  15.9 3.6 %collective-permute-start.6 = (bf16[112,768]{1,0:T(8,128)(2,1)}, bf16[112,768]{1,0:T(8,128)(2,1)S(1)}, u32[]{:S(2)}, u32[]{:S(2)}) collective-permute-start(bf16[112,768]{1,0:T(8,128)(2,1)} %get-tuple-element.146.refs_4_), channel_id=1, source_target_pairs={{0,24},{8,16},{16,8},{24,0},{1,25},{9,17},{17,9},{25,1},{2,26},{10... | collective-permute-start | bytes 516104 | tf_op jit(solution)/shard_map/ppermute | solution.py:35
  20.3 5.7 %collective-permute-done.6.refs_7_ = bf16[112,768]{1,0:T(8,128)(2,1)S(1)} collective-permute-done((bf16[112,768]{1,0:T(8,128)(2,1)}, bf16[112,768]{1,0:T(8,128)(2,1)S(1)}, u32[]{:S(2)}, u32[]{:S(2)}) %collective-permute-start.6) | collective-permute-done | bytes 172064 | tf_op jit(solution)/shard_map/ppermute | solution.py:35
  26.0 7.0 %collective-permute-done.5.refs_6_ = bf16[112,768]{1,0:T(8,128)(2,1)S(1)} collective-permute-done((bf16[112,768]{1,0:T(8,128)(2,1)}, bf16[112,768]{1,0:T(8,128)(2,1)S(1)}, u32[]{:S(2)}, u32[]{:S(2)}) %collective-permute-start.5) | collective-permute-done | bytes 172064 | tf_op jit(solution)/shard_map/ppermute | solution.py:35
  35.9 2.7 project.1
  50.4 11.9 %attend.1 = (bf16[256,192]{1,0:T(8,128)(2,1)S(1)}, bf16[256,192]{1,0:T(8,128)(2,1)S(1)}, bf16[256,192]{1,0:T(8,128)(2,1)S(1)}, bf16[256,192]{1,0:T(8,128)(2,1)S(1)}, f32[8,1024]{1,0:T(8,128)S(1)}) custom-call(bf16[1024,256]{1,0:T(8,128)(2,1)S(1)} %get-tuple-element.149.q_ref, bf16[1024,512]{1,0:T(8,128)(2,1)S(1)} %get-tuple-element.150.refs_0_.refs_2_, ...), custom_call_target="tpu_custom_call" | custom-call | flops 6442450944 | bytes 3407872 | tf_op jit(solution)/shard_map/attend/pallas_call | solution.py:830
  69.4 4.7 %collective-permute-done.19.refs_2_.refs_6_ = bf16[256,192]{1,0:T(8,128)(2,1)S(1)} collective-permute-done((bf16[256,192]{1,0:T(8,128)(2,1)S(1)}, bf16[256,192]{1,0:T(8,128)(2,1)S(1)}, u32[]{:S(2)}, u32[]{:S(2)}) %collective-permute-start.19) | collective-permute-done | bytes 98336 | tf_op jit(solution)/shard_map/ppermute | solution.py:35
  82.7 2.4 collective-permute-done.29.refs_9_
  85.1 4.3 %collective-permute-done.28.refs_8_ = bf16[192,768]{1,0:T(8,128)(2,1)S(1)} collective-permute-done((bf16[192,768]{1,0:T(8,128)(2,1)S(1)}, bf16[192,768]{1,0:T(8,128)(2,1)S(1)}, u32[]{:S(2)}, u32[]{:S(2)}) %collective-permute-start.28) | collective-permute-done | bytes 294944 | tf_op jit(solution)/shard_map/ppermute | solution.py:35
  92.9 7.3 %collective-permute-done.33.refs_13_ = bf16[192,768]{1,0:T(8,128)(2,1)S(1)} collective-permute-done((bf16[192,768]{1,0:T(8,128)(2,1)S(1)}, bf16[192,768]{1,0:T(8,128)(2,1)S(1)}, u32[]{:S(2)}, u32[]{:S(2)}) %collective-permute-start.33) | collective-permute-done | bytes 294944 | tf_op jit(solution)/shard_map/ppermute | solution.py:35
  100.2 5.3 %collective-permute-done.32.refs_12_ = bf16[192,768]{1,0:T(8,128)(2,1)S(1)} collective-permute-done((bf16[192,768]{1,0:T(8,128)(2,1)S(1)}, bf16[192,768]{1,0:T(8,128)(2,1)S(1)}, u32[]{:S(2)}, u32[]{:S(2)}) %collective-permute-start.32) | collective-permute-done | bytes 294944 | tf_op jit(solution)/shard_map/ppermute | solution.py:35
  105.6 10.0 %feed_forward.1 = (bf16[4,512,384]{2,1,0:T(8,128)(2,1)S(1)}, bf16[4,512,384]{2,1,0:T(8,128)(2,1)S(1)}, f32[256,768]{1,0:T(8,128)S(1)}, bf16[256,768]{1,0:T(8,128)(2,1)S(1)}) custom-call(s32[4]{0:T(128)S(1)} %copy-done.2, bf16[256,768]{1,0:T(8,128)(2,1)S(1)} %get-tuple-element.161.mine_ref.x_mine, ...), custom_call_target="tpu_custom_call" | custom-call | flops 2415919104 | bytes 1 | tf_op jit(solution)/shard_map/feed_forward/pallas_call | solution.py:653
  121.0 3.3 %shrink_grad.1 = (bf16[2,192,768]{2,1,0:T(8,128)(2,1)S(1)}, bf16[2,192,768]{2,1,0:T(8,128)(2,1)S(1)}, bf16[2,192,768]{2,1,0:T(8,128)(2,1)S(1)}, bf16[2,192,768]{2,1,0:T(8,128)(2,1)S(1)}) custom-call(s32[4]{0:T(128)S(1)} %copy-done.2, bf16[256,768]{1,0:T(8,128)(2,1)S(1)} %get-tuple-element.175.d_mine, bf16[256,768]{1,0:T(8,128)(2,1)S(1)} %collective-permute-done.35.d_other, ...), custom_call_target="tpu_custom_call" | custom-call | flops 1207959552 | bytes 1 | tf_op jit(solution)/shard_map/shrink_grad/pallas_call | solution.py:653
  126.5 13.9 %feed_backward.1 = (bf16[2,384,384]{2,1,0:T(8,128)(2,1)S(1)}, bf16[2,384,384]{2,1,0:T(8,128)(2,1)S(1)}, bf16[2,384,384]{2,1,0:T(8,128)(2,1)S(1)}, bf16[2,384,384...) custom-call(s32[4]{0:T(128)S(1)} %copy-done.2, ...), custom_call_target="tpu_custom_call" | custom-call | flops 3623878656 | bytes 1 | tf_op jit(solution)/shard_map/feed_backward/pallas_call | solution.py:653
  142.3 2.3 norm_backward.1
  149.0 2.9 %collective-permute-done.39.refs_0_ = bf16[256,192]{1,0:T(8,128)(2,1)S(1)} collective-permute-done((bf16[256,192]{1,0:T(8,128)(2,1)S(1)}, bf16[256,192]{1,0:T(8,128)(2,1)S(1)}, u32[]{:S(2)}, u32[]{:S(2)}) %collective-permute-start.39) | collective-permute-done | bytes 98336 | tf_op jit(solution)/shard_map/ppermute | solution.py:35
  151.8 2.8 collective-permute-done.40.refs_0_
  156.7 5.1 %attend_grad.4 = (bf16[256,192]{1,0:T(8,128)(2,1)S(1)}, bf16[1024,512]{1,0:T(8,128)(2,1)S(1)}, bf16[1024,512]{1,0:T(8,128)(2,1)S(1)}) custom-call(bf16[1024,256]{1,0:T(8,128)(2,1)S(1)} %get-tuple-element.149.q_ref, f32[8,1024]{1,0:T(8,128)S(1)} %get-tuple-element.170.lse_ref, bf16[256,192]{1,0:T(8,128)(2,1)S(1)} %get-tuple-element.196.refs_0_, ...), custom_call_target="tpu_custom_call" | custom-call | flops 4026531840 | bytes 5767168 | tf_op jit(solution)/shard_map/attend_grad/pallas_call | solution.py:1291
  161.8 2.4 collective-permute-done.43
  169.3 5.1 %attend_grad.5 = (bf16[256,192]{1,0:T(8,128)(2,1)S(1)}, bf16[1024,512]{1,0:T(8,128)(2,1)S(1)}, bf16[1024,512]{1,0:T(8,128)(2,1)S(1)}) custom-call(bf16[1024,256]{1,0:T(8,128)(2,1)S(1)} %get-tuple-element.149.q_ref, f32[8,1024]{1,0:T(8,128)S(1)} %get-tuple-element.170.lse_ref, bf16[256,192]{1,0:T(8,128)(2,1)S(1)} %collective-permute-done.39.refs_0_, ...), custom_call_target="tpu_custom_call" | custom-call | flops 4026531840 | bytes 5767168 | tf_op jit(solution)/shard_map/attend_grad/pallas_call | solution.py:1291
  174.3 5.3 %attend_grad.6 = (bf16[256,192]{1,0:T(8,128)(2,1)S(1)}, bf16[1024,512]{1,0:T(8,128)(2,1)S(1)}, bf16[1024,512]{1,0:T(8,128)(2,1)S(1)}) custom-call(bf16[1024,256]{1,0:T(8,128)(2,1)S(1)} %get-tuple-element.149.q_ref, f32[8,1024]{1,0:T(8,128)S(1)} %get-tuple-element.170.lse_ref, bf16[256,192]{1,0:T(8,128)(2,1)S(1)} %collective-permute-done.40.refs_0_, ...), custom_call_target="tpu_custom_call" | custom-call | flops 4026531840 | bytes 5767168 | tf_op jit(solution)/shard_map/attend_grad/pallas_call | solution.py:1291
  187.6 5.1 %attend_grad.7 = (bf16[256,192]{1,0:T(8,128)(2,1)S(1)}, bf16[1024,512]{1,0:T(8,128)(2,1)S(1)}, bf16[1024,512]{1,0:T(8,128)(2,1)S(1)}) custom-call(bf16[1024,256]{1,0:T(8,128)(2,1)S(1)} %get-tuple-element.149.q_ref, f32[8,1024]{1,0:T(8,128)S(1)} %get-tuple-element.170.lse_ref, bf16[256,192]{1,0:T(8,128)(2,1)S(1)} %collective-permute-done.41.refs_0_, ...), custom_call_target="tpu_custom_call" | custom-call | flops 4026531840 | bytes 5767168 | tf_op jit(solution)/shard_map/attend_grad/pallas_call | solution.py:1291
  194.3 2.9 %collective-permute-done.52 = bf16[112,768]{1,0:T(8,128)(2,1)S(1)} collective-permute-done((bf16[112,768]{1,0:T(8,128)(2,1)S(1)}, bf16[112,768]{1,0:T(8,128)(2,1)S(1)}, u32[]{:S(2)}, u32[]{:S(2)}) %collective-permute-start.52) | collective-permute-done | bytes 172064 | tf_op jit(solution)/shard_map/ppermute | solution.py:35
  208.8 4.9 %project_grad.1 = (bf16[1024,768]{1,0:T(8,128)(2,1)S(1)}, bf16[4,112,576]{2,1,0:T(8,128)(2,1)S(1)}, bf16[4,112,576]{2,1,0:T(8,128)(2,1)S(1)}) custom-call(s32[4]{0:T(128)S(1)} %copy-done.2, bf16[256,192]{1,0:T(8,128)(2,1)S(1)} %get-tuple-element.197.refs_0_, bf16[256,192]{1,0:T(8,128)(2,1)S(1)} %get-tuple-element.210.refs_1_, ...), custom_call_target="tpu_custom_call" | custom-call | flops 1207959552 | bytes 1 | tf_op jit(solution)/shard_map/project_grad/pallas_call | solution.py:653
  219.4 2.6 collective-permute-done.61
  225.5 2.4 collective-permute-start.70
  233.1 3.7 %finish_shrink.1 = f32[768,768]{1,0:T(8,128)} custom-call(s32[4]{0:T(128)S(1)} %copy-done.2, bf16[96,768]{1,0:T(8,128)(2,1)S(1)} %fusion.13.refs_0_, bf16[96,768]{1,0:T(8,128)(2,1)S(1)} %collective-permute-done.54.refs_1_, bf16[96,768]{1,0:T(8,128)(2,1)S(1)} %collective-permute-done.55.refs_2_, bf16[96,768]{1,0:T(8,128)(2,1)S(1)} %collective-permute-done.56.refs_3_, ...), custom_call_target="tpu_custom_call" | custom-call | flops 1000000 | bytes 1 | tf_op jit(solution)/shard_map/finish_shrink/pallas_call | solution.py:653
  243.0 8.6 %collective-permute-done.63 = bf16[256,768]{1,0:T(8,128)(2,1)S(1)} collective-permute-done((bf16[256,768]{1,0:T(8,128)(2,1)S(1)}, bf16[256,768]{1,0:T(8,128)(2,1)S(1)}, u32[]{:S(2)}, u32[]{:S(2)}) %collective-permute-start.63) | collective-permute-done | bytes 393248 | tf_op jit(solution)/shard_map/ppermute | solution.py:35
  256.2 3.1 %collective-permute-done.77.refs_3_ = bf16[192,384]{1,0:T(8,128)(2,1)S(1)} collective-permute-done((bf16[192,384]{1,0:T(8,128)(2,1)S(1)}, bf16[192,384]{1,0:T(8,128)(2,1)S(1)}, u32[]{:S(2)}, u32[]{:S(2)}) %collective-permute-start.77) | collective-permute-done | bytes 147488 | tf_op jit(solution)/shard_map/ppermute | solution.py:35
  266.8 3.7 %finish_expand.1 = f32[192,3072]{1,0:T(8,128)} custom-call(s32[4]{0:T(128)S(1)} %copy-done.2, bf16[192,384]{1,0:T(8,128)(2,1)S(1)} %fusion.10.refs_0_, bf16[192,384]{1,0:T(8,128)(2,1)S(1)} %collective-permute-done.75.refs_1_, bf16[192,384]{1,0:T(8,128)(2,1)S(1)} %collective-permute-done.76.refs_2_, bf16[192,384]{1,0:T(8,128)(2,1)S(1)} %collective-permute-done.77.refs_3_, ...), custom_call_target="tpu_custom_call" | custom-call | flops 1000000000 | bytes 1 | tf_op jit(solution)/shard_map/finish_expand/pallas_call | solution.py:653
  274.2 2.9 %finish_attend.1 = (f32[192,2304]{1,0:T(8,128)}, f32[8,576]{1,0:T(8,128)S(1)}) custom-call(s32[4]{0:T(128)S(1)} %copy-done.2, bf16[112,576]{1,0:T(8,128)(2,1)S(1)} %fusion.15.refs_0_, bf16[112,576]{1,0:T(8,128)(2,1)S(1)} %collective-permute-done.67.refs_1_, bf16[112,576]{1,0:T(8,128)(2,1)S(1)} %collective-permute-done.68.refs_2_, ...), custom_call_target="tpu_custom_call" | custom-call | flops 1000000000 | bytes 1 | tf_op jit(solution)/shard_map/finish_attend/pallas_call | solution.py:653
  (270 shorter events, 121.0 us)
Async XLA Ops:
  0.6 12.4 %collective-permute-start.1 = (bf16[256,768]{1,0:T(8,128)(2,1)}, bf16[256,768]{1,0:T(8,128)(2,1)S(1)}, u32[]{:S(2)}, u32[]{:S(2)}) collective-permute-start(bf16[256,768]{1,0:T(8,128)(2,1)} %bitcast.71), channel_id=1, source_target_pairs={{0,2},{1,3},{2,0},{3,1},{4,6},{5,7},{6,4},{7,5},{8,10},{9,11},{10,... | collective-permute-start | bytes 1179656 | tf_op jit(solution)/shard_map/ppermute | solution.py:35
  10.3 22.8 %collective-permute-start.3 = (bf16[192,768]{1,0:T(8,128)(2,1)}, bf16[192,768]{1,0:T(8,128)(2,1)S(1)}, u32[]{:S(2)}, u32[]{:S(2)}) collective-permute-start(bf16[192,768]{1,0:T(8,128)(2,1)} %get-tuple-element.165.refs_0_), channel_id=1, source_target_pairs={{0,8},{8,0},{16,24},{24,16},{1,9},{9,1},{17,25},{25,17},{2,10},{10... | collective-permute-start | bytes 884744 | tf_op jit(solution)/shard_map/ppermute | solution.py:35
  14.5 19.1 %collective-permute-start.2 = (bf16[256,768]{1,0:T(8,128)(2,1)S(1)}, bf16[256,768]{1,0:T(8,128)(2,1)S(1)}, u32[]{:S(2)}, u32[]{:S(2)}) collective-permute-start(bf16[256,768]{1,0:T(8,128)(2,1)S(1)} %bitcast.73), channel_id=1, source_target_pairs={{0,3},{1,2},{2,1},{3,0},{4,7},{5,6},{6,5},{7,4},{8,11},{9,10},{10,... | collective-permute-start | bytes 1179656 | tf_op jit(solution)/shard_map/ppermute | solution.py:35
  19.5 13.5 %collective-permute-start.5 = (bf16[112,768]{1,0:T(8,128)(2,1)}, bf16[112,768]{1,0:T(8,128)(2,1)S(1)}, u32[]{:S(2)}, u32[]{:S(2)}) collective-permute-start(bf16[112,768]{1,0:T(8,128)(2,1)} %get-tuple-element.146.refs_4_), channel_id=1, source_target_pairs={{0,16},{8,24},{16,0},{24,8},{1,17},{9,25},{17,1},{25,9},{2,18},{10... | collective-permute-start | bytes 516104 | tf_op jit(solution)/shard_map/ppermute | solution.py:35
  19.5 14.0 %collective-permute-start.4 = (bf16[112,768]{1,0:T(8,128)(2,1)}, bf16[112,768]{1,0:T(8,128)(2,1)S(1)}, u32[]{:S(2)}, u32[]{:S(2)}) collective-permute-start(bf16[112,768]{1,0:T(8,128)(2,1)} %get-tuple-element.146.refs_4_), channel_id=1, source_target_pairs={{0,8},{8,0},{16,24},{24,16},{1,9},{9,1},{17,25},{25,17},{2,10},{10... | collective-permute-start | bytes 516104 | tf_op jit(solution)/shard_map/ppermute | solution.py:35
  44.2 18.1 %collective-permute-start.17 = (bf16[192,768]{1,0:T(8,128)(2,1)S(1)}, bf16[192,768]{1,0:T(8,128)(2,1)S(1)}, u32[]{:S(2)}, u32[]{:S(2)}) collective-permute-start(bf16[192,768]{1,0:T(8,128)(2,1)S(1)} %collective-permute-done.3.refs_2_), channel_id=1, source_target_pairs={{0,3},{1,2},{2,1},{3,0},{4,7},{5,6},{6,5},{7,4},{8,11},{9,10},{10,... | collective-permute-start | bytes 884744 | tf_op jit(solution)/shard_map/ppermute | solution.py:35
  46.6 15.7 %collective-permute-start.16 = (bf16[192,768]{1,0:T(8,128)(2,1)S(1)}, bf16[192,768]{1,0:T(8,128)(2,1)S(1)}, u32[]{:S(2)}, u32[]{:S(2)}) collective-permute-start(bf16[192,768]{1,0:T(8,128)(2,1)S(1)} %collective-permute-done.3.refs_2_), channel_id=1, source_target_pairs={{0,2},{1,3},{2,0},{3,1},{4,6},{5,7},{6,4},{7,5},{8,10},{9,11},{10,... | collective-permute-start | bytes 884744 | tf_op jit(solution)/shard_map/ppermute | solution.py:35
  49.8 12.5 %collective-permute-start.15 = (bf16[192,768]{1,0:T(8,128)(2,1)S(1)}, bf16[192,768]{1,0:T(8,128)(2,1)S(1)}, u32[]{:S(2)}, u32[]{:S(2)}) collective-permute-start(bf16[192,768]{1,0:T(8,128)(2,1)S(1)} %collective-permute-done.3.refs_2_), channel_id=1, source_target_pairs={{0,1},{1,0},{2,3},{3,2},{4,5},{5,4},{6,7},{7,6},{8,9},{9,8},{10,11... | collective-permute-start | bytes 884744 | tf_op jit(solution)/shard_map/ppermute | solution.py:35
  50.3 15.5 %collective-permute-start.26 = (bf16[192,768]{1,0:T(8,128)(2,1)S(1)}, bf16[192,768]{1,0:T(8,128)(2,1)S(1)}, u32[]{:S(2)}, u32[]{:S(2)}) collective-permute-start(bf16[192,768]{1,0:T(8,128)(2,1)S(1)} %copy-done.13), channel_id=1, source_target_pairs={{0,16},{8,24},{16,0},{24,8},{1,17},{9,25},{17,1},{25,9},{2,18},{10... | collective-permute-start | bytes 884744 | tf_op jit(solution)/shard_map/ppermute | solution.py:35
  63.9 13.2 %collective-permute-start.24 = (bf16[96,768]{1,0:T(8,128)(2,1)S(1)}, bf16[96,768]{1,0:T(8,128)(2,1)S(1)}, u32[]{:S(2)}, u32[]{:S(2)}) collective-permute-start(bf16[96,768]{1,0:T(8,128)(2,1)S(1)} %collective-permute-done.13.refs_3_), channel_id=1, source_target_pairs={{0,4},{4,0},{1,5},{5,1},{2,6},{6,2},{3,7},{7,3},{8,12},{12,8},{9,1... | collective-permute-start | bytes 442376 | tf_op jit(solution)/shard_map/ppermute | solution.py:35
  64.4 13.3 %collective-permute-start.23 = (bf16[96,768]{1,0:T(8,128)(2,1)S(1)}, bf16[96,768]{1,0:T(8,128)(2,1)S(1)}, u32[]{:S(2)}, u32[]{:S(2)}) collective-permute-start(bf16[96,768]{1,0:T(8,128)(2,1)S(1)} %collective-permute-done.12.refs_2_), channel_id=1, source_target_pairs={{0,4},{4,0},{1,5},{5,1},{2,6},{6,2},{3,7},{7,3},{8,12},{12,8},{9,1... | collective-permute-start | bytes 442376 | tf_op jit(solution)/shard_map/ppermute | solution.py:35
  75.5 13.9 %collective-permute-start.28 = (bf16[192,768]{1,0:T(8,128)(2,1)S(1)}, bf16[192,768]{1,0:T(8,128)(2,1)S(1)}, u32[]{:S(2)}, u32[]{:S(2)}) collective-permute-start(bf16[192,768]{1,0:T(8,128)(2,1)S(1)} %collective-permute-done.26.refs_6_), channel_id=1, source_target_pairs={{0,2},{1,3},{2,0},{3,1},{4,6},{5,7},{6,4},{7,5},{8,10},{9,11},{10,... | collective-permute-start | bytes 884744 | tf_op jit(solution)/shard_map/ppermute | solution.py:35
  77.0 12.4 %collective-permute-start.27 = (bf16[192,768]{1,0:T(8,128)(2,1)S(1)}, bf16[192,768]{1,0:T(8,128)(2,1)S(1)}, u32[]{:S(2)}, u32[]{:S(2)}) collective-permute-start(bf16[192,768]{1,0:T(8,128)(2,1)S(1)} %collective-permute-done.26.refs_6_), channel_id=1, source_target_pairs={{0,1},{1,0},{2,3},{3,2},{4,5},{5,4},{6,7},{7,6},{8,9},{9,8},{10,11... | collective-permute-start | bytes 884744 | tf_op jit(solution)/shard_map/ppermute | solution.py:35
  91.0 14.6 %collective-permute-start.32 = (bf16[192,768]{1,0:T(8,128)(2,1)S(1)}, bf16[192,768]{1,0:T(8,128)(2,1)S(1)}, u32[]{:S(2)}, u32[]{:S(2)}) collective-permute-start(bf16[192,768]{1,0:T(8,128)(2,1)S(1)} %collective-permute-done.30.refs_10_), channel_id=1, source_target_pairs={{0,2},{1,3},{2,0},{3,1},{4,6},{5,7},{6,4},{7,5},{8,10},{9,11},{10,... | collective-permute-start | bytes 884744 | tf_op jit(solution)/shard_map/ppermute | solution.py:35
  91.6 14.0 %collective-permute-start.31 = (bf16[192,768]{1,0:T(8,128)(2,1)S(1)}, bf16[192,768]{1,0:T(8,128)(2,1)S(1)}, u32[]{:S(2)}, u32[]{:S(2)}) collective-permute-start(bf16[192,768]{1,0:T(8,128)(2,1)S(1)} %collective-permute-done.30.refs_10_), channel_id=1, source_target_pairs={{0,1},{1,0},{2,3},{3,2},{4,5},{5,4},{6,7},{7,6},{8,9},{9,8},{10,11... | collective-permute-start | bytes 884744 | tf_op jit(solution)/shard_map/ppermute | solution.py:35
  124.3 16.2 %collective-permute-start.37 = (bf16[2,192,768]{2,1,0:T(8,128)(2,1)S(1)}, bf16[2,192,768]{2,1,0:T(8,128)(2,1)S(1)}, u32[]{:S(2)}, u32[]{:S(2)}) collective-permute-start(bf16[2,192,768]{2,1,0:T(8,128)(2,1)S(1)} %get-tuple-element.180), channel_id=1, source_target_pairs={{0,2},{1,3},{2,0},{3,1},{4,6},{5,7},{6,4},{7,5},{8,10},{9,11},{10,... | collective-permute-start | bytes 1769480 | tf_op jit(solution)/shard_map/ppermute | solution.py:35
  124.9 15.5 %collective-permute-start.36 = (bf16[2,192,768]{2,1,0:T(8,128)(2,1)S(1)}, bf16[2,192,768]{2,1,0:T(8,128)(2,1)S(1)}, u32[]{:S(2)}, u32[]{:S(2)}) collective-permute-start(bf16[2,192,768]{2,1,0:T(8,128)(2,1)S(1)} %get-tuple-element.174), channel_id=1, source_target_pairs={{0,1},{1,0},{2,3},{3,2},{4,5},{5,4},{6,7},{7,6},{8,9},{9,8},{10,11... | collective-permute-start | bytes 1769480 | tf_op jit(solution)/shard_map/ppermute | solution.py:35
  165.0 14.7 %collective-permute-start.47 = (bf16[2,96,768]{2,1,0:T(8,128)(2,1)S(1)}, bf16[2,96,768]{2,1,0:T(8,128)(2,1)S(1)}, u32[]{:S(2)}, u32[]{:S(2)}) collective-permute-start(bf16[2,96,768]{2,1,0:T(8,128)(2,1)S(1)} %bitcast.81), channel_id=1, source_target_pairs={{0,8},{8,0},{16,24},{24,16},{1,9},{9,1},{17,25},{25,17},{2,10},{10... | collective-permute-start | bytes 884744 | tf_op jit(solution)/shard_map/ppermute | solution.py:35
  166.2 14.6 %collective-permute-start.48 = (bf16[2,112,768]{2,1,0:T(8,128)(2,1)S(1)}, bf16[2,112,768]{2,1,0:T(8,128)(2,1)S(1)}, u32[]{:S(2)}, u32[]{:S(2)}) collective-permute-start(bf16[2,112,768]{2,1,0:T(8,128)(2,1)S(1)} %get-tuple-element.263), channel_id=1, source_target_pairs={{0,8},{8,0},{16,24},{24,16},{1,9},{9,1},{17,25},{25,17},{2,10},{10... | collective-permute-start | bytes 1032200 | tf_op jit(solution)/shard_map/ppermute | solution.py:35
  167.4 14.1 %collective-permute-start.45 = (bf16[2,384,384]{2,1,0:T(8,128)(2,1)S(1)}, bf16[2,384,384]{2,1,0:T(8,128)(2,1)S(1)}, u32[]{:S(2)}, u32[]{:S(2)}) collective-permute-start(bf16[2,384,384]{2,1,0:T(8,128)(2,1)S(1)} %get-tuple-element.215), channel_id=1, source_target_pairs={{0,1},{1,0},{2,3},{3,2},{4,5},{5,4},{6,7},{7,6},{8,9},{9,8},{10,11... | collective-permute-start | bytes 1769480 | tf_op jit(solution)/shard_map/ppermute | solution.py:35
  168.4 13.8 %collective-permute-start.46 = (bf16[2,384,384]{2,1,0:T(8,128)(2,1)S(1)}, bf16[2,384,384]{2,1,0:T(8,128)(2,1)S(1)}, u32[]{:S(2)}, u32[]{:S(2)}) collective-permute-start(bf16[2,384,384]{2,1,0:T(8,128)(2,1)S(1)} %get-tuple-element.216), channel_id=1, source_target_pairs={{0,2},{1,3},{2,0},{3,1},{4,6},{5,7},{6,4},{7,5},{8,10},{9,11},{10,... | collective-permute-start | bytes 1769480 | tf_op jit(solution)/shard_map/ppermute | solution.py:35
  182.3 12.0 %collective-permute-start.51 = (bf16[96,768]{1,0:T(8,128)(2,1)S(1)}, bf16[96,768]{1,0:T(8,128)(2,1)S(1)}, u32[]{:S(2)}, u32[]{:S(2)}) collective-permute-start(bf16[96,768]{1,0:T(8,128)(2,1)S(1)} %fusion.14), channel_id=1, source_target_pairs={{0,16},{8,24},{16,0},{24,8},{1,17},{9,25},{17,1},{25,9},{2,18},{10... | collective-permute-start | bytes 442376 | tf_op jit(solution)/shard_map/ppermute | solution.py:35
  184.4 12.7 %collective-permute-start.52 = (bf16[112,768]{1,0:T(8,128)(2,1)S(1)}, bf16[112,768]{1,0:T(8,128)(2,1)S(1)}, u32[]{:S(2)}, u32[]{:S(2)}) collective-permute-start(bf16[112,768]{1,0:T(8,128)(2,1)S(1)} %fusion.16), channel_id=1, source_target_pairs={{0,16},{8,24},{16,0},{24,8},{1,17},{9,25},{17,1},{25,9},{2,18},{10... | collective-permute-start | bytes 516104 | tf_op jit(solution)/shard_map/ppermute | solution.py:35
  199.1 14.7 %collective-permute-start.56 = (bf16[96,768]{1,0:T(8,128)(2,1)S(1)}, bf16[96,768]{1,0:T(8,128)(2,1)S(1)}, u32[]{:S(2)}, u32[]{:S(2)}) collective-permute-start(bf16[96,768]{1,0:T(8,128)(2,1)S(1)} %fusion.13.refs_0_), channel_id=1, source_target_pairs={{0,3},{1,2},{2,1},{3,0},{4,7},{5,6},{6,5},{7,4},{8,11},{9,10},{10,... | collective-permute-start | bytes 442376 | tf_op jit(solution)/shard_map/ppermute | solution.py:35
  200.5 13.3 %collective-permute-start.55 = (bf16[96,768]{1,0:T(8,128)(2,1)S(1)}, bf16[96,768]{1,0:T(8,128)(2,1)S(1)}, u32[]{:S(2)}, u32[]{:S(2)}) collective-permute-start(bf16[96,768]{1,0:T(8,128)(2,1)S(1)} %fusion.13.refs_0_), channel_id=1, source_target_pairs={{0,2},{1,3},{2,0},{3,1},{4,6},{5,7},{6,4},{7,5},{8,10},{9,11},{10,... | collective-permute-start | bytes 442376 | tf_op jit(solution)/shard_map/ppermute | solution.py:35
  201.6 12.2 %collective-permute-start.54 = (bf16[96,768]{1,0:T(8,128)(2,1)S(1)}, bf16[96,768]{1,0:T(8,128)(2,1)S(1)}, u32[]{:S(2)}, u32[]{:S(2)}) collective-permute-start(bf16[96,768]{1,0:T(8,128)(2,1)S(1)} %fusion.13.refs_0_), channel_id=1, source_target_pairs={{0,1},{1,0},{2,3},{3,2},{4,5},{5,4},{6,7},{7,6},{8,9},{9,8},{10,11... | collective-permute-start | bytes 442376 | tf_op jit(solution)/shard_map/ppermute | solution.py:35
  204.8 19.6 %collective-permute-start.58 = (bf16[2,192,384]{2,1,0:T(8,128)(2,1)S(1)}, bf16[2,192,384]{2,1,0:T(8,128)(2,1)S(1)}, u32[]{:S(2)}, u32[]{:S(2)}) collective-permute-start(bf16[2,192,384]{2,1,0:T(8,128)(2,1)S(1)} %bitcast.80), channel_id=1, source_target_pairs={{0,8},{8,0},{16,24},{24,16},{1,9},{9,1},{17,25},{25,17},{2,10},{10... | collective-permute-start | bytes 884744 | tf_op jit(solution)/shard_map/ppermute | solution.py:35
  231.0 24.2 %collective-permute-start.86 = (bf16[96,768]{1,0:T(8,128)(2,1)}, bf16[96,768]{1,0:T(8,128)(2,1)S(1)}, u32[]{:S(2)}, u32[]{:S(2)}) collective-permute-start(bf16[96,768]{1,0:T(8,128)(2,1)} %slice.268), channel_id=1, source_target_pairs={{0,4},{4,0},{1,5},{5,1},{2,6},{6,2},{3,7},{7,3},{8,12},{12,8},{9,1... | collective-permute-start | bytes 442376 | tf_op jit(solution)/shard_map/ppermute | solution.py:35
  231.1 12.0 %collective-permute-start.62 = (bf16[256,768]{1,0:T(8,128)(2,1)S(1)}, bf16[256,768]{1,0:T(8,128)(2,1)S(1)}, u32[]{:S(2)}, u32[]{:S(2)}) collective-permute-start(bf16[256,768]{1,0:T(8,128)(2,1)S(1)} %get-tuple-element.248), channel_id=1, source_target_pairs={{0,1},{1,0},{2,3},{3,2},{4,5},{5,4},{6,7},{7,6},{8,9},{9,8},{10,11... | collective-permute-start | bytes 1179656 | tf_op jit(solution)/shard_map/ppermute | solution.py:35
  232.0 19.6 %collective-permute-start.63 = (bf16[256,768]{1,0:T(8,128)(2,1)S(1)}, bf16[256,768]{1,0:T(8,128)(2,1)S(1)}, u32[]{:S(2)}, u32[]{:S(2)}) collective-permute-start(bf16[256,768]{1,0:T(8,128)(2,1)S(1)} %get-tuple-element.249), channel_id=1, source_target_pairs={{0,2},{1,3},{2,0},{3,1},{4,6},{5,7},{6,4},{7,5},{8,10},{9,11},{10,... | collective-permute-start | bytes 1179656 | tf_op jit(solution)/shard_map/ppermute | solution.py:35
  236.8 14.8 %collective-permute-start.64 = (bf16[256,768]{1,0:T(8,128)(2,1)S(1)}, bf16[256,768]{1,0:T(8,128)(2,1)S(1)}, u32[]{:S(2)}, u32[]{:S(2)}) collective-permute-start(bf16[256,768]{1,0:T(8,128)(2,1)S(1)} %get-tuple-element.250), channel_id=1, source_target_pairs={{0,3},{1,2},{2,1},{3,0},{4,7},{5,6},{6,5},{7,4},{8,11},{9,10},{10,... | collective-permute-start | bytes 1179656 | tf_op jit(solution)/shard_map/ppermute | solution.py:35
  240.9 20.5 %collective-permute-start.66 = (bf16[112,576]{1,0:T(8,128)(2,1)S(1)}, bf16[112,576]{1,0:T(8,128)(2,1)S(1)}, u32[]{:S(2)}, u32[]{:S(2)}) collective-permute-start(bf16[112,576]{1,0:T(8,128)(2,1)S(1)} %fusion.17), channel_id=1, source_target_pairs={{0,16},{8,24},{16,0},{24,8},{1,17},{9,25},{17,1},{25,9},{2,18},{10... | collective-permute-start | bytes 387080 | tf_op jit(solution)/shard_map/ppermute | solution.py:35
  (95 other events, 732.1 us)

commit v4 on v3

--- a/solution.py
+++ b/solution.py
@@ -1363,13 +1363,40 @@
         out_refs[j][...] = part.astype(out_refs[j].dtype)
 
 
-def finish_shrink_kernel(idx, *refs):
-    pieces, out_ref = refs[:-1], refs[-1]
+def pack_kernel(idx, sx_ref, sx1_ref, sx2_ref, sy_ref, sy1_ref, sy2_ref, keep_ref, got_ref, *refs):
+    unit = sx2_ref.shape[0] // 2
+    for out_ref, first, s_refs in (
+        (refs[0], 0, (sx_ref, sx1_ref, sx2_ref)),
+        (refs[1], 2, (sy_ref, sy1_ref, sy2_ref)),
+    ):
+        for k in range(2):
+            rows = slice(k * unit, (k + 1) * unit)
+            value = s_refs[0][0, rows].astype(F32) + s_refs[1][0, rows].astype(F32)
+            out_ref[k, :unit, :] = (value + s_refs[2][rows].astype(F32)).astype(BF16)
+            value = keep_ref[first + k].astype(F32) + got_ref[first + k].astype(F32)
+            out_ref[k, unit:, :] = value.astype(BF16)
+
+
+def finish_shrink_kernel(sizes, idx, *refs):
+    uly, unit = sizes
+    pieces, (shrink_ref, mixer_ref, vec_ref) = refs[: 2 * uly], refs[2 * uly :]
+    share = mixer_ref.shape[0] // 2
     for p, ref in enumerate(pieces):
 
         @pl.when(pl.program_id(0) == p)
         def _(ref=ref):
-            out_ref[...] = ref[...].astype(F32)
+            shrink_ref[...] = ref[:unit, :].astype(F32)
+
+    def plane_sum(refs, rows):
+        values = [ref[rows, :].astype(F32) for ref in refs]
+        return (values[0] + values[1]) + (values[2] + values[3])
+
+    @pl.when(pl.program_id(0) == 0)
+    def _():
+        for group, core in ((pieces[:uly], idx[0]), (pieces[uly:], 1 - idx[0])):
+            start = pl.multiple_of(core * share, share)
+            mixer_ref[pl.ds(start, share), :] = plane_sum(group, slice(unit, unit + share))
+        vec_ref[...] = plane_sum(pieces[:uly], slice(unit + share, unit + share + 16))
 
 
 def finish_expand_kernel(sizes, idx, *refs):
@@ -1616,12 +1643,21 @@
     e_near_x, e_far_x, e_near_y, e_far_y, deb, dx_own, dx_send = feed_backward(
         scalars, sizes, [x1b, x1b_other], after(ds, s_far_x), slope, weights
     )
+    def add(*values):
+        return total(values).astype(BF16)
+
+    dx_got = swap_with(after(dx_send, s_x, s_y), "blk", 1)
+    s_next_x = add(s_near_x[1], s_x[1])
+    s_next_y = add(s_near_y[1], s_y[1])
+    s_xy = swap_with(s_next_x, "uly", 2)
+    s_yx = swap_with(s_next_y, "uly", 1)
+    dx_got = after(dx_got, s_next_x, s_next_y)
     block = (dp, share + 16, width)
     dh1, *rest_out = call(
         functools.partial(norm_backward_kernel, sizes),
         "norm_backward",
         scalars,
-        [dh2, dx_own, swap_with(after(dx_send, s_x, s_y), "blk", 1), normed, inverse, mixer_all]
+        [dh2, dx_own, dx_got, normed, inverse, mixer_all]
         + [vec, sums2]
         + [deb.reshape(uly, dp * unit), *o_cols],
         [whole(square)] * 4
@@ -1640,55 +1676,54 @@
     douts = [rest_out[0]] + [swap_with(rest_out[j], "uly", j) for j in range(1, uly)]
     m_keep, m_send = rest_out[uly:]
 
-    def add(*values):
-        return total(values).astype(BF16)
-
     def quarter(j, so_far, *deps):
         dout = after(douts[j], *deps)
         return attend_grad(q, kvs, [dout], [outs[j]], lse, heads, j, so_far)
 
-    s_near_x, s_near_y, m_send = after((s_near_x, s_near_y, m_send), dh1)
-    s_next_x = add(s_near_x[1], s_x[1])
-    s_next_y = add(s_near_y[1], s_y[1])
-    s_xy = swap_with(after(s_next_x, *douts[1:]), "uly", 2)
-    s_yx = swap_with(after(s_next_y, *douts[1:]), "uly", 1)
-    m_got = swap_with(after(m_send, *douts[1:]), "blk", 1)
-    dq_0, dkvs = quarter(0, [], s_next_x, s_next_y, *douts[1:])
-
-    s_xy, s_yx, m_got, e_far_x, e_far_y = after((s_xy, s_yx, m_got, e_far_x, e_far_y), dq_0)
-    pair = (2, unit, width)
-    s_near = add(s_near_x[0], s_x[0], s_xy).reshape(pair)
-    s_far = add(s_near_y[0], s_y[0], s_yx).reshape(pair)
-    m_near, m_far = add(m_keep[:2], m_got[:2]), add(m_keep[2:], m_got[2:])
+    s_xy, s_yx = after((s_xy, s_yx), dh1)
+    m_got = swap_with(m_send, "blk", 1)
+    dq_0, dkvs = quarter(0, [], s_xy, s_yx)
+
+    m_got, e_far_x, e_far_y, *douts[1:] = after((m_got, e_far_x, e_far_y, *douts[1:]), dq_0)
+    half_block = pl.BlockSpec((1, 2 * unit, width), lambda *_: (0, 0, 0))
+    packed = (2, unit + share + 16, width)
+    p_near, p_far = call(
+        pack_kernel,
+        "pack",
+        scalars,
+        [s_near_x, s_x, s_xy, s_near_y, s_y, s_yx, m_keep, m_got],
+        [half_block, half_block, whole(s_xy.shape)] * 2 + [whole(m_keep.shape)] * 2,
+        [jax.ShapeDtypeStruct(packed, BF16)] * 2,
+        [whole(packed)] * 2,
+        [],
+        (1,),
+        10**6,
+        16,
+    )
     e_x = swap_with(e_far_x, "uly", 1)
     e_y = swap_with(e_far_y, "uly", 2)
-    s_one = swap_with(s_far, "dp", 1)
-    m_one = swap_with(m_far, "dp", 1)
-    dq_1, dkvs = quarter(1, dkvs, s_near, s_far, m_near, m_far)
-
+    p_one = swap_with(p_far, "dp", 1)
+    dq_1, dkvs = quarter(1, dkvs, p_near, *douts[2:])
     dq_2, dkvs = quarter(2, dkvs)
 
-    e_x, e_y, s_one, m_one = after((e_x, e_y, s_one, m_one), dq_2)
+    e_x, e_y, p_one = after((e_x, e_y, p_one), dq_2)
     e_next_x = add(e_near_x[1], e_x[1])
     e_next_y = add(e_near_y[1], e_y[1])
     e_xy = swap_with(e_next_x, "uly", 2)
     e_yx = swap_with(e_next_y, "uly", 1)
-    s_next = add(s_near[1], s_one[1])
-    m_next = add(m_near[1], m_one[1])
-    s_two = swap_with(s_next, "dp", 2)
-    m_two = swap_with(m_next, "dp", 2)
-    dq_3, dkvs = quarter(3, dkvs, e_next_x, e_next_y, s_next, m_next)
-
-    dkv_got = swap_with(after(dkvs[1], e_xy, e_yx, s_two, m_two), "blk", 1)
-    e_xy, e_yx, s_two, m_two = after((e_xy, e_yx, s_two, m_two), dq_3)
+    p_next = add(p_near[1], p_one[1])
+    p_two = swap_with(p_next, "dp", 2)
+    dq_3, dkvs = quarter(3, dkvs, e_next_x, e_next_y, p_next)
+
+    dkv_got = swap_with(after(dkvs[1], e_xy, e_yx, p_two), "blk", 1)
+    e_xy, e_yx, p_two = after((e_xy, e_yx, p_two), dq_3)
+    p_own = add(p_near[0], p_one[0], p_two)
     pair = (2, shard, dp * unit)
     e_near = add(e_near_x[0], e_x[0], e_xy).reshape(pair)
     e_far = add(e_near_y[0], e_y[0], e_yx).reshape(pair)
+    p_plane = [p_own] + [swap_with(p_own, "uly", j) for j in range(1, uly)]
     e_one = swap_with(e_far, "dp", 1)
-    s_own = add(s_near[0], s_one[0], s_two)
-    m_own = add(m_near[0], m_one[0], m_two)
-    s_plane = [s_own] + [swap_with(s_own, "uly", j) for j in range(1, uly)]
-    dkv_got = after(dkv_got, e_near, e_far, s_own, m_own)
+    dkv_got = after(dkv_got, p_own, e_near, e_far)
     dqs = [dq_0, dq_1, dq_2, dq_3]
     dproj, a_keep, a_send = call(
         functools.partial(project_grad_kernel, (uly, dp, group)),
@@ -1707,13 +1742,15 @@
         2 * block_rows * width * cols,
         16,
     )
-    a_got = swap_with(after(a_send, *s_plane), "blk", 1)
-    m_plane = [m_own] + [swap_with(after(m_own, *s_plane, dproj), "uly", j) for j in range(1, uly)]
+    a_got = swap_with(after(a_send, e_one), "blk", 1)
+    e_one = after(e_one, dproj)
+    e_next = add(e_near[1], e_one[1])
+    e_two = swap_with(e_next, "dp", 2)
     token_parts = call(
         functools.partial(token_grad_kernel, uly),
         "token_grad",
         scalars,
-        [dproj, w_own, dh1],
+        [after(dproj, e_next), w_own, dh1],
         [whole((block_rows, cols)), whole((width, cols)), whole(square)],
         [jax.ShapeDtypeStruct(square, F32)] + [jax.ShapeDtypeStruct(square, BF16)] * (uly - 1),
         [whole(square)] * uly,
@@ -1730,24 +1767,30 @@
     def both_cores(pieces, *deps):
         return pieces + [swap_with(after(piece, *deps), "blk", 1) for piece in pieces]
 
-    a_got, e_one = after((a_got, e_one), token_parts[0])
+    a_got = after(a_got, token_parts[0])
     a_near, a_far = add(a_keep[:2], a_got[:2]), add(a_keep[2:], a_got[2:])
     a_one = swap_with(a_far, "dp", 1)
-    e_next = add(e_near[1], e_one[1])
-    e_two = swap_with(e_next, "dp", 2)
-    token_parts = after(token_parts, a_near, a_far, e_next, *m_plane)
+    token_parts = after(token_parts, a_near, a_far, *p_plane)
     token_got = [swap_with(token_parts[j], "uly", j) for j in range(1, uly)]
     a_next = add(a_near[1], a_one[1])
     a_two = swap_with(a_next, "dp", 2)
-    s_plane = both_cores(s_plane, a_near)
-    shrink_out = call(
-        finish_shrink_kernel,
+    p_plane = both_cores(p_plane, a_near)
+    shrink_out, mixer_out, vecs = call(
+        functools.partial(finish_shrink_kernel, (uly, unit)),
         "finish_shrink",
         scalars,
-        s_plane,
-        [whole(s_own.shape)] * parts,
-        jax.ShapeDtypeStruct((hidden // dp, width), F32),
-        pl.BlockSpec((unit, width), lambda t, s: ((s[0] * uly + s[1]) ^ t, 0)),
+        p_plane,
+        [whole(p_own.shape)] * parts,
+        [
+            jax.ShapeDtypeStruct((hidden // dp, width), F32),
+            jax.ShapeDtypeStruct((shard, width), F32),
+            jax.ShapeDtypeStruct((16, width), F32),
+        ],
+        [
+            pl.BlockSpec((unit, width), lambda t, s: ((s[0] * uly + s[1]) ^ t, 0)),
+            whole((shard, width)),
+            whole((16, width)),
+        ],
         [],
         (parts,),
         10**6,
@@ -1786,19 +1829,15 @@
         10**9,
         16,
     )
-    m_all = [value.astype(F32) for value in m_plane]
-    m_all = (m_all[0] + m_all[1]) + (m_all[2] + m_all[3])
-    m_half = m_all[:share].astype(BF16)
-    mixer_out = jnp.concatenate(xor_order([m_half, swap_with(m_half, "blk", 1)], b), 0)
-    vecs = [m_all[share + k, :shard] for k in range(6)]
-    eb_out = m_all[share + 8 : share + 8 + parts, :unit].reshape(-1)
+    eb_out = vecs[8 : 8 + parts, :unit].reshape(-1)
+    vecs = [vecs[k, :shard] for k in range(6)]
     return (
         mixed.reshape(tokens.shape),
         tokens_grad.reshape(tokens.shape),
         attend_out,
         biases[0, :group],
         biases[0, 2 * group :],
-        mixer_out.astype(F32),
+        mixer_out,
         vecs[0],
         vecs[1],
         vecs[2],

time: 284 us -> 274 us (0.965)
  waiting for transfers between devices: 88.2 us -> 104 us
  other arithmetic: 11.7 us -> 2.79 us
  local copies, waits for them, and re-layouts: 10.7 us -> 2.78 us
  starting transfers between devices: 73.8 us -> 68 us
    ppermute x87 -> x81, waiting for transfers between devices: 88.2 us -> 104 us  [swap_with(): return lax.ppermute(value, axis, [(i, i ^ offset) for i in range(size)])]
    unnamed x81 -> x19, local copies, waits for them, and re-layouts: 8.17 us -> 0.95 us
    convert_element_type x17 -> x13, other arithmetic: 8.06 us -> 1.11 us  [add(): return total(values).astype(BF16)]
    ppermute x87 -> x81, starting transfers between devices: 73.8 us -> 68 us  [swap_with(): return lax.ppermute(value, axis, [(i, i ^ offset) for i in range(size)])]
    pallas_call x15 -> x16, Pallas kernels: 59 us -> 58.9 us  [call(): pl.pallas_call(kernel, grid_spec=pltpu.PrefetchScalarGridSpec(num_scalar_...]
  transfers between devices with their start and end apart: 87 -> 81, of which waited for: 37 -> 38; matrix products, arithmetic and copies ran while one was open for 4% -> 1% of each run, Pallas kernels for 25% -> 25%
where the time goes in v4:
time: 274 us; the launch traced here: 270 us
  waiting for transfers between devices  104 us (38%)
  Pallas kernels  90.7 us (33%)
  starting transfers between devices  68 us (25%)
  other arithmetic  2.79 us (1%)
  local copies, waits for them, and re-layouts  2.78 us (1%)
    ppermute x81, waiting for transfers between devices, swap_with(): return lax.ppermute(value, axis, [(i, i ^ offset) for i in range(size)])  104 us
    ppermute x81, starting transfers between devices, swap_with(): return lax.ppermute(value, axis, [(i, i ^ offset) for i in range(size)])  68 us
    pallas_call x16, Pallas kernels, call(): pl.pallas_call(kernel, grid_spec=pltpu.PrefetchScalarGridSpec(num_scalar_...  58.9 us
    pallas_call x4, Pallas kernels, attend_grad(): pl.pallas_call(functools.partial(attend_grad_kernel, heads, blocks, piece...  20.1 us
    pallas_call x1, Pallas kernels, attend(): pl.pallas_call(functools.partial(attend_kernel, heads, blocks), grid=(pie...  11.7 us
  transfers between devices with their start and end apart: 81, of which 38 were waited for; matrix products, arithmetic and copies ran while one was open for 1% of the time, Pallas kernels for 25%

profile of v4, /device:TPU:0, one launch (start us, length us, event | category | flops | bytes accessed | tf_op | source)
XLA Modules:
  0.0 270.3 jit_solution(3066395253916930548)
XLA Ops:
  0.6 3.0 %collective-permute-start.1 = (bf16[256,768]{1,0:T(8,128)(2,1)}, bf16[256,768]{1,0:T(8,128)(2,1)S(1)}, u32[]{:S(2)}, u32[]{:S(2)}) collective-permute-start(bf16[256,768]{1,0:T(8,128)(2,1)} %bitcast.56), channel_id=1, source_target_pairs={{0,2},{1,3},{2,0},{3,1},{4,6},{5,7},{6,4},{7,5},{8,10},{9,11},{10,... | collective-permute-start | bytes 1179656 | tf_op jit(solution)/shard_map/ppermute | solution.py:35
  6.4 3.8 %fetch.1 = (bf16[112,768]{1,0:T(8,128)(2,1)}, bf16[192,768]{1,0:T(8,128)(2,1)}) custom-call(s32[4]{0:T(128)} %pad_add_fusion.idx, bf16[2,96,2304]{2,1,0:T(8,128)(2,1)} %bitcast.74, bf16[192,3072]{1,0:T(8,128)(2,1)} %expand_ref.3, bf16[8,96,768]{2,1,0:T(8,128)(2,1)} %bitcast.64, bf16[192,768]{1,0:T(8,128)(2,1)} %mixer_ref.1, bf16[192]{0:T(256)(128)(2,1)} %refs_0_.1, ...), custom_call_target="tpu_custom_call" | custom-call | flops 1000000000 | bytes 1 | tf_op jit(solution)/shard_map/fetch/pallas_call | solution.py:653
  15.9 3.6 %collective-permute-start.6 = (bf16[112,768]{1,0:T(8,128)(2,1)}, bf16[112,768]{1,0:T(8,128)(2,1)S(1)}, u32[]{:S(2)}, u32[]{:S(2)}) collective-permute-start(bf16[112,768]{1,0:T(8,128)(2,1)} %get-tuple-element.147.refs_4_), channel_id=1, source_target_pairs={{0,24},{8,16},{16,8},{24,0},{1,25},{9,17},{17,9},{25,1},{2,26},{10... | collective-permute-start | bytes 516104 | tf_op jit(solution)/shard_map/ppermute | solution.py:35
  20.3 5.7 %collective-permute-done.6.refs_7_ = bf16[112,768]{1,0:T(8,128)(2,1)S(1)} collective-permute-done((bf16[112,768]{1,0:T(8,128)(2,1)}, bf16[112,768]{1,0:T(8,128)(2,1)S(1)}, u32[]{:S(2)}, u32[]{:S(2)}) %collective-permute-start.6) | collective-permute-done | bytes 172064 | tf_op jit(solution)/shard_map/ppermute | solution.py:35
  26.0 6.9 %collective-permute-done.5.refs_6_ = bf16[112,768]{1,0:T(8,128)(2,1)S(1)} collective-permute-done((bf16[112,768]{1,0:T(8,128)(2,1)}, bf16[112,768]{1,0:T(8,128)(2,1)S(1)}, u32[]{:S(2)}, u32[]{:S(2)}) %collective-permute-start.5) | collective-permute-done | bytes 172064 | tf_op jit(solution)/shard_map/ppermute | solution.py:35
  35.8 2.8 %project.1 = (bf16[768,768]{1,0:T(8,128)(2,1)S(1)}, bf16[1024,256]{1,0:T(8,128)(2,1)S(1)}, bf16[1024,512]{1,0:T(8,128)(2,1)S(1)}, f32[16,768]{1,0:T(8,128)S(1)},...) custom-call(s32[4]{0:T(128)S(1)} %copy-done.2, bf16[256,768]{1,0:T(8,128)(2,1)S(1)} %bitcast.59, ...), custom_call_target="tpu_custom_call" | custom-call | flops 1207959552 | bytes 1 | tf_op jit(solution)/shard_map/project/pallas_call | solution.py:653
  50.3 11.7 %attend.1 = (bf16[256,192]{1,0:T(8,128)(2,1)S(1)}, bf16[256,192]{1,0:T(8,128)(2,1)S(1)}, bf16[256,192]{1,0:T(8,128)(2,1)S(1)}, bf16[256,192]{1,0:T(8,128)(2,1)S(1)}, f32[8,1024]{1,0:T(8,128)S(1)}) custom-call(bf16[1024,256]{1,0:T(8,128)(2,1)S(1)} %get-tuple-element.150.q_ref, bf16[1024,512]{1,0:T(8,128)(2,1)S(1)} %get-tuple-element.151.refs_0_.refs_2_, ...), custom_call_target="tpu_custom_call" | custom-call | flops 6442450944 | bytes 3407872 | tf_op jit(solution)/shard_map/attend/pallas_call | solution.py:830
  68.8 5.1 %collective-permute-done.19.refs_2_.refs_6_ = bf16[256,192]{1,0:T(8,128)(2,1)S(1)} collective-permute-done((bf16[256,192]{1,0:T(8,128)(2,1)S(1)}, bf16[256,192]{1,0:T(8,128)(2,1)S(1)}, u32[]{:S(2)}, u32[]{:S(2)}) %collective-permute-start.19) | collective-permute-done | bytes 98336 | tf_op jit(solution)/shard_map/ppermute | solution.py:35
  82.6 2.2 collective-permute-done.29.refs_9_
  84.8 3.4 %collective-permute-done.28.refs_8_ = bf16[192,768]{1,0:T(8,128)(2,1)S(1)} collective-permute-done((bf16[192,768]{1,0:T(8,128)(2,1)S(1)}, bf16[192,768]{1,0:T(8,128)(2,1)S(1)}, u32[]{:S(2)}, u32[]{:S(2)}) %collective-permute-start.28) | collective-permute-done | bytes 294944 | tf_op jit(solution)/shard_map/ppermute | solution.py:35
  92.7 7.4 %collective-permute-done.33.refs_13_ = bf16[192,768]{1,0:T(8,128)(2,1)S(1)} collective-permute-done((bf16[192,768]{1,0:T(8,128)(2,1)S(1)}, bf16[192,768]{1,0:T(8,128)(2,1)S(1)}, u32[]{:S(2)}, u32[]{:S(2)}) %collective-permute-start.33) | collective-permute-done | bytes 294944 | tf_op jit(solution)/shard_map/ppermute | solution.py:35
  100.1 4.3 %collective-permute-done.32.refs_12_ = bf16[192,768]{1,0:T(8,128)(2,1)S(1)} collective-permute-done((bf16[192,768]{1,0:T(8,128)(2,1)S(1)}, bf16[192,768]{1,0:T(8,128)(2,1)S(1)}, u32[]{:S(2)}, u32[]{:S(2)}) %collective-permute-start.32) | collective-permute-done | bytes 294944 | tf_op jit(solution)/shard_map/ppermute | solution.py:35
  105.4 10.0 %feed_forward.1 = (bf16[4,512,384]{2,1,0:T(8,128)(2,1)S(1)}, bf16[4,512,384]{2,1,0:T(8,128)(2,1)S(1)}, f32[256,768]{1,0:T(8,128)S(1)}, bf16[256,768]{1,0:T(8,128)(2,1)S(1)}) custom-call(s32[4]{0:T(128)S(1)} %copy-done.2, bf16[256,768]{1,0:T(8,128)(2,1)S(1)} %get-tuple-element.162.mine_ref.x_mine, ...), custom_call_target="tpu_custom_call" | custom-call | flops 2415919104 | bytes 1 | tf_op jit(solution)/shard_map/feed_forward/pallas_call | solution.py:653
  120.8 3.2 %shrink_grad.1 = (bf16[2,192,768]{2,1,0:T(8,128)(2,1)S(1)}, bf16[2,192,768]{2,1,0:T(8,128)(2,1)S(1)}, bf16[2,192,768]{2,1,0:T(8,128)(2,1)S(1)}, bf16[2,192,768]{2,1,0:T(8,128)(2,1)S(1)}) custom-call(s32[4]{0:T(128)S(1)} %copy-done.2, bf16[256,768]{1,0:T(8,128)(2,1)S(1)} %get-tuple-element.176.d_mine, bf16[256,768]{1,0:T(8,128)(2,1)S(1)} %collective-permute-done.35.d_other, ...), custom_call_target="tpu_custom_call" | custom-call | flops 1207959552 | bytes 1 | tf_op jit(solution)/shard_map/shrink_grad/pallas_call | solution.py:653
  126.2 14.1 %feed_backward.1 = (bf16[2,384,384]{2,1,0:T(8,128)(2,1)S(1)}, bf16[2,384,384]{2,1,0:T(8,128)(2,1)S(1)}, bf16[2,384,384]{2,1,0:T(8,128)(2,1)S(1)}, bf16[2,384,384...) custom-call(s32[4]{0:T(128)S(1)} %copy-done.2, ...), custom_call_target="tpu_custom_call" | custom-call | flops 3623878656 | bytes 1 | tf_op jit(solution)/shard_map/feed_backward/pallas_call | solution.py:653
  142.3 2.3 norm_backward.1
  146.9 7.2 %collective-permute-done.40.sy2_ref = bf16[192,768]{1,0:T(8,128)(2,1)S(1)} collective-permute-done((bf16[192,768]{1,0:T(8,128)(2,1)S(1)}, bf16[192,768]{1,0:T(8,128)(2,1)S(1)}, u32[]{:S(2)}, u32[]{:S(2)}) %collective-permute-start.40) | collective-permute-done | bytes 294944 | tf_op jit(solution)/shard_map/ppermute | solution.py:35
  158.5 5.0 %attend_grad.4 = (bf16[256,192]{1,0:T(8,128)(2,1)S(1)}, bf16[1024,512]{1,0:T(8,128)(2,1)S(1)}, bf16[1024,512]{1,0:T(8,128)(2,1)S(1)}) custom-call(bf16[1024,256]{1,0:T(8,128)(2,1)S(1)} %get-tuple-element.150.q_ref, f32[8,1024]{1,0:T(8,128)S(1)} %get-tuple-element.171.lse_ref, bf16[256,192]{1,0:T(8,128)(2,1)S(1)} %get-tuple-element.194.refs_0_, ...), custom_call_target="tpu_custom_call" | custom-call | flops 4026531840 | bytes 5767168 | tf_op jit(solution)/shard_map/attend_grad/pallas_call | solution.py:1291
  167.2 5.0 %attend_grad.5 = (bf16[256,192]{1,0:T(8,128)(2,1)S(1)}, bf16[1024,512]{1,0:T(8,128)(2,1)S(1)}, bf16[1024,512]{1,0:T(8,128)(2,1)S(1)}) custom-call(bf16[1024,256]{1,0:T(8,128)(2,1)S(1)} %get-tuple-element.150.q_ref, f32[8,1024]{1,0:T(8,128)S(1)} %get-tuple-element.171.lse_ref, bf16[256,192]{1,0:T(8,128)(2,1)S(1)} %collective-permute-done.42.refs_0_, ...), custom_call_target="tpu_custom_call" | custom-call | flops 4026531840 | bytes 5767168 | tf_op jit(solution)/shard_map/attend_grad/pallas_call | solution.py:1291
  172.2 5.2 %attend_grad.6 = (bf16[256,192]{1,0:T(8,128)(2,1)S(1)}, bf16[1024,512]{1,0:T(8,128)(2,1)S(1)}, bf16[1024,512]{1,0:T(8,128)(2,1)S(1)}) custom-call(bf16[1024,256]{1,0:T(8,128)(2,1)S(1)} %get-tuple-element.150.q_ref, f32[8,1024]{1,0:T(8,128)S(1)} %get-tuple-element.171.lse_ref, bf16[256,192]{1,0:T(8,128)(2,1)S(1)} %collective-permute-done.43.refs_0_, ...), custom_call_target="tpu_custom_call" | custom-call | flops 4026531840 | bytes 5767168 | tf_op jit(solution)/shard_map/attend_grad/pallas_call | solution.py:1291
  183.1 2.4 collective-permute-start.50
  185.6 5.0 %attend_grad.7 = (bf16[256,192]{1,0:T(8,128)(2,1)S(1)}, bf16[1024,512]{1,0:T(8,128)(2,1)S(1)}, bf16[1024,512]{1,0:T(8,128)(2,1)S(1)}) custom-call(bf16[1024,256]{1,0:T(8,128)(2,1)S(1)} %get-tuple-element.150.q_ref, f32[8,1024]{1,0:T(8,128)S(1)} %get-tuple-element.171.lse_ref, bf16[256,192]{1,0:T(8,128)(2,1)S(1)} %collective-permute-done.44.refs_0_, ...), custom_call_target="tpu_custom_call" | custom-call | flops 4026531840 | bytes 5767168 | tf_op jit(solution)/shard_map/attend_grad/pallas_call | solution.py:1291
  190.6 6.2 %collective-permute-done.50 = bf16[208,768]{1,0:T(8,128)(2,1)S(1)} collective-permute-done((bf16[208,768]{1,0:T(8,128)(2,1)S(1)}, bf16[208,768]{1,0:T(8,128)(2,1)S(1)}, u32[]{:S(2)}, u32[]{:S(2)}) %collective-permute-start.50) | collective-permute-done | bytes 319520 | tf_op jit(solution)/shard_map/ppermute | solution.py:35
  201.4 3.3 %project_grad.1 = (bf16[1024,768]{1,0:T(8,128)(2,1)S(1)}, bf16[4,112,576]{2,1,0:T(8,128)(2,1)S(1)}, bf16[4,112,576]{2,1,0:T(8,128)(2,1)S(1)}) custom-call(s32[4]{0:T(128)S(1)} %copy-done.2, bf16[256,192]{1,0:T(8,128)(2,1)S(1)} %get-tuple-element.195.refs_0_, bf16[256,192]{1,0:T(8,128)(2,1)S(1)} %get-tuple-element.211.refs_1_, ...), custom_call_target="tpu_custom_call" | custom-call | flops 1207959552 | bytes 1 | tf_op jit(solution)/shard_map/project_grad/pallas_call | solution.py:653
  209.3 5.4 %collective-permute-done.54.refs_1_ = bf16[208,768]{1,0:T(8,128)(2,1)S(1)} collective-permute-done((bf16[208,768]{1,0:T(8,128)(2,1)S(1)}, bf16[208,768]{1,0:T(8,128)(2,1)S(1)}, u32[]{:S(2)}, u32[]{:S(2)}) %collective-permute-start.54) | collective-permute-done | bytes 319520 | tf_op jit(solution)/shard_map/ppermute | solution.py:35
  215.3 3.4 %collective-permute-start.65 = (bf16[192,384]{1,0:T(8,128)(2,1)S(1)}, bf16[192,384]{1,0:T(8,128)(2,1)S(1)}, u32[]{:S(2)}, u32[]{:S(2)}) collective-permute-start(bf16[192,384]{1,0:T(8,128)(2,1)S(1)} %fusion.10), channel_id=1, source_target_pairs={{0,16},{8,24},{16,0},{24,8},{1,17},{9,25},{17,1},{25,9},{2,18},{10... | collective-permute-start | bytes 442376 | tf_op jit(solution)/shard_map/ppermute | solution.py:35
  219.9 6.5 %collective-permute-done.65 = bf16[192,384]{1,0:T(8,128)(2,1)S(1)} collective-permute-done((bf16[192,384]{1,0:T(8,128)(2,1)S(1)}, bf16[192,384]{1,0:T(8,128)(2,1)S(1)}, u32[]{:S(2)}, u32[]{:S(2)}) %collective-permute-start.65) | collective-permute-done | bytes 147488 | tf_op jit(solution)/shard_map/ppermute | solution.py:35
  230.1 4.0 %finish_shrink.1 = (f32[768,768]{1,0:T(8,128)}, f32[192,768]{1,0:T(8,128)}, f32[16,768]{1,0:T(8,128)S(1)}) custom-call(s32[4]{0:T(128)S(1)} %copy-done.2, bf16[208,768]{1,0:T(8,128)(2,1)S(1)} %fusion.refs_0_, bf16[208,768]{1,0:T(8,128)(2,1)S(1)} %collective-permute-done.54.refs_1_, bf16[208,768]{1,0:T(8,128)(2,1)S(1)} %collective-permute-done.55.refs_2_, ...), custom_call_target="tpu_custom_call" | custom-call | flops 1000000 | bytes 1 | tf_op jit(solution)/shard_map/finish_shrink/pallas_call | solution.py:653
  234.2 11.6 %collective-permute-done.58 = bf16[256,768]{1,0:T(8,128)(2,1)S(1)} collective-permute-done((bf16[256,768]{1,0:T(8,128)(2,1)S(1)}, bf16[256,768]{1,0:T(8,128)(2,1)S(1)}, u32[]{:S(2)}, u32[]{:S(2)}) %collective-permute-start.58) | collective-permute-done | bytes 393248 | tf_op jit(solution)/shard_map/ppermute | solution.py:35
  249.5 3.9 %collective-permute-done.72.refs_3_ = bf16[192,384]{1,0:T(8,128)(2,1)S(1)} collective-permute-done((bf16[192,384]{1,0:T(8,128)(2,1)S(1)}, bf16[192,384]{1,0:T(8,128)(2,1)S(1)}, u32[]{:S(2)}, u32[]{:S(2)}) %collective-permute-start.72) | collective-permute-done | bytes 147488 | tf_op jit(solution)/shard_map/ppermute | solution.py:35
  260.7 3.7 %finish_expand.1 = f32[192,3072]{1,0:T(8,128)} custom-call(s32[4]{0:T(128)S(1)} %copy-done.2, bf16[192,384]{1,0:T(8,128)(2,1)S(1)} %fusion.9.refs_0_, bf16[192,384]{1,0:T(8,128)(2,1)S(1)} %collective-permute-done.70.refs_1_, bf16[192,384]{1,0:T(8,128)(2,1)S(1)} %collective-permute-done.71.refs_2_, bf16[192,384]{1,0:T(8,128)(2,1)S(1)} %collective-permute-done.72.refs_3_, ...), custom_call_target="tpu_custom_call" | custom-call | flops 1000000000 | bytes 1 | tf_op jit(solution)/shard_map/finish_expand/pallas_call | solution.py:653
  266.6 2.9 %finish_attend.1 = (f32[192,2304]{1,0:T(8,128)}, f32[8,576]{1,0:T(8,128)S(1)}) custom-call(s32[4]{0:T(128)S(1)} %copy-done.2, bf16[112,576]{1,0:T(8,128)(2,1)S(1)} %fusion.11.refs_0_, bf16[112,576]{1,0:T(8,128)(2,1)S(1)} %collective-permute-done.62.refs_1_, bf16[112,576]{1,0:T(8,128)(2,1)S(1)} %collective-permute-done.63.refs_2_, ...), custom_call_target="tpu_custom_call" | custom-call | flops 1000000000 | bytes 1 | tf_op jit(solution)/shard_map/finish_attend/pallas_call | solution.py:653
  (189 shorter events, 98.3 us)
Async XLA Ops:
  0.6 12.4 %collective-permute-start.1 = (bf16[256,768]{1,0:T(8,128)(2,1)}, bf16[256,768]{1,0:T(8,128)(2,1)S(1)}, u32[]{:S(2)}, u32[]{:S(2)}) collective-permute-start(bf16[256,768]{1,0:T(8,128)(2,1)} %bitcast.56), channel_id=1, source_target_pairs={{0,2},{1,3},{2,0},{3,1},{4,6},{5,7},{6,4},{7,5},{8,10},{9,11},{10,... | collective-permute-start | bytes 1179656 | tf_op jit(solution)/shard_map/ppermute | solution.py:35
  10.3 22.7 %collective-permute-start.3 = (bf16[192,768]{1,0:T(8,128)(2,1)}, bf16[192,768]{1,0:T(8,128)(2,1)S(1)}, u32[]{:S(2)}, u32[]{:S(2)}) collective-permute-start(bf16[192,768]{1,0:T(8,128)(2,1)} %get-tuple-element.166.refs_0_), channel_id=1, source_target_pairs={{0,8},{8,0},{16,24},{24,16},{1,9},{9,1},{17,25},{25,17},{2,10},{10... | collective-permute-start | bytes 884744 | tf_op jit(solution)/shard_map/ppermute | solution.py:35
  14.5 19.1 %collective-permute-start.2 = (bf16[256,768]{1,0:T(8,128)(2,1)S(1)}, bf16[256,768]{1,0:T(8,128)(2,1)S(1)}, u32[]{:S(2)}, u32[]{:S(2)}) collective-permute-start(bf16[256,768]{1,0:T(8,128)(2,1)S(1)} %bitcast.58), channel_id=1, source_target_pairs={{0,3},{1,2},{2,1},{3,0},{4,7},{5,6},{6,5},{7,4},{8,11},{9,10},{10,... | collective-permute-start | bytes 1179656 | tf_op jit(solution)/shard_map/ppermute | solution.py:35
  19.5 13.4 %collective-permute-start.5 = (bf16[112,768]{1,0:T(8,128)(2,1)}, bf16[112,768]{1,0:T(8,128)(2,1)S(1)}, u32[]{:S(2)}, u32[]{:S(2)}) collective-permute-start(bf16[112,768]{1,0:T(8,128)(2,1)} %get-tuple-element.147.refs_4_), channel_id=1, source_target_pairs={{0,16},{8,24},{16,0},{24,8},{1,17},{9,25},{17,1},{25,9},{2,18},{10... | collective-permute-start | bytes 516104 | tf_op jit(solution)/shard_map/ppermute | solution.py:35
  19.5 13.9 %collective-permute-start.4 = (bf16[112,768]{1,0:T(8,128)(2,1)}, bf16[112,768]{1,0:T(8,128)(2,1)S(1)}, u32[]{:S(2)}, u32[]{:S(2)}) collective-permute-start(bf16[112,768]{1,0:T(8,128)(2,1)} %get-tuple-element.147.refs_4_), channel_id=1, source_target_pairs={{0,8},{8,0},{16,24},{24,16},{1,9},{9,1},{17,25},{25,17},{2,10},{10... | collective-permute-start | bytes 516104 | tf_op jit(solution)/shard_map/ppermute | solution.py:35
  44.1 17.9 %collective-permute-start.17 = (bf16[192,768]{1,0:T(8,128)(2,1)S(1)}, bf16[192,768]{1,0:T(8,128)(2,1)S(1)}, u32[]{:S(2)}, u32[]{:S(2)}) collective-permute-start(bf16[192,768]{1,0:T(8,128)(2,1)S(1)} %collective-permute-done.3.refs_2_), channel_id=1, source_target_pairs={{0,3},{1,2},{2,1},{3,0},{4,7},{5,6},{6,5},{7,4},{8,11},{9,10},{10,... | collective-permute-start | bytes 884744 | tf_op jit(solution)/shard_map/ppermute | solution.py:35
  46.5 15.5 %collective-permute-start.16 = (bf16[192,768]{1,0:T(8,128)(2,1)S(1)}, bf16[192,768]{1,0:T(8,128)(2,1)S(1)}, u32[]{:S(2)}, u32[]{:S(2)}) collective-permute-start(bf16[192,768]{1,0:T(8,128)(2,1)S(1)} %collective-permute-done.3.refs_2_), channel_id=1, source_target_pairs={{0,2},{1,3},{2,0},{3,1},{4,6},{5,7},{6,4},{7,5},{8,10},{9,11},{10,... | collective-permute-start | bytes 884744 | tf_op jit(solution)/shard_map/ppermute | solution.py:35
  49.7 12.3 %collective-permute-start.15 = (bf16[192,768]{1,0:T(8,128)(2,1)S(1)}, bf16[192,768]{1,0:T(8,128)(2,1)S(1)}, u32[]{:S(2)}, u32[]{:S(2)}) collective-permute-start(bf16[192,768]{1,0:T(8,128)(2,1)S(1)} %collective-permute-done.3.refs_2_), channel_id=1, source_target_pairs={{0,1},{1,0},{2,3},{3,2},{4,5},{5,4},{6,7},{7,6},{8,9},{9,8},{10,11... | collective-permute-start | bytes 884744 | tf_op jit(solution)/shard_map/ppermute | solution.py:35
  50.2 15.5 %collective-permute-start.26 = (bf16[192,768]{1,0:T(8,128)(2,1)S(1)}, bf16[192,768]{1,0:T(8,128)(2,1)S(1)}, u32[]{:S(2)}, u32[]{:S(2)}) collective-permute-start(bf16[192,768]{1,0:T(8,128)(2,1)S(1)} %copy-done.5), channel_id=1, source_target_pairs={{0,16},{8,24},{16,0},{24,8},{1,17},{9,25},{17,1},{25,9},{2,18},{10... | collective-permute-start | bytes 884744 | tf_op jit(solution)/shard_map/ppermute | solution.py:35
  63.5 13.4 %collective-permute-start.24 = (bf16[96,768]{1,0:T(8,128)(2,1)S(1)}, bf16[96,768]{1,0:T(8,128)(2,1)S(1)}, u32[]{:S(2)}, u32[]{:S(2)}) collective-permute-start(bf16[96,768]{1,0:T(8,128)(2,1)S(1)} %collective-permute-done.13.refs_3_), channel_id=1, source_target_pairs={{0,4},{4,0},{1,5},{5,1},{2,6},{6,2},{3,7},{7,3},{8,12},{12,8},{9,1... | collective-permute-start | bytes 442376 | tf_op jit(solution)/shard_map/ppermute | solution.py:35
  64.1 13.4 %collective-permute-start.23 = (bf16[96,768]{1,0:T(8,128)(2,1)S(1)}, bf16[96,768]{1,0:T(8,128)(2,1)S(1)}, u32[]{:S(2)}, u32[]{:S(2)}) collective-permute-start(bf16[96,768]{1,0:T(8,128)(2,1)S(1)} %collective-permute-done.12.refs_2_), channel_id=1, source_target_pairs={{0,4},{4,0},{1,5},{5,1},{2,6},{6,2},{3,7},{7,3},{8,12},{12,8},{9,1... | collective-permute-start | bytes 442376 | tf_op jit(solution)/shard_map/ppermute | solution.py:35
  75.3 13.0 %collective-permute-start.28 = (bf16[192,768]{1,0:T(8,128)(2,1)S(1)}, bf16[192,768]{1,0:T(8,128)(2,1)S(1)}, u32[]{:S(2)}, u32[]{:S(2)}) collective-permute-start(bf16[192,768]{1,0:T(8,128)(2,1)S(1)} %collective-permute-done.26.refs_6_), channel_id=1, source_target_pairs={{0,2},{1,3},{2,0},{3,1},{4,6},{5,7},{6,4},{7,5},{8,10},{9,11},{10,... | collective-permute-start | bytes 884744 | tf_op jit(solution)/shard_map/ppermute | solution.py:35
  76.9 12.4 %collective-permute-start.27 = (bf16[192,768]{1,0:T(8,128)(2,1)S(1)}, bf16[192,768]{1,0:T(8,128)(2,1)S(1)}, u32[]{:S(2)}, u32[]{:S(2)}) collective-permute-start(bf16[192,768]{1,0:T(8,128)(2,1)S(1)} %collective-permute-done.26.refs_6_), channel_id=1, source_target_pairs={{0,1},{1,0},{2,3},{3,2},{4,5},{5,4},{6,7},{7,6},{8,9},{9,8},{10,11... | collective-permute-start | bytes 884744 | tf_op jit(solution)/shard_map/ppermute | solution.py:35
  90.8 13.6 %collective-permute-start.32 = (bf16[192,768]{1,0:T(8,128)(2,1)S(1)}, bf16[192,768]{1,0:T(8,128)(2,1)S(1)}, u32[]{:S(2)}, u32[]{:S(2)}) collective-permute-start(bf16[192,768]{1,0:T(8,128)(2,1)S(1)} %collective-permute-done.30.refs_10_), channel_id=1, source_target_pairs={{0,2},{1,3},{2,0},{3,1},{4,6},{5,7},{6,4},{7,5},{8,10},{9,11},{10,... | collective-permute-start | bytes 884744 | tf_op jit(solution)/shard_map/ppermute | solution.py:35
  92.2 13.2 %collective-permute-start.31 = (bf16[192,768]{1,0:T(8,128)(2,1)S(1)}, bf16[192,768]{1,0:T(8,128)(2,1)S(1)}, u32[]{:S(2)}, u32[]{:S(2)}) collective-permute-start(bf16[192,768]{1,0:T(8,128)(2,1)S(1)} %collective-permute-done.30.refs_10_), channel_id=1, source_target_pairs={{0,1},{1,0},{2,3},{3,2},{4,5},{5,4},{6,7},{7,6},{8,9},{9,8},{10,11... | collective-permute-start | bytes 884744 | tf_op jit(solution)/shard_map/ppermute | solution.py:35
  124.0 16.3 %collective-permute-start.37 = (bf16[2,192,768]{2,1,0:T(8,128)(2,1)S(1)}, bf16[2,192,768]{2,1,0:T(8,128)(2,1)S(1)}, u32[]{:S(2)}, u32[]{:S(2)}) collective-permute-start(bf16[2,192,768]{2,1,0:T(8,128)(2,1)S(1)} %get-tuple-element.181), channel_id=1, source_target_pairs={{0,2},{1,3},{2,0},{3,1},{4,6},{5,7},{6,4},{7,5},{8,10},{9,11},{10,... | collective-permute-start | bytes 1769480 | tf_op jit(solution)/shard_map/ppermute | solution.py:35
  125.5 15.1 %collective-permute-start.36 = (bf16[2,192,768]{2,1,0:T(8,128)(2,1)S(1)}, bf16[2,192,768]{2,1,0:T(8,128)(2,1)S(1)}, u32[]{:S(2)}, u32[]{:S(2)}) collective-permute-start(bf16[2,192,768]{2,1,0:T(8,128)(2,1)S(1)} %get-tuple-element.175), channel_id=1, source_target_pairs={{0,1},{1,0},{2,3},{3,2},{4,5},{5,4},{6,7},{7,6},{8,9},{9,8},{10,11... | collective-permute-start | bytes 1769480 | tf_op jit(solution)/shard_map/ppermute | solution.py:35
  144.6 19.0 %collective-permute-start.41 = (bf16[4,112,768]{2,1,0:T(8,128)(2,1)S(1)}, bf16[4,112,768]{2,1,0:T(8,128)(2,1)S(1)}, u32[]{:S(2)}, u32[]{:S(2)}) collective-permute-start(bf16[4,112,768]{2,1,0:T(8,128)(2,1)S(1)} %get-tuple-element.196), channel_id=1, source_target_pairs={{0,4},{4,0},{1,5},{5,1},{2,6},{6,2},{3,7},{7,3},{8,12},{12,8},{9,1... | collective-permute-start | bytes 2064392 | tf_op jit(solution)/shard_map/ppermute | solution.py:35
  164.5 13.7 %collective-permute-start.45 = (bf16[2,384,384]{2,1,0:T(8,128)(2,1)S(1)}, bf16[2,384,384]{2,1,0:T(8,128)(2,1)S(1)}, u32[]{:S(2)}, u32[]{:S(2)}) collective-permute-start(bf16[2,384,384]{2,1,0:T(8,128)(2,1)S(1)} %get-tuple-element.216), channel_id=1, source_target_pairs={{0,1},{1,0},{2,3},{3,2},{4,5},{5,4},{6,7},{7,6},{8,9},{9,8},{10,11... | collective-permute-start | bytes 1769480 | tf_op jit(solution)/shard_map/ppermute | solution.py:35
  165.6 13.4 %collective-permute-start.46 = (bf16[2,384,384]{2,1,0:T(8,128)(2,1)S(1)}, bf16[2,384,384]{2,1,0:T(8,128)(2,1)S(1)}, u32[]{:S(2)}, u32[]{:S(2)}) collective-permute-start(bf16[2,384,384]{2,1,0:T(8,128)(2,1)S(1)} %get-tuple-element.217), channel_id=1, source_target_pairs={{0,2},{1,3},{2,0},{3,1},{4,6},{5,7},{6,4},{7,5},{8,10},{9,11},{10,... | collective-permute-start | bytes 1769480 | tf_op jit(solution)/shard_map/ppermute | solution.py:35
  166.7 14.1 %collective-permute-start.47 = (bf16[2,208,768]{2,1,0:T(8,128)(2,1)S(1)}, bf16[2,208,768]{2,1,0:T(8,128)(2,1)S(1)}, u32[]{:S(2)}, u32[]{:S(2)}) collective-permute-start(bf16[2,208,768]{2,1,0:T(8,128)(2,1)S(1)} %get-tuple-element.218), channel_id=1, source_target_pairs={{0,8},{8,0},{16,24},{24,16},{1,9},{9,1},{17,25},{25,17},{2,10},{10... | collective-permute-start | bytes 1916936 | tf_op jit(solution)/shard_map/ppermute | solution.py:35
  183.1 13.6 %collective-permute-start.50 = (bf16[208,768]{1,0:T(8,128)(2,1)S(1)}, bf16[208,768]{1,0:T(8,128)(2,1)S(1)}, u32[]{:S(2)}, u32[]{:S(2)}) collective-permute-start(bf16[208,768]{1,0:T(8,128)(2,1)S(1)} %fusion.3), channel_id=1, source_target_pairs={{0,16},{8,24},{16,0},{24,8},{1,17},{9,25},{17,1},{25,9},{2,18},{10... | collective-permute-start | bytes 958472 | tf_op jit(solution)/shard_map/ppermute | solution.py:35
  197.8 20.9 %collective-permute-start.56 = (bf16[208,768]{1,0:T(8,128)(2,1)S(1)}, bf16[208,768]{1,0:T(8,128)(2,1)S(1)}, u32[]{:S(2)}, u32[]{:S(2)}) collective-permute-start(bf16[208,768]{1,0:T(8,128)(2,1)S(1)} %fusion.refs_0_), channel_id=1, source_target_pairs={{0,3},{1,2},{2,1},{3,0},{4,7},{5,6},{6,5},{7,4},{8,11},{9,10},{10,... | collective-permute-start | bytes 958472 | tf_op jit(solution)/shard_map/ppermute | solution.py:35
  199.4 15.9 %collective-permute-start.55 = (bf16[208,768]{1,0:T(8,128)(2,1)S(1)}, bf16[208,768]{1,0:T(8,128)(2,1)S(1)}, u32[]{:S(2)}, u32[]{:S(2)}) collective-permute-start(bf16[208,768]{1,0:T(8,128)(2,1)S(1)} %fusion.refs_0_), channel_id=1, source_target_pairs={{0,2},{1,3},{2,0},{3,1},{4,6},{5,7},{6,4},{7,5},{8,10},{9,11},{10,... | collective-permute-start | bytes 958472 | tf_op jit(solution)/shard_map/ppermute | solution.py:35
  200.0 14.7 %collective-permute-start.54 = (bf16[208,768]{1,0:T(8,128)(2,1)S(1)}, bf16[208,768]{1,0:T(8,128)(2,1)S(1)}, u32[]{:S(2)}, u32[]{:S(2)}) collective-permute-start(bf16[208,768]{1,0:T(8,128)(2,1)S(1)} %fusion.refs_0_), channel_id=1, source_target_pairs={{0,1},{1,0},{2,3},{3,2},{4,5},{5,4},{6,7},{7,6},{8,9},{9,8},{10,11... | collective-permute-start | bytes 958472 | tf_op jit(solution)/shard_map/ppermute | solution.py:35
  208.7 18.4 %collective-permute-start.66 = (bf16[208,768]{1,0:T(8,128)(2,1)S(1)}, bf16[208,768]{1,0:T(8,128)(2,1)S(1)}, u32[]{:S(2)}, u32[]{:S(2)}) collective-permute-start(bf16[208,768]{1,0:T(8,128)(2,1)S(1)} %fusion.refs_0_), channel_id=1, source_target_pairs={{0,4},{4,0},{1,5},{5,1},{2,6},{6,2},{3,7},{7,3},{8,12},{12,8},{9,1... | collective-permute-start | bytes 958472 | tf_op jit(solution)/shard_map/ppermute | solution.py:35
  214.7 13.9 %collective-permute-start.67 = (bf16[208,768]{1,0:T(8,128)(2,1)S(1)}, bf16[208,768]{1,0:T(8,128)(2,1)S(1)}, u32[]{:S(2)}, u32[]{:S(2)}) collective-permute-start(bf16[208,768]{1,0:T(8,128)(2,1)S(1)} %collective-permute-done.54.refs_1_), channel_id=1, source_target_pairs={{0,4},{4,0},{1,5},{5,1},{2,6},{6,2},{3,7},{7,3},{8,12},{12,8},{9,1... | collective-permute-start | bytes 958472 | tf_op jit(solution)/shard_map/ppermute | solution.py:35
  215.3 13.2 %collective-permute-start.68 = (bf16[208,768]{1,0:T(8,128)(2,1)S(1)}, bf16[208,768]{1,0:T(8,128)(2,1)S(1)}, u32[]{:S(2)}, u32[]{:S(2)}) collective-permute-start(bf16[208,768]{1,0:T(8,128)(2,1)S(1)} %collective-permute-done.55.refs_2_), channel_id=1, source_target_pairs={{0,4},{4,0},{1,5},{5,1},{2,6},{6,2},{3,7},{7,3},{8,12},{12,8},{9,1... | collective-permute-start | bytes 958472 | tf_op jit(solution)/shard_map/ppermute | solution.py:35
  218.7 15.5 %collective-permute-start.57 = (bf16[256,768]{1,0:T(8,128)(2,1)S(1)}, bf16[256,768]{1,0:T(8,128)(2,1)S(1)}, u32[]{:S(2)}, u32[]{:S(2)}) collective-permute-start(bf16[256,768]{1,0:T(8,128)(2,1)S(1)} %get-tuple-element.247), channel_id=1, source_target_pairs={{0,1},{1,0},{2,3},{3,2},{4,5},{5,4},{6,7},{7,6},{8,9},{9,8},{10,11... | collective-permute-start | bytes 1179656 | tf_op jit(solution)/shard_map/ppermute | solution.py:35
  226.3 19.5 %collective-permute-start.58 = (bf16[256,768]{1,0:T(8,128)(2,1)S(1)}, bf16[256,768]{1,0:T(8,128)(2,1)S(1)}, u32[]{:S(2)}, u32[]{:S(2)}) collective-permute-start(bf16[256,768]{1,0:T(8,128)(2,1)S(1)} %get-tuple-element.248), channel_id=1, source_target_pairs={{0,2},{1,3},{2,0},{3,1},{4,6},{5,7},{6,4},{7,5},{8,10},{9,11},{10,... | collective-permute-start | bytes 1179656 | tf_op jit(solution)/shard_map/ppermute | solution.py:35
  227.1 18.7 %collective-permute-start.59 = (bf16[256,768]{1,0:T(8,128)(2,1)S(1)}, bf16[256,768]{1,0:T(8,128)(2,1)S(1)}, u32[]{:S(2)}, u32[]{:S(2)}) collective-permute-start(bf16[256,768]{1,0:T(8,128)(2,1)S(1)} %get-tuple-element.249), channel_id=1, source_target_pairs={{0,3},{1,2},{2,1},{3,0},{4,7},{5,6},{6,5},{7,4},{8,11},{9,10},{10,... | collective-permute-start | bytes 1179656 | tf_op jit(solution)/shard_map/ppermute | solution.py:35
  228.5 18.8 %collective-permute-start.60 = (bf16[2,112,576]{2,1,0:T(8,128)(2,1)S(1)}, bf16[2,112,576]{2,1,0:T(8,128)(2,1)S(1)}, u32[]{:S(2)}, u32[]{:S(2)}) collective-permute-start(bf16[2,112,576]{2,1,0:T(8,128)(2,1)S(1)} %get-tuple-element.265), channel_id=1, source_target_pairs={{0,8},{8,0},{16,24},{24,16},{1,9},{9,1},{17,25},{25,17},{2,10},{10... | collective-permute-start | bytes 774152 | tf_op jit(solution)/shard_map/ppermute | solution.py:35
  (58 other events, 455.4 us)
